TPU v7x, 32 devices: a whole 2x2x4 slice. The times are simulated.
32 devices in a mesh: wide: 8 (over y, x, core), narrow: 4 (over z).
Axes of the slice: x: 2, y: 2, z: 4, core: 2. Of those that a mesh axis runs over, the one named last changes fastest.
Arguments:
- series: float32 [512, 640], P(('wide', 'narrow'))
- pad_mask: int32 [512, 640], P(('wide', 'narrow')), may hold values from 0 to 1, as said below
- freq_class: int32 [512], P(('wide', 'narrow')), may hold values from 0 to 2, as said below
- owner: int32 [322], replicated, may hold values from 0 to 511, as said below
- step: int32 [1], replicated, may hold values from 1 to 20
- master: float32 [512, 64, 1280], P(('wide', 'narrow')), may hold values from -0.15625 to 0.15625
- moment1: float32 [512, 64, 1280], P(('wide', 'narrow')), may hold values from -3.0517578e-05 to 3.0517578e-05
- moment2: float32 [512, 64, 1280], P(('wide', 'narrow')), may hold values from 3.7893486e-12 to 1.5157394e-11
- small_master: float32 [11520], replicated
- small_m1: float32 [11520], replicated, may hold values from -0.00012207031 to 0.00012207031
- small_m2: float32 [11520], replicated, may hold values from 6.062958e-11 to 2.425183e-10
Outputs:
- loss: float32 [], replicated
- grad_norm: float32 [], replicated
- new_master: float32 [512, 64, 1280], P(('wide', 'narrow'))
- new_moment1: float32 [512, 64, 1280], P(('wide', 'narrow'))
- new_moment2: float32 [512, 64, 1280], P(('wide', 'narrow'))
- weight_copy: bfloat16 [512, 64, 1280], P(('wide', 'narrow'))
- small_new: float32 [11520], replicated
- small_new_m1: float32 [11520], replicated
- small_new_m2: float32 [11520], replicated
Inputs may be any that keep to these rules, and one draw needn't show every extreme that they name: `pad_mask`: 1 marks padding; in each series the padding is a prefix shorter than 512 points. `freq_class`: every class occurs. `owner`: distinct slots; slot s lies on the device of index s // 16 along wide+narrow; some device holds 16 blocks, others fewer.
All inputs are finite; a program needn't handle non-finite values.
Results may differ from a plain program's by a relative error of at most 0.0056.
The roundings to bfloat16 on the way count: a program that leaves them out, or rounds other values in their place, can miss the bound.
Values may be sent and summed in bfloat16 or wider, within the bound.
A program may use at most 512 MiB of HBM per device.

v0:
```python
import jax
import jax.numpy as jnp
from jax import lax
from jax.sharding import PartitionSpec as P

D = 1280
HEADS = 16
HDIM = 80
FF = 5120
PATCH = 32
HORIZON = 128
NQ = 9
NPATCH = 16
NCLASS = 3
BR = 64
TOTAL_SLOTS = 512
CTX = 512
OUTW = 1280
ROWS = 20608
NBLK = 322


CLIP = 0.01
RATE = 0.03
DECAY = 0.1
BETA = 0.5
EPSILON = 1e-08


def matmul(left, right):
    return jnp.dot(left, right, preferred_element_type=jnp.float32)


def tmatmul(left, right):
    return lax.dot_general(
        left, right, (((0,), (0,)), ((), ())), preferred_element_type=jnp.float32
    )


def backmul(left, right):
    return lax.dot_general(
        left, right, (((1,), (1,)), ((), ())), preferred_element_type=jnp.float32
    )


def silu(value):
    return value / (1.0 + jnp.exp(-value))


def silu_slope(value):
    sigmoid = 1.0 / (1.0 + jnp.exp(-value))
    return sigmoid * (1.0 + value * (1.0 - sigmoid))


def rms_norm(hidden, gain):
    return hidden * lax.rsqrt(jnp.mean(hidden * hidden, axis=-1, keepdims=True) + 1e-06) * gain


def tables():
    half = HDIM // 2
    inverse = jnp.power(10000.0, -2.0 * jnp.arange(half, dtype=jnp.float32) / HDIM)
    angle = jnp.arange(NPATCH, dtype=jnp.float32)[:, None] * inverse[None, :]
    return (jnp.cos(angle)[None, :, None, :], jnp.sin(angle)[None, :, None, :])


def rotate(value, cosine, sine):
    half = HDIM // 2
    first = value[..., :half]
    second = value[..., half:]
    return jnp.concatenate(
        [first * cosine - second * sine, first * sine + second * cosine], axis=-1
    )


def split_rows(flat_rows):
    shapes = (
        (2 * PATCH, 2 * D),
        (D, D),
        (D, 3 * D),
        (D, D),
        (D, FF),
        (FF, D),
        (D, D + OUTW),
        (D, OUTW),
    )
    pieces = []
    start = 0
    for first, second in shapes:
        number = first * second // D
        pieces.append(flat_rows[start : start + number].reshape(first, second))
        start += number
    return tuple(pieces)


def split_small(small):
    freq = small[: NCLASS * D].reshape(NCLASS, D)
    rest = small[NCLASS * D :]
    return (
        freq,
        rest[0:D],
        rest[D : 2 * D],
        rest[2 * D : 3 * D],
        rest[3 * D : 4 * D],
        rest[4 * D : 5 * D],
        rest[5 * D : 5 * D + OUTW],
    )


def prepare(series, pad_mask):
    valid = (1 - pad_mask).astype(jnp.float32)
    count_series = series.shape[0]
    context = (series[:, :CTX] * valid[:, :CTX]).reshape(count_series, NPATCH, PATCH)
    marks = pad_mask[:, :CTX].astype(jnp.float32).reshape(count_series, NPATCH, PATCH)
    feat = jnp.concatenate([context, marks], axis=-1)
    index = (jnp.arange(NPATCH, dtype=jnp.int32)[:, None] + 1) * PATCH + jnp.arange(
        HORIZON, dtype=jnp.int32
    )[None, :]
    return (feat, series[:, index], valid[:, index])


def class_sums(out, target, tmask, onehot):
    pred = out.reshape(onehot.shape[0], NPATCH, HORIZON, NQ + 1)
    error = pred[..., 0] - target
    square = jnp.sum(error * error * tmask, axis=(1, 2))
    levels = (jnp.arange(NQ, dtype=jnp.float32) + 1.0) / (NQ + 1)
    diff = target[..., None] - pred[..., 1:]
    pinball = jnp.sum(jnp.maximum(levels * diff, (levels - 1.0) * diff), axis=-1)
    quant = jnp.sum(pinball * tmask, axis=(1, 2))
    return jnp.stack([jnp.sum(onehot * square[:, None], 0), jnp.sum(onehot * quant[:, None], 0)])


def layer_forward(state_zero, mats, parts, cosine, sine, causal):
    w_qkv, w_out, w_up, w_down = (mats[2], mats[3], mats[4], mats[5])
    gain_one, gain_two = (parts[3], parts[4])
    count_series = state_zero.shape[0] // NPATCH
    normed_one = rms_norm(state_zero, gain_one).astype(jnp.bfloat16)
    qkv = matmul(normed_one, w_qkv).reshape(count_series, NPATCH, 3, HEADS, HDIM)
    queries = (rotate(qkv[:, :, 0], cosine, sine) * HDIM ** (-0.5)).astype(jnp.bfloat16)
    key_rot = rotate(qkv[:, :, 1], cosine, sine).astype(jnp.bfloat16)
    value_all = qkv[:, :, 2].astype(jnp.bfloat16)
    scores = jnp.einsum("sqhd,skhd->shqk", queries, key_rot, preferred_element_type=jnp.float32)
    scores = jnp.where(causal, scores, -1e30)
    peak = jnp.max(scores, axis=-1, keepdims=True)
    expo = jnp.exp(scores - peak)
    total = jnp.sum(expo, axis=-1, keepdims=True)
    log_total = peak + jnp.log(total)
    attend = (expo / total).astype(jnp.bfloat16)
    mixed = jnp.einsum("shqk,skhd->sqhd", attend, value_all, preferred_element_type=jnp.float32)
    mixed = mixed.astype(jnp.bfloat16).reshape(state_zero.shape[0], D)
    state_one = state_zero + matmul(mixed, w_out)
    normed_two = rms_norm(state_one, gain_two).astype(jnp.bfloat16)
    up_pre = matmul(normed_two, w_up)
    activ = silu(up_pre).astype(jnp.bfloat16)
    state_two = state_one + matmul(activ, w_down)
    return (
        state_two,
        (
            normed_one,
            queries,
            key_rot,
            value_all,
            log_total,
            mixed,
            state_one,
            normed_two,
            up_pre,
            activ,
        ),
    )


def layer_backward(grad_two, state_zero, kept, mats, parts, cosine, sine, causal):
    (
        normed_one,
        queries,
        key_rot,
        value_all,
        log_total,
        mixed,
        state_one,
        normed_two,
        up_pre,
        activ,
    ) = kept
    w_qkv, w_out, w_up, w_down = (mats[2], mats[3], mats[4], mats[5])
    gain_one, gain_two = (parts[3], parts[4])
    tokens = state_zero.shape[0]
    count_series = tokens // NPATCH
    grad_mlp = grad_two.astype(jnp.bfloat16)
    grad_down = tmatmul(activ, grad_mlp)
    grad_act = backmul(grad_mlp, w_down)
    grad_up_pre = (grad_act * silu_slope(up_pre)).astype(jnp.bfloat16)
    grad_up = tmatmul(normed_two, grad_up_pre)
    grad_normed = backmul(grad_up_pre, w_up)
    _, pull = jax.vjp(rms_norm, state_one, gain_two)
    grad_norm_in, grad_gain_two = pull(grad_normed)
    grad_one = grad_two + grad_norm_in
    grad_proj = grad_one.astype(jnp.bfloat16)
    grad_wout = tmatmul(mixed, grad_proj)
    grad_mixed = (
        backmul(grad_proj, w_out).astype(jnp.bfloat16).reshape(count_series, NPATCH, HEADS, HDIM)
    )
    scores = jnp.einsum("sqhd,skhd->shqk", queries, key_rot, preferred_element_type=jnp.float32)
    attend = jnp.where(causal, jnp.exp(scores - log_total), 0.0)
    grad_attend = jnp.einsum(
        "sqhd,skhd->shqk", grad_mixed, value_all, preferred_element_type=jnp.float32
    )
    grad_scores = (
        attend * (grad_attend - jnp.sum(grad_attend * attend, axis=-1, keepdims=True))
    ).astype(jnp.bfloat16)
    grad_query = jnp.einsum(
        "shqk,skhd->sqhd", grad_scores, key_rot, preferred_element_type=jnp.float32
    )
    grad_key = jnp.einsum(
        "shqk,sqhd->skhd", grad_scores, queries, preferred_element_type=jnp.float32
    )
    grad_value = jnp.einsum(
        "shqk,sqhd->skhd",
        attend.astype(jnp.bfloat16),
        grad_mixed,
        preferred_element_type=jnp.float32,
    )
    grad_qkv = jnp.stack(
        [
            rotate(grad_query, cosine, -sine) * HDIM ** (-0.5),
            rotate(grad_key, cosine, -sine),
            grad_value,
        ],
        axis=2,
    )
    grad_qkv = grad_qkv.reshape(tokens, 3 * D).astype(jnp.bfloat16)
    grad_wqkv = tmatmul(normed_one, grad_qkv)
    grad_normed_one = backmul(grad_qkv, w_qkv)
    _, pull = jax.vjp(rms_norm, state_zero, gain_one)
    grad_zero_in, grad_gain_one = pull(grad_normed_one)
    return (
        grad_one + grad_zero_in,
        (grad_wqkv, grad_wout, grad_up, grad_down),
        grad_gain_one,
        grad_gain_two,
    )


def adamw(weight, first, second, grad, step):
    power = step[0].astype(jnp.float32)
    first = BETA * first + (1.0 - BETA) * grad
    second = BETA * second + (1.0 - BETA) * grad * grad
    fix_one = 1.0 - jnp.power(BETA, power)
    fix_two = 1.0 - jnp.power(BETA, power)
    new = weight - RATE * (
        first / fix_one / (jnp.sqrt(second / fix_two) + EPSILON) + DECAY * weight
    )
    return (new, first, second)


def on_device(
    series,
    pad_mask,
    freq_class,
    owner,
    step,
    master,
    moment1,
    moment2,
    small_master,
    small_m1,
    small_m2,
):
    slot_count = master.shape[0]
    gathered = lax.all_gather(master.astype(jnp.bfloat16), ("wide", "narrow"), axis=0, tiled=True)
    mats = split_rows(gathered[owner].reshape(ROWS, D))
    tok_in, tok_out, head_in, head_out = (mats[0], mats[1], mats[6], mats[7])
    parts = split_small(small_master)
    freq, bias_one, bias_two, head_bias, out_bias = (
        parts[0],
        parts[1],
        parts[2],
        parts[5],
        parts[6],
    )
    feat, target, tmask = prepare(series, pad_mask)
    count_series = series.shape[0]
    tokens = count_series * NPATCH
    onehot = (freq_class[:, None] == jnp.arange(NCLASS, dtype=jnp.int32)[None, :]).astype(
        jnp.float32
    )
    local_counts = jnp.sum(onehot * jnp.sum(tmask, axis=(1, 2))[:, None], 0)
    counts = lax.psum(local_counts, ("wide", "narrow"))
    class_weight = 1.0 / (counts * NCLASS)
    cosine, sine = tables()
    causal = jnp.arange(NPATCH)[:, None] >= jnp.arange(NPATCH)[None, :]
    patch_in = feat.reshape(tokens, 2 * PATCH).astype(jnp.bfloat16)
    tok_pre = matmul(patch_in, tok_in)
    hidden = silu(tok_pre[:, :D] + bias_one).astype(jnp.bfloat16)
    class_rows = jnp.repeat(jnp.dot(onehot, freq, precision=lax.Precision.HIGHEST), NPATCH, axis=0)
    state_zero = matmul(hidden, tok_out) + bias_two + tok_pre[:, D:] + class_rows
    state_two, _ = layer_forward(state_zero, mats, parts, cosine, sine, causal)
    state_low = state_two.astype(jnp.bfloat16)
    head_pre = matmul(state_low, head_in)
    head_hidden = silu(head_pre[:, :D] + head_bias).astype(jnp.bfloat16)
    out = matmul(head_hidden, head_out) + out_bias + head_pre[:, D:]

    def loss_of(value):
        sums_here = class_sums(value, target, tmask, onehot)
        return (jnp.sum((sums_here[0] + sums_here[1] / NQ) * class_weight), sums_here)

    _, pull, local_sums = jax.vjp(loss_of, out, has_aux=True)
    (grad_out,) = pull(jnp.ones((), jnp.float32))
    sums = lax.psum(local_sums, ("wide", "narrow"))
    grad_out = grad_out.astype(jnp.bfloat16)
    grad_out_bias = jnp.sum(grad_out.astype(jnp.float32), axis=0)
    grad_head_out = tmatmul(head_hidden, grad_out)
    grad_head_first = backmul(grad_out, head_out) * silu_slope(head_pre[:, :D] + head_bias)
    grad_head_bias = jnp.sum(grad_head_first, axis=0)
    grad_head_pre = jnp.concatenate([grad_head_first, grad_out.astype(jnp.float32)], axis=1).astype(
        jnp.bfloat16
    )
    grad_head_in = tmatmul(state_low, grad_head_pre)
    grad_two = backmul(grad_head_pre, head_in)
    _, kept = layer_forward(state_zero, mats, parts, cosine, sine, causal)
    grad_zero, layer_grads, grad_gain_one, grad_gain_two = layer_backward(
        grad_two, state_zero, kept, mats, parts, cosine, sine, causal
    )
    grad_prod = grad_zero.astype(jnp.bfloat16)
    grad_tok_out = tmatmul(hidden, grad_prod)
    grad_first = backmul(grad_prod, tok_out) * silu_slope(tok_pre[:, :D] + bias_one)
    grad_tok_pre = jnp.concatenate([grad_first, grad_zero], axis=1).astype(jnp.bfloat16)
    grad_tok_in = tmatmul(patch_in, grad_tok_pre)
    grad_freq = jnp.dot(
        onehot.T,
        grad_zero.reshape(count_series, NPATCH, D).sum(axis=1),
        precision=lax.Precision.HIGHEST,
    )
    small_local = jnp.concatenate(
        [
            grad_freq.reshape(-1),
            jnp.sum(grad_first, axis=0),
            jnp.sum(grad_zero, axis=0),
            grad_gain_one,
            grad_gain_two,
            grad_head_bias,
            grad_out_bias,
        ]
    )
    small_grad = lax.psum(small_local, ("wide", "narrow"))
    grad_list = (grad_tok_in, grad_tok_out) + tuple(layer_grads) + (grad_head_in, grad_head_out)
    grad_blocks = jnp.concatenate([piece.reshape(-1, D) for piece in grad_list], axis=0).reshape(
        NBLK, BR, D
    )
    inverse = (
        jnp.full((TOTAL_SLOTS,), NBLK, jnp.int32).at[owner].set(jnp.arange(NBLK, dtype=jnp.int32))
    )
    picked = grad_blocks[jnp.minimum(inverse, NBLK - 1)]
    slot_buffer = picked * (inverse < NBLK).astype(jnp.float32)[:, None, None]
    wide_count = lax.axis_size("wide")
    narrow_count = lax.axis_size("narrow")
    slot_buffer = slot_buffer.reshape(wide_count, narrow_count, slot_count, BR, D)
    partial_value = jnp.sum(
        lax.all_to_all(
            slot_buffer.astype(jnp.bfloat16), "wide", split_axis=0, concat_axis=0, tiled=True
        ).astype(slot_buffer.dtype),
        axis=0,
    )
    returned = lax.all_to_all(partial_value, "narrow", split_axis=0, concat_axis=0, tiled=True)
    owned = jnp.sum(returned, axis=0)
    local_square = jnp.sum(owned * owned)
    square_total = lax.psum(local_square, ("wide", "narrow"))
    grad_norm = jnp.sqrt(square_total + jnp.sum(small_grad * small_grad))
    scale = jnp.minimum(1.0, CLIP / grad_norm)
    loss = jnp.sum((sums[0] + sums[1] / NQ) * class_weight)
    new_master, new_m1, new_m2 = adamw(master, moment1, moment2, owned * scale, step)
    small_new, small_new_m1, small_new_m2 = adamw(
        small_master, small_m1, small_m2, small_grad * scale, step
    )
    return (
        loss,
        grad_norm,
        new_master,
        new_m1,
        new_m2,
        new_master.astype(jnp.bfloat16),
        small_new,
        small_new_m1,
        small_new_m2,
    )


def solution(mesh):
    return jax.shard_map(
        on_device,
        mesh=mesh,
        in_specs=(
            P(("wide", "narrow"), None),
            P(("wide", "narrow"), None),
            P(("wide", "narrow")),
            P(),
            P(),
            P(("wide", "narrow"), None, None),
            P(("wide", "narrow"), None, None),
            P(("wide", "narrow"), None, None),
            P(),
            P(),
            P(),
        ),
        out_specs=(
            P(),
            P(),
            P(("wide", "narrow"), None, None),
            P(("wide", "narrow"), None, None),
            P(("wide", "narrow"), None, None),
            P(("wide", "narrow"), None, None),
            P(),
            P(),
            P(),
        ),
        check_vma=False,
    )
```

profile of v0, /device:TPU:0, one launch (start us, length us, event | category | flops | bytes accessed | tf_op | source)
XLA Modules:
  0.0 2617.3 jit_solution(11782157767011893342)
XLA Ops:
  7.2 4.3 convert_element_type.120
  12.6 5.5 gather_fusion.2
  18.4 46.7 %psum.29 = f32[3]{0:T(128)S(1)} all-reduce(f32[3]{0:T(128)S(1)} %select_reduce_fusion.3), channel_id=1, replica_groups=mesh['wide'=8,'narrow'=4] {'wide','narrow'}, use_global_device_ids=true, to_apply=%region_12.13 | all-reduce | flops 3 | bytes 24 | tf_op jit(solution)/shard_map/psum | solution.py:288
  65.6 5.5 gather_fusion.1
  80.4 371.0 %all-gather.2.cloned.1.call-done = bf16[512,64,1280]{2,1,0:T(8,128)(2,1)} async-done(((bf16[16,64,1280]{2,1,0:T(8,128)(2,1)}), bf16[512,64,1280]{2,1,0:T(8,128)(2,1)}) %all-gather.2.cloned.1.call-update) | async-done | bytes 83886096 | tf_op jit(solution)/shard_map/all_gather | solution.py:270
  451.4 38.6 %gather_fusion = bf16[322,64,1280]{2,1,0:T(8,128)(2,1)} fusion(bf16[512,64,1280]{2,1,0:T(8,128)(2,1)} %all-gather.2.cloned.1.call-done, s32[1024]{0:T(1024)S(1)} %pad_clamp_fusion.1), kind=kCustom, calls=%fused_computation | custom fusion | bytes 105514248 | tf_op jit(solution)/shard_map/gather | solution.py:271
  490.0 6.9 fusion.72
  496.9 8.6 slice.209
  505.5 17.6 fusion.71
  523.2 6.4 slice.220
  533.9 15.7 reshape.351
  549.7 13.7 copy.116
  563.6 7.3 fusion.76
  582.8 21.0 reshape.353
  603.8 10.6 reshape.354
  614.3 7.3 fusion.65
  621.6 10.9 fusion.5
  640.0 6.0 reshape.355
  646.0 7.9 slice.225
  653.8 6.8 copy.143
  669.8 6.8 convert_element_type.133
  676.7 5.1 fusion.73
  683.3 6.1 fusion.26
  689.3 11.9 fusion
  701.2 9.0 multiply_reduce_fusion.2
  731.6 6.1 convert_element_type.141
  737.8 8.0 multiply_reduce_fusion.3
  745.8 8.5 fusion.78
  754.3 10.6 fusion.64
  764.9 6.5 fusion.25
  778.0 5.3 convolution_dynamic-update-slice_fusion.3
  783.2 21.4 reshape.358
  804.6 15.1 constant_dynamic-update-slice_fusion.2
  823.4 29.5 %reshape.359 = f32[5120,1280]{1,0:T(8,128)} reshape(f32[1280,5120]{1,0:T(8,128)} %fusion.64) | data formatting | bytes 52428800 | tf_op jit(solution)/shard_map/reshape | solution.py:347
  852.9 20.2 constant_dynamic-update-slice_fusion.1
  873.1 11.3 convolution_dynamic-update-slice_fusion
  884.4 14.6 reshape.360
  899.0 10.4 constant_dynamic-update-slice_fusion
  913.5 107.3 %gather_fusion.3 = f32[512,64,1280]{2,1,0:T(8,128)} fusion(f32[322,64,1280]{2,1,0:T(8,128)} %bitcast.39, s32[1024]{0:T(1024)S(1)} %copy-done.66), kind=kCustom, calls=%fused_computation.3 | custom fusion | bytes 335546368 | tf_op jit(solution)/shard_map/gather | solution.py:353
  1020.8 80.0 %multiply_convert_fusion = bf16[8,4,16,64,1280]{4,3,2,1,0:T(8,128)(2,1)} fusion(f32[8,4,16,64,1280]{4,3,2,1,0:T(8,128)} %bitcast.40, f32[8,4,16]{2,1,0:T(4,128)S(1)} %copy-done.54), kind=kLoop, calls=%fused_computation.6 | loop fusion | flops 83886080 | bytes 251660288 | tf_op jit(solution)/shard_map/convert_element_type | solution.py:360
  1100.9 924.7 %all_to_all.10 = bf16[8,4,16,64,1280]{4,3,2,1,0:T(8,128)(2,1)} all-to-all(bf16[8,4,16,64,1280]{4,3,2,1,0:T(8,128)(2,1)} %multiply_convert_fusion), channel_id=1, replica_groups=mesh['wide'=8,'narrow'=4] {'wide'}, dimensions={0} | all-to-all | bytes 167772160 | tf_op jit(solution)/shard_map/all_to_all | solution.py:359
  2025.6 52.5 %convert_reduce_fusion = f32[4,16,64,1280]{3,2,1,0:T(8,128)} fusion(bf16[8,4,16,64,1280]{4,3,2,1,0:T(8,128)(2,1)} %all_to_all.10), kind=kLoop, calls=%fused_computation.5 | loop fusion | flops 78643200 | bytes 104857600 | tf_op jit(solution)/shard_map/reduce_sum | solution.py:358
  2078.1 7.9 all-to-all-start.1
  2087.5 450.9 %all-to-all-done.1 = f32[4,16,64,1280]{3,2,1,0:T(8,128)} async-done(((f32[4,16,64,1280]{3,2,1,0:T(8,128)}), f32[4,16,64,1280]{3,2,1,0:T(8,128)}, u32[]{:S(2)}, u32[]{:S(2)}) %all-to-all-start.1) | async-done | bytes 20971552 | tf_op jit(solution)/shard_map/all_to_all | solution.py:364
  2538.4 10.8 reduce_sum.306
  2549.3 4.5 multiply_reduce_fusion
  2553.7 37.6 %all-reduce.4 = (f32[2,3]{1,0:T(2,128)S(1)}, f32[]{:T(128)}, f32[11520]{0:T(1024)S(1)}) all-reduce(f32[2,3]{1,0:T(2,128)S(1)} %pad_maximum_fusion.9, f32[]{:T(128)} %multiply_reduce_fusion, f32[11520]{0:T(1024)S(1)} %constant_dynamic-update-slice_fusion.5), channel_id=1, replica_groups=mesh['wide'=8,'narrow'=4] {'wide','narrow'}, use_global_device_ids=true, to_apply=%region_9.10 | all-reduce | flops 11527 | bytes 92216 | tf_op jit(solution)/shard_map/psum | solution.py:309
  2594.6 14.5 fusion.67
  (302 shorter events, 83.5 us)
Async XLA Ops:
  7.2 444.2 %all-gather.2.cloned.1.call-start = ((), (), s32[]{:S(2)}) async-start(), calls=%async_computation.2 | async-start | bytes 86507520 | tf_op jit(solution)/shard_map/all_gather | solution.py:270
  11.5 53.6 %copy-start.48 = (f32[16,640]{1,0:T(8,128)S(1)}, f32[16,640]{1,0:T(8,128)}, u32[]{:S(2)}) copy-start(f32[16,640]{1,0:T(8,128)} %param.11) | copy-start | bytes 122884
  12.3 53.3 %slice-start.4 = ((f32[11520]{0:T(1024)}), f32[3840]{0:T(1024)S(1)}, s32[]{:S(2)}) async-start(f32[11520]{0:T(1024)} %param.19), calls=%async_computation.7 | async-start | bytes 32768 | tf_op jit(solution)/shard_map/slice | solution.py:96
  65.1 14.4 copy-start.45
  65.4 464.2 %copy-start.40 = (bf16[256,32]{1,0:T(8,128)(2,1)}, bf16[256,32]{1,0:T(8,128)(2,1)S(1)}, u32[]{:S(2)}) copy-start(bf16[256,32]{1,0:T(8,128)(2,1)S(1)} %concatenate.49) | copy-start | bytes 49156
  65.6 464.1 %copy-start.42 = (bf16[256,32]{1,0:T(8,128)(2,1)}, bf16[256,32]{1,0:T(8,128)(2,1)S(1)}, u32[]{:S(2)}) copy-start(bf16[256,32]{1,0:T(8,128)(2,1)S(1)} %concatenate.50) | copy-start | bytes 49156
  77.7 498.4 %copy-start.49 = (pred[16,16]{0,1:T(8,128)(4,1)}, pred[16,16]{0,1:T(8,128)(4,1)S(1)}, u32[]{:S(2)}) copy-start(pred[16,16]{0,1:T(8,128)(4,1)S(1)} %iota_compare_fusion) | copy-start | bytes 772
  80.1 450.2 %copy-start.70 = (f32[1280]{0:T(1024)}, f32[1280]{0:T(1024)S(1)}, u32[]{:S(2)}) copy-start(f32[1280]{0:T(1024)S(1)} %get-tuple-element.58) | copy-start | bytes 15364
  80.1 483.3 %copy-start.51 = (f32[1280]{0:T(1024)}, f32[1280]{0:T(1024)S(1)}, u32[]{:S(2)}) copy-start(f32[1280]{0:T(1024)S(1)} %get-tuple-element.56) | copy-start | bytes 15364
  533.9 15.8 copy-start.79
  533.9 29.5 %copy-start.3 = (f32[256,1280]{1,0:T(8,128)}, f32[256,1280]{1,0:T(8,128)S(1)}, u32[]{:S(2)}) copy-start(f32[256,1280]{1,0:T(8,128)S(1)} %get-tuple-element.68) | copy-start | bytes 3932164
  533.9 29.5 %copy-start.62 = (f32[256]{0:T(256)}, f32[256]{0:T(256)S(1)}, u32[]{:S(2)}) copy-start(f32[256]{0:T(256)S(1)} %fusion.53) | copy-start | bytes 3076
  582.8 21.0 copy-start.64
  582.8 38.9 %copy-start = (f32[256,1280]{1,0:T(8,128)}, f32[256,1280]{1,0:T(8,128)S(1)}, u32[]{:S(2)}) copy-start(f32[256,1280]{1,0:T(8,128)S(1)} %get-tuple-element.72) | copy-start | bytes 3932164
  582.8 31.6 %copy-start.57 = (f32[256]{0:T(256)}, f32[256]{0:T(256)S(1)}, u32[]{:S(2)}) copy-start(f32[256]{0:T(256)S(1)} %fusion.54) | copy-start | bytes 3076
  614.3 18.2 slice-start.2
  621.6 10.9 copy-start.88
  621.6 10.9 slice-start.3
  689.3 11.9 copy-start.1
  701.2 9.0 copy-start.65
  701.2 9.0 copy-start.34
  701.2 9.0 copy-start.58
  754.3 10.6 copy-start.27
  754.3 10.6 copy-start.38
  754.3 10.6 copy-start.39
  804.6 15.1 copy-start.18
  823.4 49.7 %slice-start.5 = ((s8[5242880]{0:T(1024)(128)(4,1)}), s8[1048576]{0:T(1024)(128)(4,1)S(1)}, s32[]{:S(2)}) async-start(s8[5242880]{0:T(1024)(128)(4,1)} %bitcast.164), calls=%async_computation.8 | async-start | bytes 2097152
  852.9 20.2 copy-start.35
  852.9 20.2 slice-start.6
  899.0 10.4 copy-start.31
  899.0 10.4 copy-start.69
  899.0 10.4 copy-start.90
  913.5 107.3 %copy-start.54 = (f32[8,4,16]{2,1,0:T(4,128)S(1)}, f32[8,4,16]{2,1,0:T(4,128)}, u32[]{:S(2)}) copy-start(f32[8,4,16]{2,1,0:T(4,128)} %reshape.364) | copy-start | bytes 6148
  2078.1 8.6 copy-start.6
  2078.1 8.8 copy-start.78
  2078.1 9.0 copy-start.60
  2078.1 9.3 copy-start.84
  2078.1 9.3 copy-start.85
  2078.1 9.3 copy-start.76
  2078.1 9.3 copy-start.61
  2078.1 9.3 copy-start.75
  2078.1 9.4 copy-start.74
  2078.1 9.4 copy-start.73
  2078.1 460.3 %all-to-all-start.1 = ((f32[4,16,64,1280]{3,2,1,0:T(8,128)}), f32[4,16,64,1280]{3,2,1,0:T(8,128)}, u32[]{:S(2)}, u32[]{:S(2)}) async-start(f32[4,16,64,1280]{3,2,1,0:T(8,128)} %convert_reduce_fusion), calls=%async_computation.1 | async-start | bytes 41943040 | tf_op jit(solution)/shard_map/all_to_all | solution.py:364
  2549.3 44.0 %copy-start.87 = (f32[3]{0:T(128)S(1)}, f32[3]{0:T(128)}, u32[]{:S(2)}) copy-start(f32[3]{0:T(128)} %copy-done.86) | copy-start | bytes 40
  2549.3 44.7 %copy-start.46 = (f32[11520]{0:T(1024)S(1)}, f32[11520]{0:T(1024)}, u32[]{:S(2)}) copy-start(f32[11520]{0:T(1024)} %param.19) | copy-start | bytes 138244
  2549.3 44.7 %copy-start.55 = (f32[11520]{0:T(1024)S(1)}, f32[11520]{0:T(1024)}, u32[]{:S(2)}) copy-start(f32[11520]{0:T(1024)} %param.21) | copy-start | bytes 138244
  2549.3 44.7 %copy-start.56 = (f32[11520]{0:T(1024)S(1)}, f32[11520]{0:T(1024)}, u32[]{:S(2)}) copy-start(f32[11520]{0:T(1024)} %param.20) | copy-start | bytes 138244
  (52 other events, 195.4 us)
Sparse Core Ops, SparseCore 0:
  11.7 439.6 all-gather.1
where the time goes:
time: 2630 us; the launch traced here: 2620 us
  blocking collectives  1010 us (38%)
  waiting for transfers between devices  822 us (31%)
  local copies, waits for them, and re-layouts  438 us (17%)
  other arithmetic  185 us (7%)
  matrix products  137 us (5%)
    all_to_all x1, blocking collectives, on_device(): lax.all_to_all(slot_buffer.astype(jnp.bfloat16), 'wide', split_axis=0, co...  925 us
    all_to_all x1, waiting for transfers between devices, on_device(): lax.all_to_all(partial_value, 'narrow', split_axis=0, concat_axis=0, tile...  451 us
    all_gather x1, waiting for transfers between devices, on_device(): lax.all_gather(master.astype(jnp.bfloat16), ('wide', 'narrow'), axis=0, t...  371 us
    gather x1, local copies, waits for them, and re-layouts, on_device(): picked = grad_blocks[jnp.minimum(inverse, NBLK - 1)]  107 us
    convert_element_type x1, other arithmetic, on_device(): slot_buffer.astype(jnp.bfloat16)  80 us
    unnamed x203, local copies, waits for them, and re-layouts  66.1 us
    reshape x4, local copies, waits for them, and re-layouts, on_device(): piece.reshape(-1, D)  65.5 us
    reshape x5, local copies, waits for them, and re-layouts, split_rows(): pieces.append(flat_rows[start:start + number].reshape(first, second))  61.1 us
  transfers between devices with their start and end apart: 2, of which 2 were waited for; matrix products, arithmetic and copies ran while one was open for 1% of the time, Pallas kernels for 0%

commit v1 on v0

--- a/solution.py
+++ b/solution.py
@@ -344,25 +344,18 @@
     )
     small_grad = lax.psum(small_local, ("wide", "narrow"))
     grad_list = (grad_tok_in, grad_tok_out) + tuple(layer_grads) + (grad_head_in, grad_head_out)
-    grad_blocks = jnp.concatenate([piece.reshape(-1, D) for piece in grad_list], axis=0).reshape(
-        NBLK, BR, D
-    )
+    grad_blocks = jnp.concatenate(
+        [piece.astype(jnp.bfloat16).reshape(-1, D) for piece in grad_list], axis=0
+    ).reshape(NBLK, BR, D)
     inverse = (
         jnp.full((TOTAL_SLOTS,), NBLK, jnp.int32).at[owner].set(jnp.arange(NBLK, dtype=jnp.int32))
     )
     picked = grad_blocks[jnp.minimum(inverse, NBLK - 1)]
-    slot_buffer = picked * (inverse < NBLK).astype(jnp.float32)[:, None, None]
-    wide_count = lax.axis_size("wide")
-    narrow_count = lax.axis_size("narrow")
-    slot_buffer = slot_buffer.reshape(wide_count, narrow_count, slot_count, BR, D)
-    partial_value = jnp.sum(
-        lax.all_to_all(
-            slot_buffer.astype(jnp.bfloat16), "wide", split_axis=0, concat_axis=0, tiled=True
-        ).astype(slot_buffer.dtype),
-        axis=0,
-    )
-    returned = lax.all_to_all(partial_value, "narrow", split_axis=0, concat_axis=0, tiled=True)
-    owned = jnp.sum(returned, axis=0)
+    slot_buffer = jnp.where((inverse < NBLK)[:, None, None], picked, 0.0).astype(jnp.bfloat16)
+    partial_value = lax.psum_scatter(slot_buffer, "wide", scatter_dimension=0, tiled=True)
+    owned = lax.psum_scatter(
+        partial_value.astype(jnp.float32), "narrow", scatter_dimension=0, tiled=True
+    )
     local_square = jnp.sum(owned * owned)
     square_total = lax.psum(local_square, ("wide", "narrow"))
     grad_norm = jnp.sqrt(square_total + jnp.sum(small_grad * small_grad))

time: 2630 us -> 1880 us (0.71)
  blocking collectives: 1010 us -> 89 us
  waiting for transfers between devices: 822 us -> 1180 us
  local copies, waits for them, and re-layouts: 438 us -> 347 us
  other arithmetic: 185 us -> 111 us
    all_to_all x1 -> x0, blocking collectives: 925 us -> none  [on_device(): lax.all_to_all(slot_buffer.astype(jnp.bfloat16), 'wide', split_axis=0, co...]
    unnamed x1 -> x4, waiting for transfers between devices: 0.02 us -> 461 us
    all_to_all x1 -> x0, waiting for transfers between devices: 451 us -> none  [on_device(): lax.all_to_all(partial_value, 'narrow', split_axis=0, concat_axis=0, tile...]
    reduce_scatter x0 -> x1, waiting for transfers between devices: none -> 345 us  [on_device(): lax.psum_scatter(partial_value.astype(jnp.float32), 'narrow', scatter_dim...]
    convert_element_type x1, other arithmetic: 80 us -> 13.8 us  [on_device(): partial_value.astype(jnp.float32)]
    reduce_sum x2 -> x0, other arithmetic: 63.3 us -> none  [the longest x1 52.5 us: on_device(): jnp.sum(lax.all_to_all(slot_buffer.astype(jnp.bfloat16), 'wide', split_ax...]
    select_n x0 -> x1, other arithmetic: none -> 54.7 us  [on_device(): jnp.where((inverse < NBLK)[:, None, None], picked, 0.0).astype(jnp.bfloat16)]
    gather x1, local copies, waits for them, and re-layouts: 107 us -> 55.3 us  [on_device(): picked = grad_blocks[jnp.minimum(inverse, NBLK - 1)]]
  transfers between devices with their start and end apart: 2 -> 3, of which waited for: 2 -> 3; matrix products, arithmetic and copies ran while one was open for 1% -> 1% of each run, Pallas kernels for 0% -> 0%
where the time goes in v1:
time: 1880 us; the launch traced here: 1870 us
  waiting for transfers between devices  1180 us (63%)
  local copies, waits for them, and re-layouts  347 us (18%)
  matrix products  121 us (6%)
  other arithmetic  111 us (6%)
  blocking collectives  89 us (5%)
  between operations  18.9 us (1%)
    unnamed x4, waiting for transfers between devices  461 us
    all_gather x1, waiting for transfers between devices, on_device(): lax.all_gather(master.astype(jnp.bfloat16), ('wide', 'narrow'), axis=0, t...  371 us
    reduce_scatter x1, waiting for transfers between devices, on_device(): lax.psum_scatter(partial_value.astype(jnp.float32), 'narrow', scatter_dim...  345 us
    reshape x5, local copies, waits for them, and re-layouts, split_rows(): pieces.append(flat_rows[start:start + number].reshape(first, second))  61.1 us
    gather x1, local copies, waits for them, and re-layouts, on_device(): picked = grad_blocks[jnp.minimum(inverse, NBLK - 1)]  55.3 us
    select_n x1, other arithmetic, on_device(): jnp.where((inverse < NBLK)[:, None, None], picked, 0.0).astype(jnp.bfloat16)  54.7 us
    psum x1, blocking collectives, on_device(): counts = lax.psum(local_counts, ('wide', 'narrow'))  46.7 us
    reshape x4, local copies, waits for them, and re-layouts, on_device(): piece.astype(jnp.bfloat16).reshape(-1, D)  46.6 us
  transfers between devices with their start and end apart: 3, of which 3 were waited for; matrix products, arithmetic and copies ran while one was open for 1% of the time, Pallas kernels for 0%

profile of v1, /device:TPU:0, one launch (start us, length us, event | category | flops | bytes accessed | tf_op | source)
XLA Modules:
  0.0 1865.2 jit_solution(3121452004845963317)
XLA Ops:
  7.2 4.3 convert_element_type.142
  12.6 5.5 gather_fusion.2
  18.4 46.7 %psum.29 = f32[3]{0:T(128)S(1)} all-reduce(f32[3]{0:T(128)S(1)} %select_reduce_fusion.3), channel_id=1, replica_groups=mesh['wide'=8,'narrow'=4] {'wide','narrow'}, use_global_device_ids=true, to_apply=%region_12.13 | all-reduce | flops 3 | bytes 24 | tf_op jit(solution)/shard_map/psum | solution.py:288
  66.5 5.5 gather_fusion.1
  79.9 371.5 %all-gather.2.cloned.1.call-done = bf16[512,64,1280]{2,1,0:T(8,128)(2,1)} async-done(((bf16[16,64,1280]{2,1,0:T(8,128)(2,1)}), bf16[512,64,1280]{2,1,0:T(8,128)(2,1)}) %all-gather.2.cloned.1.call-update) | async-done | bytes 83886096 | tf_op jit(solution)/shard_map/all_gather | solution.py:270
  451.4 38.7 %gather_fusion = bf16[322,64,1280]{2,1,0:T(8,128)(2,1)} fusion(bf16[512,64,1280]{2,1,0:T(8,128)(2,1)} %all-gather.2.cloned.1.call-done, s32[1024]{0:T(1024)S(1)} %pad_clamp_fusion.1), kind=kCustom, calls=%fused_computation | custom fusion | bytes 105514248 | tf_op jit(solution)/shard_map/gather | solution.py:271
  490.1 6.9 fusion.73
  497.0 8.7 slice.209
  505.6 17.6 fusion.72
  523.2 6.3 slice.220
  534.0 15.8 reshape.346
  549.7 13.8 copy.116
  563.7 7.3 fusion.77
  579.1 20.5 %reshape.348 = bf16[1280,5120]{1,0:T(8,128)(2,1)} reshape(bf16[80,64,1280]{2,1,0:T(8,128)(2,1)} %get-tuple-element.35) | data formatting | bytes 26214400 | tf_op jit(solution)/shard_map/reshape | solution.py:90
  599.6 3.6 multiply_reduce_fusion.6
  603.3 11.0 reshape.349
  614.3 7.1 fusion.66
  621.4 10.9 fusion.9
  639.7 5.9 reshape.350
  645.7 8.0 slice.225
  654.7 6.0 copy.143
  666.8 3.8 copy.129
  670.7 7.0 convert_element_type.155
  678.0 4.3 fusion.74
  683.1 5.8 fusion.28
  689.0 11.9 fusion.4
  700.8 9.0 multiply_reduce_fusion.2
  732.0 6.1 convert_element_type.163
  738.1 8.0 multiply_reduce_fusion.3
  746.1 5.5 convolution_convert_fusion.2
  751.6 6.8 convolution_convert_fusion.1
  758.5 4.6 convolution_convert_fusion.3
  769.4 4.4 fusion.3
  773.7 15.3 reshape.353
  789.0 8.3 constant_dynamic-update-slice_fusion.2
  800.1 20.6 %reshape.354 = bf16[5120,1280]{1,0:T(8,128)(2,1)} reshape(bf16[1280,5120]{1,0:T(8,128)(2,1)} %convolution_convert_fusion.1) | data formatting | bytes 26214400 | tf_op jit(solution)/shard_map/reshape | solution.py:348
  820.7 11.4 constant_dynamic-update-slice_fusion.1
  832.2 7.9 fusion
  840.1 10.6 reshape.355
  850.7 6.1 constant_dynamic-update-slice_fusion
  859.8 55.3 %gather_fusion.3 = bf16[512,64,1280]{2,1,0:T(8,128)(2,1)} fusion(bf16[322,64,1280]{2,1,0:T(8,128)(2,1)} %bitcast.144, s32[1024]{0:T(1024)S(1)} %copy-done.67), kind=kCustom, calls=%fused_computation.3 | custom fusion | bytes 167774208 | tf_op jit(solution)/shard_map/gather | solution.py:353
  915.2 54.7 %broadcast_select_fusion = bf16[512,64,1280]{2,1,0:T(8,128)(2,1)} fusion(bf16[512,64,1280]{2,1,0:T(8,128)(2,1)} %gather_fusion.3, pred[512]{0:T(512)(128)(4,1)S(1)} %copy-done.89), kind=kLoop, calls=%fused_computation.5 | loop fusion | flops 41943040 | bytes 167772672 | tf_op jit(solution)/shard_map/jit(_where)/select_n | solution.py:354
  969.9 461.1 %reduce-scatter.7.cloned.1.call-done = bf16[64,64,1280]{2,1,0:T(8,128)(2,1)} async-done(((bf16[512,64,1280]{2,1,0:T(8,128)(2,1)}), bf16[64,64,1280]{2,1,0:T(8,128)(2,1)}) %reduce-scatter.7.cloned.1.call-update) | async-done | bytes 10485776
  1431.1 13.8 convert_element_type.173
  1447.1 345.4 %reduce-scatter.5.cloned.1.call-done = f32[16,64,1280]{2,1,0:T(8,128)} async-done(((f32[64,64,1280]{2,1,0:T(8,128)}), f32[16,64,1280]{2,1,0:T(8,128)}) %reduce-scatter.5.cloned.1.call-update) | async-done | bytes 5242896 | tf_op jit(solution)/shard_map/reduce_scatter | solution.py:356
  1792.5 4.4 multiply_reduce_fusion
  1796.9 42.3 %all-reduce.5 = (f32[2,3]{1,0:T(2,128)S(1)}, f32[]{:T(128)}, f32[11520]{0:T(1024)S(1)}) all-reduce(f32[2,3]{1,0:T(2,128)S(1)} %pad_maximum_fusion.9, f32[]{:T(128)} %multiply_reduce_fusion, f32[11520]{0:T(1024)S(1)} %constant_dynamic-update-slice_fusion.5), channel_id=1, replica_groups=mesh['wide'=8,'narrow'=4] {'wide','narrow'}, use_global_device_ids=true, to_apply=%region_9.10 | all-reduce | flops 11527 | bytes 92216 | tf_op jit(solution)/shard_map/psum | solution.py:309
  1842.6 14.5 fusion.68
  (307 shorter events, 76.0 us)
Async XLA Ops:
  7.2 444.2 %all-gather.2.cloned.1.call-start = ((), (), s32[]{:S(2)}) async-start(), calls=%async_computation.2 | async-start | bytes 86507520 | tf_op jit(solution)/shard_map/all_gather | solution.py:270
  11.5 6.8 copy-start.78
  11.5 54.5 %slice-start.4 = ((f32[11520]{0:T(1024)}), f32[3840]{0:T(1024)S(1)}, s32[]{:S(2)}) async-start(f32[11520]{0:T(1024)} %param.19), calls=%async_computation.9 | async-start | bytes 32768 | tf_op jit(solution)/shard_map/slice | solution.py:96
  11.6 54.7 %copy-start.50 = (f32[16,640]{1,0:T(8,128)S(1)}, f32[16,640]{1,0:T(8,128)}, u32[]{:S(2)}) copy-start(f32[16,640]{1,0:T(8,128)} %param.11) | copy-start | bytes 122884
  11.6 1419.5 %reduce-scatter.7.cloned.1.call-start = ((), (), s32[]{:S(2)}) async-start(), calls=%async_computation.4 | async-start | bytes 94371840
  65.1 7.9 copy-start.84
  65.1 13.9 copy-start.43
  66.2 463.5 %copy-start.45 = (bf16[256,32]{1,0:T(8,128)(2,1)}, bf16[256,32]{1,0:T(8,128)(2,1)S(1)}, u32[]{:S(2)}) copy-start(bf16[256,32]{1,0:T(8,128)(2,1)S(1)} %concatenate.50) | copy-start | bytes 49156
  66.5 463.2 %copy-start.47 = (bf16[256,32]{1,0:T(8,128)(2,1)}, bf16[256,32]{1,0:T(8,128)(2,1)S(1)}, u32[]{:S(2)}) copy-start(bf16[256,32]{1,0:T(8,128)(2,1)S(1)} %concatenate.49) | copy-start | bytes 49156
  76.6 499.4 %copy-start.51 = (pred[16,16]{0,1:T(8,128)(4,1)}, pred[16,16]{0,1:T(8,128)(4,1)S(1)}, u32[]{:S(2)}) copy-start(pred[16,16]{0,1:T(8,128)(4,1)S(1)} %iota_compare_fusion) | copy-start | bytes 772
  79.7 450.7 %copy-start.71 = (f32[1280]{0:T(1024)}, f32[1280]{0:T(1024)S(1)}, u32[]{:S(2)}) copy-start(f32[1280]{0:T(1024)S(1)} %get-tuple-element.58) | copy-start | bytes 15364
  79.7 483.8 %copy-start.53 = (f32[1280]{0:T(1024)}, f32[1280]{0:T(1024)S(1)}, u32[]{:S(2)}) copy-start(f32[1280]{0:T(1024)S(1)} %get-tuple-element.56) | copy-start | bytes 15364
  523.2 6.3 slice-start
  533.9 15.8 copy-start.80
  534.0 29.5 %copy-start.3 = (f32[256,1280]{1,0:T(8,128)}, f32[256,1280]{1,0:T(8,128)S(1)}, u32[]{:S(2)}) copy-start(f32[256,1280]{1,0:T(8,128)S(1)} %get-tuple-element.68) | copy-start | bytes 3932164
  534.0 29.5 %copy-start.63 = (f32[256]{0:T(256)}, f32[256]{0:T(256)S(1)}, u32[]{:S(2)}) copy-start(f32[256]{0:T(256)S(1)} %fusion.55) | copy-start | bytes 3076
  563.7 7.3 copy-start.23
  603.2 11.0 copy-start.65
  603.2 18.1 copy-start
  603.3 11.0 copy-start.60
  614.3 18.0 slice-start.2
  621.4 10.9 copy-start.90
  621.4 10.9 slice-start.3
  645.7 8.0 slice-start.1
  654.7 7.0 copy-start.32
  670.7 7.3 copy-start.69
  688.9 11.9 copy-start.1
  700.8 9.0 copy-start.66
  700.8 9.0 copy-start.33
  700.8 9.0 copy-start.61
  732.0 6.1 copy-start.4
  732.0 6.1 copy-start.54
  732.0 6.1 copy-start.64
  738.1 8.0 copy-start.17
  738.1 8.0 copy-start.24
  751.6 6.8 copy-start.26
  751.6 6.8 copy-start.38
  751.6 6.8 copy-start.40
  789.0 8.3 copy-start.9
  800.1 32.1 %slice-start.5 = ((s8[5242880]{0:T(1024)(128)(4,1)}), s8[1048576]{0:T(1024)(128)(4,1)S(1)}, s32[]{:S(2)}) async-start(s8[5242880]{0:T(1024)(128)(4,1)} %bitcast.165), calls=%async_computation.10 | async-start | bytes 2097152
  820.7 11.4 copy-start.34
  820.7 11.4 slice-start.6
  859.8 55.3 %copy-start.89 = (pred[512]{0:T(512)(128)(4,1)S(1)}, pred[512]{0:T(512)(128)(4,1)}, u32[]{:S(2)}) copy-start(pred[512]{0:T(512)(128)(4,1)} %broadcast_compare_fusion) | copy-start | bytes 1540
  969.9 822.6 %reduce-scatter.5.cloned.1.call-start = ((), (), s32[]{:S(2)}) async-start(), calls=%async_computation.3 | async-start | bytes 26214400 | tf_op jit(solution)/shard_map/reduce_scatter | solution.py:356
  1447.0 392.2 %copy-start.88 = (f32[3]{0:T(128)S(1)}, f32[3]{0:T(128)}, u32[]{:S(2)}) copy-start(f32[3]{0:T(128)} %copy-done.87) | copy-start | bytes 40
  1447.0 394.8 %copy-start.44 = (f32[11520]{0:T(1024)S(1)}, f32[11520]{0:T(1024)}, u32[]{:S(2)}) copy-start(f32[11520]{0:T(1024)} %param.19) | copy-start | bytes 138244
  1447.1 394.8 %copy-start.56 = (f32[11520]{0:T(1024)S(1)}, f32[11520]{0:T(1024)}, u32[]{:S(2)}) copy-start(f32[11520]{0:T(1024)} %param.21) | copy-start | bytes 138244
  1447.1 394.8 %copy-start.57 = (f32[11520]{0:T(1024)S(1)}, f32[11520]{0:T(1024)}, u32[]{:S(2)}) copy-start(f32[11520]{0:T(1024)} %param.20) | copy-start | bytes 138244
  (55 other events, 154.0 us)
Sparse Core Ops, SparseCore 0:
  11.7 439.6 all-gather.1
  970.0 461.0 reduce-scatter.6
  1445.1 347.3 reduce-scatter.4

commit v2 on v1

--- a/solution.py
+++ b/solution.py
@@ -1,6 +1,10 @@
+import functools
+
 import jax
 import jax.numpy as jnp
 from jax import lax
+from jax.experimental import pallas as pl
+from jax.experimental.pallas import tpu as pltpu
 from jax.sharding import PartitionSpec as P
 
 D = 1280
@@ -72,24 +76,154 @@
     )
 
 
-def split_rows(flat_rows):
-    shapes = (
-        (2 * PATCH, 2 * D),
-        (D, D),
-        (D, 3 * D),
-        (D, D),
-        (D, FF),
-        (FF, D),
-        (D, D + OUTW),
-        (D, OUTW),
-    )
-    pieces = []
-    start = 0
-    for first, second in shapes:
-        number = first * second // D
-        pieces.append(flat_rows[start : start + number].reshape(first, second))
-        start += number
-    return tuple(pieces)
+MATS = (
+    (2 * PATCH, 2, 2),
+    (D, 1, 4),
+    (D, 3, 6),
+    (D, 1, 4),
+    (D, FF // D, 8),
+    (FF, 1, 8),
+    (D, (D + OUTW) // D, 4),
+    (D, 1, 4),
+)
+BASES = tuple(sum(r * g for r, g, _ in MATS[:i]) // BR for i in range(len(MATS)))
+LANES = 128
+VMEM_LIMIT = 56 * 1024 * 1024
+
+
+def unpack_kernel(groups, count, owner_ref, *refs):
+    out_ref = refs[count]
+    if groups == 1:
+        for b in range(count):
+            out_ref[b * BR : (b + 1) * BR, :] = refs[b][...]
+        return
+    wide_ref = refs[count + 1]
+    for b in range(count):
+        for c in range(D // LANES):
+            wide_ref[c, b * BR : (b + 1) * BR, :] = refs[b][
+                :, c * LANES : (c + 1) * LANES
+            ].astype(jnp.float32)
+    rows = count * BR // groups
+    for j in range(groups):
+        for c in range(D // LANES):
+            at = j * D + c * LANES
+            out_ref[:, at : at + LANES] = wide_ref[c, pl.ds(j, rows, stride=groups), :].astype(
+                jnp.bfloat16
+            )
+
+
+def unpack(gathered, owner, which):
+    total, groups, count = MATS[which]
+    base = BASES[which]
+    rows = count * BR // groups
+
+    def spec(b):
+        return pl.BlockSpec(
+            (None, BR, D), lambda i, own, b=b: (own[base + i * count + b], 0, 0)
+        )
+
+    return pl.pallas_call(
+        functools.partial(unpack_kernel, groups, count),
+        out_shape=jax.ShapeDtypeStruct((total, groups * D), jnp.bfloat16),
+        grid_spec=pltpu.PrefetchScalarGridSpec(
+            num_scalar_prefetch=1,
+            grid=(total // rows,),
+            in_specs=[spec(b) for b in range(count)],
+            out_specs=pl.BlockSpec((rows, groups * D), lambda i, own: (i, 0)),
+            scratch_shapes=[]
+            if groups == 1
+            else [pltpu.VMEM((D // LANES, count * BR, LANES), jnp.float32)],
+        ),
+        compiler_params=pltpu.CompilerParams(vmem_limit_bytes=VMEM_LIMIT),
+        cost_estimate=pl.CostEstimate(
+            flops=0, bytes_accessed=4 * total * groups * D, transcendentals=0
+        ),
+        name=f"unpack_{which}",
+    )(owner, *([gathered] * count))
+
+
+def grad_kernel(groups, count, base, steps, owner_ref, left_ref, right_ref, *refs):
+    out_ref, stage_ref, sems = refs[-3 - (groups > 1)], refs[-2 - (groups > 1)], refs[-1 - (groups > 1)]
+    step = pl.program_id(0)
+    slot = lax.rem(step, 2)
+    rows = count * BR // groups
+
+    def copy(at, b, when):
+        return pltpu.make_async_copy(
+            stage_ref.at[at, pl.ds(b * BR, BR), :],
+            out_ref.at[owner_ref[base + when * count + b]],
+            sems.at[at, b],
+        )
+
+    @pl.when(step >= 2)
+    def _():
+        for b in range(count):
+            copy(slot, b, step - 2).wait()
+
+    left = left_ref[...]
+    for j in range(groups):
+        part = tmatmul(left, right_ref[:, j * D : (j + 1) * D])
+        if groups == 1:
+            stage_ref[slot] = part.astype(jnp.bfloat16)
+        else:
+            for c in range(D // LANES):
+                refs[-1][c, pl.ds(j, rows, stride=groups), :] = part[
+                    :, c * LANES : (c + 1) * LANES
+                ]
+    if groups > 1:
+        for c in range(D // LANES):
+            stage_ref[slot, :, c * LANES : (c + 1) * LANES] = refs[-1][c].astype(jnp.bfloat16)
+    for b in range(count):
+        copy(slot, b, step).start()
+
+    @pl.when(step == steps - 1)
+    def _():
+        for b in range(count):
+            copy(slot, b, step).wait()
+
+    if steps > 1:
+
+        @pl.when(step == steps - 1)
+        def _():
+            for b in range(count):
+                copy(1 - slot, b, step - 1).wait()
+
+
+def grad_blocks(left, right, owner, which, slots):
+    total, groups, count = MATS[which]
+    rows = count * BR // groups
+    steps = total // rows
+    tokens = left.shape[0]
+    scratch = [
+        pltpu.VMEM((2, count * BR, D), jnp.bfloat16),
+        pltpu.SemaphoreType.DMA((2, count)),
+    ]
+    if groups > 1:
+        scratch.append(pltpu.VMEM((D // LANES, count * BR, LANES), jnp.float32))
+    held = [] if slots is None else [slots]
+    return pl.pallas_call(
+        functools.partial(grad_kernel, groups, count, BASES[which], steps),
+        out_shape=jax.ShapeDtypeStruct((TOTAL_SLOTS, BR, D), jnp.bfloat16),
+        grid_spec=pltpu.PrefetchScalarGridSpec(
+            num_scalar_prefetch=1,
+            grid=(steps,),
+            in_specs=[
+                pl.BlockSpec((tokens, rows), lambda i, own: (0, i)),
+                pl.BlockSpec((tokens, groups * D), lambda i, own: (0, 0)),
+            ]
+            + [pl.BlockSpec(memory_space=pl.ANY)] * len(held),
+            out_specs=pl.BlockSpec(memory_space=pl.ANY),
+            scratch_shapes=scratch,
+        ),
+        input_output_aliases={3: 0} if held else {},
+        compiler_params=pltpu.CompilerParams(vmem_limit_bytes=VMEM_LIMIT),
+        cost_estimate=pl.CostEstimate(
+            flops=2 * tokens * total * groups * D,
+            bytes_accessed=2 * total * groups * D,
+            transcendentals=0,
+        ),
+        name=f"grad_{which}",
+    )(owner, left, right, *held)
 
 
 def split_small(small):
@@ -169,7 +303,9 @@
     )
 
 
-def layer_backward(grad_two, state_zero, kept, mats, parts, cosine, sine, causal):
+def layer_backward(
+    grad_two, state_zero, kept, mats, parts, cosine, sine, causal, owner, slots
+):
     (
         normed_one,
         queries,
@@ -187,16 +323,16 @@
     tokens = state_zero.shape[0]
     count_series = tokens // NPATCH
     grad_mlp = grad_two.astype(jnp.bfloat16)
-    grad_down = tmatmul(activ, grad_mlp)
+    slots = grad_blocks(activ, grad_mlp, owner, 5, slots)
     grad_act = backmul(grad_mlp, w_down)
     grad_up_pre = (grad_act * silu_slope(up_pre)).astype(jnp.bfloat16)
-    grad_up = tmatmul(normed_two, grad_up_pre)
+    slots = grad_blocks(normed_two, grad_up_pre, owner, 4, slots)
     grad_normed = backmul(grad_up_pre, w_up)
     _, pull = jax.vjp(rms_norm, state_one, gain_two)
     grad_norm_in, grad_gain_two = pull(grad_normed)
     grad_one = grad_two + grad_norm_in
     grad_proj = grad_one.astype(jnp.bfloat16)
-    grad_wout = tmatmul(mixed, grad_proj)
+    slots = grad_blocks(mixed, grad_proj, owner, 3, slots)
     grad_mixed = (
         backmul(grad_proj, w_out).astype(jnp.bfloat16).reshape(count_series, NPATCH, HEADS, HDIM)
     )
@@ -229,13 +365,13 @@
         axis=2,
     )
     grad_qkv = grad_qkv.reshape(tokens, 3 * D).astype(jnp.bfloat16)
-    grad_wqkv = tmatmul(normed_one, grad_qkv)
+    slots = grad_blocks(normed_one, grad_qkv, owner, 2, slots)
     grad_normed_one = backmul(grad_qkv, w_qkv)
     _, pull = jax.vjp(rms_norm, state_zero, gain_one)
     grad_zero_in, grad_gain_one = pull(grad_normed_one)
     return (
         grad_one + grad_zero_in,
-        (grad_wqkv, grad_wout, grad_up, grad_down),
+        slots,
         grad_gain_one,
         grad_gain_two,
     )
@@ -268,7 +404,7 @@
 ):
     slot_count = master.shape[0]
     gathered = lax.all_gather(master.astype(jnp.bfloat16), ("wide", "narrow"), axis=0, tiled=True)
-    mats = split_rows(gathered[owner].reshape(ROWS, D))
+    mats = tuple(unpack(gathered, owner, which) for which in range(len(MATS)))
     tok_in, tok_out, head_in, head_out = (mats[0], mats[1], mats[6], mats[7])
     parts = split_small(small_master)
     freq, bias_one, bias_two, head_bias, out_bias = (
@@ -309,23 +445,23 @@
     sums = lax.psum(local_sums, ("wide", "narrow"))
     grad_out = grad_out.astype(jnp.bfloat16)
     grad_out_bias = jnp.sum(grad_out.astype(jnp.float32), axis=0)
-    grad_head_out = tmatmul(head_hidden, grad_out)
+    slots = grad_blocks(head_hidden, grad_out, owner, 7, None)
     grad_head_first = backmul(grad_out, head_out) * silu_slope(head_pre[:, :D] + head_bias)
     grad_head_bias = jnp.sum(grad_head_first, axis=0)
     grad_head_pre = jnp.concatenate([grad_head_first, grad_out.astype(jnp.float32)], axis=1).astype(
         jnp.bfloat16
     )
-    grad_head_in = tmatmul(state_low, grad_head_pre)
+    slots = grad_blocks(state_low, grad_head_pre, owner, 6, slots)
     grad_two = backmul(grad_head_pre, head_in)
     _, kept = layer_forward(state_zero, mats, parts, cosine, sine, causal)
-    grad_zero, layer_grads, grad_gain_one, grad_gain_two = layer_backward(
-        grad_two, state_zero, kept, mats, parts, cosine, sine, causal
+    grad_zero, slots, grad_gain_one, grad_gain_two = layer_backward(
+        grad_two, state_zero, kept, mats, parts, cosine, sine, causal, owner, slots
     )
     grad_prod = grad_zero.astype(jnp.bfloat16)
-    grad_tok_out = tmatmul(hidden, grad_prod)
+    slots = grad_blocks(hidden, grad_prod, owner, 1, slots)
     grad_first = backmul(grad_prod, tok_out) * silu_slope(tok_pre[:, :D] + bias_one)
     grad_tok_pre = jnp.concatenate([grad_first, grad_zero], axis=1).astype(jnp.bfloat16)
-    grad_tok_in = tmatmul(patch_in, grad_tok_pre)
+    slots = grad_blocks(patch_in, grad_tok_pre, owner, 0, slots)
     grad_freq = jnp.dot(
         onehot.T,
         grad_zero.reshape(count_series, NPATCH, D).sum(axis=1),
@@ -343,19 +479,12 @@
         ]
     )
     small_grad = lax.psum(small_local, ("wide", "narrow"))
-    grad_list = (grad_tok_in, grad_tok_out) + tuple(layer_grads) + (grad_head_in, grad_head_out)
-    grad_blocks = jnp.concatenate(
-        [piece.astype(jnp.bfloat16).reshape(-1, D) for piece in grad_list], axis=0
-    ).reshape(NBLK, BR, D)
-    inverse = (
-        jnp.full((TOTAL_SLOTS,), NBLK, jnp.int32).at[owner].set(jnp.arange(NBLK, dtype=jnp.int32))
-    )
-    picked = grad_blocks[jnp.minimum(inverse, NBLK - 1)]
-    slot_buffer = jnp.where((inverse < NBLK)[:, None, None], picked, 0.0).astype(jnp.bfloat16)
-    partial_value = lax.psum_scatter(slot_buffer, "wide", scatter_dimension=0, tiled=True)
-    owned = lax.psum_scatter(
-        partial_value.astype(jnp.float32), "narrow", scatter_dimension=0, tiled=True
-    )
+    partial_value = lax.psum_scatter(slots, "wide", scatter_dimension=0, tiled=True)
+    owned = lax.psum_scatter(partial_value, "narrow", scatter_dimension=0, tiled=True)
+    rank = lax.axis_index("wide") * lax.axis_size("narrow") + lax.axis_index("narrow")
+    mine = rank * slot_count + jnp.arange(slot_count, dtype=jnp.int32)
+    filled = jnp.any(owner[:, None] == mine[None, :], axis=0)
+    owned = jnp.where(filled[:, None, None], owned.astype(jnp.float32), 0.0)
     local_square = jnp.sum(owned * owned)
     square_total = lax.psum(local_square, ("wide", "narrow"))
     grad_norm = jnp.sqrt(square_total + jnp.sum(small_grad * small_grad))

time: 1880 us -> 1490 us (0.79)
  local copies, waits for them, and re-layouts: 347 us -> 84.3 us
  waiting for transfers between devices: 1180 us -> 1010 us
  Pallas kernels: 0 us -> 140 us
  other arithmetic: 111 us -> 40.7 us
  matrix products: 121 us -> 92.5 us
    reduce_scatter x1, waiting for transfers between devices: 345 us -> 178 us  [on_device(): lax.psum_scatter(partial_value, 'narrow', scatter_dimension=0, tiled=True)]
    pallas_call x0 -> x16, Pallas kernels: none -> 140 us  [the longest x8 73.4 us: unpack(): pl.pallas_call(functools.partial(unpack_kernel, groups, count), out_shape...]
    reshape x9 -> x1, local copies, waits for them, and re-layouts: 108 us -> 8.01 us  [layer_forward(): matmul(normed_one, w_qkv).reshape(count_series, NPATCH, 3, HEADS, HDIM)]
    gather x2 -> x0, local copies, waits for them, and re-layouts: 94 us -> none  [the longest x1 55.3 us: on_device(): picked = grad_blocks[jnp.minimum(inverse, NBLK - 1)]]
    select_n x3 -> x0, other arithmetic: 54.7 us -> none  [the longest x1 54.7 us: on_device(): jnp.where((inverse < NBLK)[:, None, None], picked, 0.0).astype(jnp.bfloat16)]
    dot_general x8 -> x0, matrix products: 35.4 us -> none  [tmatmul(): lax.dot_general(left, right, (((0,), (0,)), ((), ())), preferred_element_...]
    slice x7 -> x3, local copies, waits for them, and re-layouts: 40.1 us -> 5.03 us  [the longest x1 2.63 us: layer_forward(): key_rot = rotate(qkv[:, :, 1], cosine, sine).astype(jnp.bfloat16)]
    unnamed x207 -> x197, local copies, waits for them, and re-layouts: 46.2 us -> 16.1 us
where the time goes in v2:
time: 1490 us; the launch traced here: 1480 us
  waiting for transfers between devices  1010 us (68%)
  Pallas kernels  140 us (9%)
  matrix products  92.5 us (6%)
  blocking collectives  88.8 us (6%)
  local copies, waits for them, and re-layouts  84.3 us (6%)
  other arithmetic  40.7 us (3%)
  between operations  18.9 us (1%)
    unnamed x4, waiting for transfers between devices  461 us
    all_gather x1, waiting for transfers between devices, on_device(): lax.all_gather(master.astype(jnp.bfloat16), ('wide', 'narrow'), axis=0, t...  375 us
    reduce_scatter x1, waiting for transfers between devices, on_device(): lax.psum_scatter(partial_value, 'narrow', scatter_dimension=0, tiled=True)  178 us
    pallas_call x8, Pallas kernels, unpack(): pl.pallas_call(functools.partial(unpack_kernel, groups, count), out_shape...  73.4 us
    pallas_call x8, Pallas kernels, grad_blocks(): pl.pallas_call(functools.partial(grad_kernel, groups, count, BASES[which]...  66.3 us
    psum x1, blocking collectives, on_device(): counts = lax.psum(local_counts, ('wide', 'narrow'))  46.7 us
    dot_general x7, matrix products, backmul(): lax.dot_general(left, right, (((1,), (1,)), ((), ())), preferred_element_...  43.1 us
    psum x1, blocking collectives, on_device(): sums = lax.psum(local_sums, ('wide', 'narrow'))  42.1 us
  transfers between devices with their start and end apart: 3, of which 3 were waited for; matrix products, arithmetic and copies ran while one was open for 1% of the time, Pallas kernels for 0%

profile of v2, /device:TPU:0, one launch (start us, length us, event | category | flops | bytes accessed | tf_op | source)
XLA Modules:
  0.0 1479.6 jit_solution(15839814365038328930)
XLA Ops:
  7.2 4.3 convert_element_type.103
  12.6 5.5 gather_fusion.1
  18.4 46.7 %psum.29 = f32[3]{0:T(128)S(1)} all-reduce(f32[3]{0:T(128)S(1)} %select_reduce_fusion.3), channel_id=1, replica_groups=mesh['wide'=8,'narrow'=4] {'wide','narrow'}, use_global_device_ids=true, to_apply=%region_12.13 | all-reduce | flops 3 | bytes 24 | tf_op jit(solution)/shard_map/psum | solution.py:424
  65.6 5.5 gather_fusion
  76.3 375.0 %all-gather.2.cloned.1.call-done.refs_0_.refs_1_.refs_2_.refs_3_.refs_4_.refs_5_.refs_6_.refs_7_ = bf16[512,64,1280]{2,1,0:T(8,128)(2,1)} async-done(((bf16[16,64,1280]{2,1,0:T(8,128)(2,1)}), bf16[512,64,1280]{2,1,0:T(8,128)(2,1)}) %all-gather.2.cloned.1.call-update) | async-done | bytes 83886096 | tf_op jit(solution)/shard_map/all_gather | solution.py:406
  451.4 2.5 unpack_0.1
  455.8 6.0 unpack_1.1
  461.9 3.1 multiply_reduce_fusion.7
  466.3 12.8 unpack_2.1
  479.1 8.4 fusion.64
  487.5 8.0 reshape.302
  495.5 2.6 fusion.58
  508.6 6.1 unpack_3.1
  514.7 3.0 multiply_reduce_fusion.6
  519.9 15.8 %unpack_4.1 = bf16[1280,5120]{1,0:T(8,128)(2,1)} custom-call(s32[322]{0:T(512)} %owner_ref.31, bf16[512,64,1280]{2,1,0:T(8,128)(2,1)} %all-gather.2.cloned.1.call-done.refs_0_.refs_1_.refs_2_.refs_3_.refs_4_.refs_5_.refs_6_.refs_7_, bf16[512,64,1280]{2,1,0:T(8,128)(2,1)} %all-gather.2.cloned.1.call-done.refs_0_.refs_1_.refs_2_.refs_3_.refs_4_.refs_5_.refs_6_.refs_7_, ...), custom_call_target="tpu_custom_call" | custom-call | bytes 26214400 | tf_op jit(solution)/shard_map/unpack_4/pallas_call | solution.py:125
  535.7 11.2 divide_convert_fusion
  546.9 13.6 unpack_5.1
  560.5 6.8 fusion.6.left_ref
  567.3 10.5 unpack_6.1
  577.8 4.7 fusion.65
  583.0 6.1 unpack_7.1
  589.1 2.9 fusion.4
  592.5 6.1 reshape.304
  598.5 7.9 slice.161
  606.5 6.0 copy.162
  616.0 3.8 copy.149
  619.8 7.7 convert_element_type.116
  627.5 4.1 fusion.59
  633.0 6.0 fusion.62
  639.0 11.7 fusion.right_ref
  650.7 8.9 multiply_reduce_fusion.2
  664.0 2.8 reshape.305
  674.4 6.3 grad_7.1.refs_0_
  688.3 5.4 convert_element_type.123.right_ref
  693.7 8.0 multiply_reduce_fusion.3
  705.0 2.5 fusion.60
  707.5 9.7 grad_6.1.refs_0_
  717.2 11.3 grad_5.1.refs_0_
  728.5 12.5 grad_4.1.refs_0_
  741.0 6.1 grad_3.1.refs_0_
  747.1 11.0 grad_2.1.refs_0_
  758.2 6.3 grad_1.1.refs_0_
  765.6 3.2 grad_0.1
  768.9 461.2 %reduce-scatter.7.cloned.1.call-done = bf16[64,64,1280]{2,1,0:T(8,128)(2,1)} async-done(((bf16[512,64,1280]{2,1,0:T(8,128)(2,1)}), bf16[64,64,1280]{2,1,0:T(8,128)(2,1)}) %reduce-scatter.7.cloned.1.call-update) | async-done | bytes 10485776
  1232.2 178.2 %reduce-scatter.5.cloned.1.call-done = bf16[16,64,1280]{2,1,0:T(8,128)(2,1)} async-done(((bf16[64,64,1280]{2,1,0:T(8,128)(2,1)}), bf16[16,64,1280]{2,1,0:T(8,128)(2,1)}) %reduce-scatter.5.cloned.1.call-update) | async-done | bytes 2621456 | tf_op jit(solution)/shard_map/reduce_scatter | solution.py:483
  1410.5 3.9 multiply_reduce_fusion
  1414.4 42.1 %all-reduce.5 = (f32[2,3]{1,0:T(2,128)S(1)}, f32[]{:T(128)}, f32[11520]{0:T(1024)S(1)}) all-reduce(f32[2,3]{1,0:T(2,128)S(1)} %pad_maximum_fusion.7, f32[]{:T(128)} %multiply_reduce_fusion, f32[11520]{0:T(1024)S(1)} %constant_dynamic-update-slice_fusion), channel_id=1, replica_groups=mesh['wide'=8,'narrow'=4] {'wide','narrow'}, use_global_device_ids=true, to_apply=%region_9.10 | all-reduce | flops 11527 | bytes 92216 | tf_op jit(solution)/shard_map/psum | solution.py:445
  1459.7 11.7 fusion.52
  (287 shorter events, 55.3 us)
Async XLA Ops:
  7.2 444.2 %all-gather.2.cloned.1.call-start = ((), (), s32[]{:S(2)}) async-start(), calls=%async_computation.2 | async-start | bytes 86507520 | tf_op jit(solution)/shard_map/all_gather | solution.py:406
  11.5 6.8 copy-start.83
  11.5 53.6 %copy-start.52 = (f32[16,640]{1,0:T(8,128)S(1)}, f32[16,640]{1,0:T(8,128)}, u32[]{:S(2)}) copy-start(f32[16,640]{1,0:T(8,128)} %param.11) | copy-start | bytes 122884
  11.6 54.0 %slice-start.1 = ((f32[11520]{0:T(1024)}), f32[3840]{0:T(1024)S(1)}, s32[]{:S(2)}) async-start(f32[11520]{0:T(1024)} %param.19), calls=%async_computation.6 | async-start | bytes 32768 | tf_op jit(solution)/shard_map/slice | solution.py:230
  11.6 1218.5 %reduce-scatter.7.cloned.1.call-start = ((), (), s32[]{:S(2)}) async-start(), calls=%async_computation.4 | async-start | bytes 94371840
  65.3 10.2 copy-start.49
  73.5 380.3 %copy-start.92 = (f32[3]{0:T(128)}, f32[3]{0:T(128)S(1)}, u32[]{:S(2)}) copy-start(f32[3]{0:T(128)S(1)} %get-tuple-element.36) | copy-start | bytes 40
  74.3 379.6 %copy-start.45 = (bf16[256,64]{1,0:T(8,128)(2,1)}, bf16[256,64]{1,0:T(8,128)(2,1)S(1)}, u32[]{:S(2)}) copy-start(bf16[256,64]{1,0:T(8,128)(2,1)S(1)} %pad_maximum_fusion.6.left_ref) | copy-start | bytes 98308
  76.1 379.2 %copy-start.63 = (f32[1280]{0:T(1024)}, f32[1280]{0:T(1024)S(1)}, u32[]{:S(2)}) copy-start(f32[1280]{0:T(1024)S(1)} %get-tuple-element.56) | copy-start | bytes 15364
  76.1 389.0 %copy-start.55 = (f32[1280]{0:T(1024)}, f32[1280]{0:T(1024)S(1)}, u32[]{:S(2)}) copy-start(f32[1280]{0:T(1024)S(1)} %get-tuple-element.54) | copy-start | bytes 15364
  455.3 6.6 copy-start.13
  455.7 6.1 copy-start.24
  465.0 14.1 copy-start.72
  466.3 12.8 copy-start.36
  500.0 6.2 copy-start.29
  508.6 6.1 copy-start.27
  508.6 6.1 copy-start.3
  517.8 18.0 %copy-start.76 = (f32[256]{0:T(256)}, f32[256]{0:T(256)S(1)}, u32[]{:S(2)}) copy-start(f32[256]{0:T(256)S(1)} %get-tuple-element.70) | copy-start | bytes 3076
  519.9 15.8 %copy-start.33 = (bf16[256,1280]{1,0:T(8,128)(2,1)S(1)}, bf16[256,1280]{1,0:T(8,128)(2,1)}, u32[]{:S(2)}) copy-start(bf16[256,1280]{1,0:T(8,128)(2,1)} %multiply_convert_fusion.1.left_ref) | copy-start | bytes 1966084
  546.9 13.6 copy-start.8
  546.9 13.6 copy-start.35
  567.3 10.5 copy-start.41
  582.5 6.6 copy-start.44
  582.9 6.2 copy-start.34
  582.9 6.2 copy-start.78
  606.5 6.0 slice-start
  606.5 6.5 copy-start.31
  606.5 6.5 copy-start.86
  606.5 6.5 copy-start.87
  619.8 7.7 copy-start.32
  633.0 6.0 copy-start.22
  639.0 11.7 copy-start.9
  639.0 11.7 copy-start.60
  639.0 11.7 copy-start.75
  650.7 8.9 copy-start.77
  674.4 6.3 copy-start.23
  674.4 6.3 copy-start.42
  693.7 8.0 copy-start.21
  693.7 8.0 copy-start.73
  693.7 8.0 copy-start.28
  758.1 6.3 copy-start.26
  758.2 6.3 copy-start.43
  768.8 641.6 %reduce-scatter.5.cloned.1.call-start = ((), (), s32[]{:S(2)}) async-start(), calls=%async_computation.3 | async-start | bytes 13107200 | tf_op jit(solution)/shard_map/reduce_scatter | solution.py:483
  1231.4 227.0 %copy-start.93 = (f32[3]{0:T(128)S(1)}, f32[3]{0:T(128)}, u32[]{:S(2)}) copy-start(f32[3]{0:T(128)} %copy-done.92) | copy-start | bytes 40
  1231.4 227.7 %copy-start.50 = (f32[11520]{0:T(1024)S(1)}, f32[11520]{0:T(1024)}, u32[]{:S(2)}) copy-start(f32[11520]{0:T(1024)} %param.19) | copy-start | bytes 138244
  1231.4 227.7 %copy-start.61 = (f32[11520]{0:T(1024)S(1)}, f32[11520]{0:T(1024)}, u32[]{:S(2)}) copy-start(f32[11520]{0:T(1024)} %param.21) | copy-start | bytes 138244
  1231.4 227.7 %copy-start.62 = (f32[11520]{0:T(1024)S(1)}, f32[11520]{0:T(1024)}, u32[]{:S(2)}) copy-start(f32[11520]{0:T(1024)} %param.20) | copy-start | bytes 138244
  1410.5 49.3 %copy-start.12 = (bf16[16,64,1280]{2,1,0:T(8,128)(2,1)S(1)}, bf16[16,64,1280]{2,1,0:T(8,128)(2,1)}, u32[]{:S(2)}) copy-start(bf16[16,64,1280]{2,1,0:T(8,128)(2,1)} %reduce-scatter.5.cloned.1.call-done) | copy-start | bytes 7864324
  (51 other events, 109.9 us)
Sparse Core Ops, SparseCore 0:
  11.7 439.6 all-gather.1
  769.0 461.0 reduce-scatter.6
  1232.4 178.0 reduce-scatter.4

commit v3 on v2

--- a/solution.py
+++ b/solution.py
@@ -224,6 +224,314 @@
         ),
         name=f"grad_{which}",
     )(owner, left, right, *held)
+
+
+CHUNKS = 16
+STEPS = CHUNKS + 7
+MESH = pl.DeviceIdType.MESH
+
+
+def total_of(*blocks):
+    result = blocks[0].astype(jnp.float32)
+    for block in blocks[1:]:
+        result = result + block.astype(jnp.float32)
+    return result
+
+
+def scatter_kernel(
+    slots_ref,
+    out_ref,
+    own,
+    pair_in,
+    pair_sum,
+    first_in,
+    second_in,
+    second_out,
+    column,
+    up_in,
+    down_in,
+    up_out,
+    down_out,
+    result,
+    own_sem,
+    pair_send,
+    pair_recv,
+    first_send,
+    first_recv,
+    second_send,
+    second_recv,
+    up_send,
+    up_recv,
+    down_send,
+    down_recv,
+    result_sem,
+):
+    wide, z = lax.axis_index("wide"), lax.axis_index("narrow")
+    core, here = lax.rem(wide, 2), lax.div(wide, 2)
+    x, y = lax.rem(here, 2), lax.div(here, 2)
+    far = 3 - here
+
+    def device(place, level):
+        return (place * 2 + core, level)
+
+    partner = (here * 2 + 1 - core, z)
+
+    def near(k, which):
+        along_y = lax.rem(k + which, 2)
+        return (y + along_y - 2 * y * along_y) * 2 + (x + (1 - along_y) - 2 * x * (1 - along_y))
+
+    barrier = pltpu.get_barrier_semaphore()
+    pl.semaphore_signal(barrier, inc=1, device_id=partner, device_id_type=MESH)
+    for which in range(2):
+        pl.semaphore_signal(
+            barrier, inc=1, device_id=device(near(0, which), z), device_id_type=MESH
+        )
+
+    @pl.when(z > 0)
+    def _():
+        pl.semaphore_signal(barrier, inc=1, device_id=device(here, z - 1), device_id_type=MESH)
+
+    @pl.when(z < 3)
+    def _():
+        pl.semaphore_signal(barrier, inc=1, device_id=device(here, z + 1), device_id_type=MESH)
+
+    pl.semaphore_wait(barrier, 3 + jnp.minimum(z, 1) + jnp.minimum(3 - z, 1))
+
+    def own_copy(k):
+        at = lax.rem(k, 2)
+        return pltpu.make_async_copy(slots_ref.at[:, core, :, k], own.at[at], own_sem.at[at])
+
+    def pair_copy(k):
+        at = lax.rem(k, 2)
+        return pltpu.make_async_remote_copy(
+            src_ref=slots_ref.at[:, 1 - core, :, k],
+            dst_ref=pair_in.at[at],
+            send_sem=pair_send.at[at],
+            recv_sem=pair_recv.at[at],
+            device_id=partner,
+            device_id_type=MESH,
+        )
+
+    def first_copy(k, part):
+        place = near(k, 0)
+        return pltpu.make_async_remote_copy(
+            src_ref=pair_sum.at[lax.rem(k, 3), far if part == 0 else place],
+            dst_ref=first_in.at[lax.rem(k, 5), part],
+            send_sem=first_send.at[lax.rem(k, 3), part],
+            recv_sem=first_recv.at[lax.rem(k, 5), part],
+            device_id=device(place, z),
+            device_id_type=MESH,
+        )
+
+    def second_copy(k):
+        return pltpu.make_async_remote_copy(
+            src_ref=second_out.at[lax.rem(k, 2)],
+            dst_ref=second_in.at[lax.rem(k, 4)],
+            send_sem=second_send.at[lax.rem(k, 2)],
+            recv_sem=second_recv.at[lax.rem(k, 4)],
+            device_id=device(near(k, 1), z),
+            device_id_type=MESH,
+        )
+
+    def line_copy(k, level, source, target, send, recv, step):
+        return pltpu.make_async_remote_copy(
+            src_ref=source.at[lax.rem(k, 2), level],
+            dst_ref=target.at[lax.rem(k, 6), level],
+            send_sem=send.at[lax.rem(k, 2), level],
+            recv_sem=recv.at[lax.rem(k, 6), level],
+            device_id=device(here, z + step),
+            device_id_type=MESH,
+        )
+
+    def up_copy(k, level):
+        return line_copy(k, level, up_out, up_in, up_send, up_recv, 1)
+
+    def down_copy(k, level):
+        return line_copy(k, level, down_out, down_in, down_send, down_recv, -1)
+
+    def result_copy(k):
+        at = lax.rem(k, 2)
+        return pltpu.make_async_copy(result.at[at], out_ref.at[k], result_sem.at[at])
+
+    def valid(k):
+        return jnp.logical_and(k >= 0, k < CHUNKS)
+
+    own_copy(0).start()
+    pair_copy(0).start()
+
+    def step(t, carry):
+        @pl.when(valid(t - 3))
+        def _():
+            first_copy(t - 3, 0).wait_send()
+            first_copy(t - 3, 1).wait_send()
+
+        @pl.when(valid(t))
+        def _():
+            own_copy(t).wait()
+            pair_copy(t).wait_recv()
+            at, ring = lax.rem(t, 2), lax.rem(t, 3)
+
+            def add(i, inner):
+                p, n = lax.div(i, 4), lax.rem(i, 4)
+                pair_sum[ring, p, n] = total_of(own[at, p, n], pair_in[at, p, n]).astype(
+                    jnp.bfloat16
+                )
+                return inner
+
+            lax.fori_loop(0, 16, add, 0)
+            first_copy(t, 0).start()
+            first_copy(t, 1).start()
+
+        @pl.when(valid(t - 1))
+        def _():
+            pair_copy(t - 1).wait_send()
+
+        @pl.when(t + 1 < CHUNKS)
+        def _():
+            own_copy(t + 1).start()
+            pair_copy(t + 1).start()
+
+        @pl.when(valid(t - 3))
+        def _():
+            second_copy(t - 3).wait_send()
+
+        @pl.when(valid(t - 1))
+        def _():
+            k = t - 1
+            first_copy(k, 0).wait_recv()
+            place = near(k, 1)
+
+            def add(n, inner):
+                second_out[lax.rem(k, 2), n] = total_of(
+                    pair_sum[lax.rem(k, 3), place, n], first_in[lax.rem(k, 5), 0, n]
+                ).astype(jnp.bfloat16)
+                return inner
+
+            lax.fori_loop(0, 4, add, 0)
+            second_copy(k).start()
+
+        @pl.when(valid(t - 2))
+        def _():
+            k = t - 2
+            first_copy(k, 1).wait_recv()
+            second_copy(k).wait_recv()
+
+            def add(n, inner):
+                column[lax.rem(k, 4), n] = total_of(
+                    pair_sum[lax.rem(k, 3), here, n],
+                    first_in[lax.rem(k, 5), 1, n],
+                    second_in[lax.rem(k, 4), n],
+                ).astype(jnp.bfloat16)
+                return inner
+
+            lax.fori_loop(0, 4, add, 0)
+
+        for lag, ahead, behind, copy, arrived, leaving in (
+            (z, lambda n: n > z, z > 0, up_copy, up_in, up_out),
+            (3 - z, lambda n: n < z, z < 3, down_copy, down_in, down_out),
+        ):
+            k = t - 2 - lag
+            for n in range(4):
+
+                @pl.when(jnp.logical_and(valid(k - 2), ahead(n)))
+                def _(n=n, k=k, copy=copy):
+                    copy(k - 2, n).wait_send()
+
+                @pl.when(
+                    jnp.logical_and(
+                        jnp.logical_and(valid(k), behind), jnp.logical_or(ahead(n), n == z)
+                    )
+                )
+                def _(n=n, k=k, copy=copy):
+                    copy(k, n).wait_recv()
+
+                moving = jnp.logical_and(valid(k), ahead(n))
+
+                @pl.when(jnp.logical_and(moving, behind))
+                def _(n=n, k=k, arrived=arrived, leaving=leaving):
+                    leaving[lax.rem(k, 2), n] = total_of(
+                        column[lax.rem(k, 4), n], arrived[lax.rem(k, 6), n]
+                    ).astype(jnp.bfloat16)
+
+                @pl.when(jnp.logical_and(moving, jnp.logical_not(behind)))
+                def _(n=n, k=k, leaving=leaving):
+                    leaving[lax.rem(k, 2), n] = column[lax.rem(k, 4), n]
+
+                @pl.when(moving)
+                def _(n=n, k=k, copy=copy):
+                    copy(k, n).start()
+
+        k = t - 5
+
+        @pl.when(valid(k - 2))
+        def _():
+            result_copy(k - 2).wait()
+
+        @pl.when(valid(k))
+        def _():
+            result[lax.rem(k, 2)] = column[lax.rem(k, 4), z].astype(jnp.float32)
+
+            @pl.when(z > 0)
+            def _():
+                result[lax.rem(k, 2)] += up_in[lax.rem(k, 6), z].astype(jnp.float32)
+
+            @pl.when(z < 3)
+            def _():
+                result[lax.rem(k, 2)] += down_in[lax.rem(k, 6), z].astype(jnp.float32)
+
+            result_copy(k).start()
+
+        return carry
+
+    lax.fori_loop(0, STEPS, step, 0)
+
+
+def scatter_sum(slots, slot_count):
+    wide, narrow = lax.axis_size("wide"), lax.axis_size("narrow")
+    if (wide, narrow, slot_count) != (8, 4, CHUNKS):
+        part = lax.psum_scatter(slots, "wide", scatter_dimension=0, tiled=True)
+        return lax.psum_scatter(
+            part.astype(jnp.float32), "narrow", scatter_dimension=0, tiled=True
+        )
+    low = functools.partial(pltpu.VMEM, dtype=jnp.bfloat16)
+    dma = pltpu.SemaphoreType.DMA
+    block = (BR, D)
+    return pl.pallas_call(
+        scatter_kernel,
+        out_shape=jax.ShapeDtypeStruct((slot_count,) + block, jnp.float32),
+        in_specs=[pl.BlockSpec(memory_space=pl.ANY)],
+        out_specs=pl.BlockSpec(memory_space=pl.ANY),
+        scratch_shapes=[
+            low((2, 4, 4) + block),
+            low((2, 4, 4) + block),
+            low((3, 4, 4) + block),
+            low((5, 2, 4) + block),
+            low((4, 4) + block),
+            low((2, 4) + block),
+            low((4, 4) + block),
+            low((6, 4) + block),
+            low((6, 4) + block),
+            low((2, 4) + block),
+            low((2, 4) + block),
+            pltpu.VMEM((2,) + block, jnp.float32),
+            dma((2,)),
+            dma((2,)),
+            dma((2,)),
+            dma((3, 2)),
+            dma((5, 2)),
+            dma((2,)),
+            dma((4,)),
+            dma((2, 4)),
+            dma((6, 4)),
+            dma((2, 4)),
+            dma((6, 4)),
+            dma((2,)),
+        ],
+        compiler_params=pltpu.CompilerParams(
+            collective_id=1, has_side_effects=True, vmem_limit_bytes=VMEM_LIMIT
+        ),
+        name="scatter_sum",
+    )(slots.reshape(4, 2, narrow, slot_count, BR, D))
 
 
 def split_small(small):
@@ -479,12 +787,11 @@
         ]
     )
     small_grad = lax.psum(small_local, ("wide", "narrow"))
-    partial_value = lax.psum_scatter(slots, "wide", scatter_dimension=0, tiled=True)
-    owned = lax.psum_scatter(partial_value, "narrow", scatter_dimension=0, tiled=True)
+    owned = scatter_sum(slots, slot_count)
     rank = lax.axis_index("wide") * lax.axis_size("narrow") + lax.axis_index("narrow")
     mine = rank * slot_count + jnp.arange(slot_count, dtype=jnp.int32)
     filled = jnp.any(owner[:, None] == mine[None, :], axis=0)
-    owned = jnp.where(filled[:, None, None], owned.astype(jnp.float32), 0.0)
+    owned = jnp.where(filled[:, None, None], owned, 0.0)
     local_square = jnp.sum(owned * owned)
     square_total = lax.psum(local_square, ("wide", "narrow"))
     grad_norm = jnp.sqrt(square_total + jnp.sum(small_grad * small_grad))

time: 1490 us -> 1240 us (0.83)
  waiting for transfers between devices: 1010 us -> 374 us
  Pallas kernels: 140 us -> 528 us
    unnamed x4 -> x1, waiting for transfers between devices: 461 us -> 0.02 us
    pallas_call x0 -> x1, Pallas kernels: none -> 387 us  [scatter_sum(): pl.pallas_call(scatter_kernel, out_shape=jax.ShapeDtypeStruct((slot_count...]
    reduce_scatter x1 -> x0, waiting for transfers between devices: 178 us -> none  [on_device(): lax.psum_scatter(partial_value, 'narrow', scatter_dimension=0, tiled=True)]
  transfers between devices with their start and end apart: 3 -> 1, of which waited for: 3 -> 1; matrix products, arithmetic and copies ran while one was open for 1% -> 1% of each run, Pallas kernels for 0% -> 0%
where the time goes in v3:
time: 1240 us; the launch traced here: 1230 us
  Pallas kernels  528 us (43%)
  waiting for transfers between devices  374 us (30%)
  matrix products  91.5 us (7%)
  blocking collectives  86.3 us (7%)
  local copies, waits for them, and re-layouts  83.3 us (7%)
  other arithmetic  43.9 us (4%)
  between operations  19.1 us (2%)
    pallas_call x1, Pallas kernels, scatter_sum(): pl.pallas_call(scatter_kernel, out_shape=jax.ShapeDtypeStruct((slot_count...  387 us
    all_gather x1, waiting for transfers between devices, on_device(): lax.all_gather(master.astype(jnp.bfloat16), ('wide', 'narrow'), axis=0, t...  374 us
    pallas_call x8, Pallas kernels, unpack(): pl.pallas_call(functools.partial(unpack_kernel, groups, count), out_shape...  73.5 us
    pallas_call x8, Pallas kernels, grad_blocks(): pl.pallas_call(functools.partial(grad_kernel, groups, count, BASES[which]...  67 us
    psum x1, blocking collectives, on_device(): counts = lax.psum(local_counts, ('wide', 'narrow'))  46.7 us
    dot_general x7, matrix products, backmul(): lax.dot_general(left, right, (((1,), (1,)), ((), ())), preferred_element_...  43.2 us
    dot_general x8, matrix products, matmul(): return jnp.dot(left, right, preferred_element_type=jnp.float32)  41.6 us
    psum x1, blocking collectives, on_device(): sums = lax.psum(local_sums, ('wide', 'narrow'))  39.6 us
  transfers between devices with their start and end apart: 1, of which 1 were waited for; matrix products, arithmetic and copies ran while one was open for 1% of the time, Pallas kernels for 0%

profile of v3, /device:TPU:0, one launch (start us, length us, event | category | flops | bytes accessed | tf_op | source)
XLA Modules:
  0.0 1225.8 jit_solution(17365800024397045363)
XLA Ops:
  7.2 4.3 convert_element_type.100
  12.6 5.5 gather_fusion.1
  18.4 46.7 %psum.29 = f32[3]{0:T(128)S(1)} all-reduce(f32[3]{0:T(128)S(1)} %select_reduce_fusion.3), channel_id=1, replica_groups=mesh['wide'=8,'narrow'=4] {'wide','narrow'}, use_global_device_ids=true, to_apply=%region_12.13 | all-reduce | flops 3 | bytes 24 | tf_op jit(solution)/shard_map/psum | solution.py:732
  65.6 5.5 gather_fusion
  77.7 373.6 %all-gather.2.cloned.1.call-done.refs_0_.refs_1_.refs_2_.refs_3_.refs_4_.refs_5_.refs_6_.refs_7_ = bf16[512,64,1280]{2,1,0:T(8,128)(2,1)} async-done(((bf16[16,64,1280]{2,1,0:T(8,128)(2,1)}), bf16[512,64,1280]{2,1,0:T(8,128)(2,1)}) %all-gather.2.cloned.1.call-update) | async-done | bytes 83886096 | tf_op jit(solution)/shard_map/all_gather | solution.py:714
  451.4 2.5 unpack_0.1
  455.8 6.0 unpack_1.1
  461.9 3.1 multiply_reduce_fusion.7
  466.3 12.8 %unpack_2.1 = bf16[1280,3840]{1,0:T(8,128)(2,1)} custom-call(s32[322]{0:T(512)} %owner_ref.31, bf16[512,64,1280]{2,1,0:T(8,128)(2,1)} %all-gather.2.cloned.1.call-done.refs_0_.refs_1_.refs_2_.refs_3_.refs_4_.refs_5_.refs_6_.refs_7_, bf16[512,64,1280]{2,1,0:T(8,128)(2,1)} %all-gather.2.cloned.1.call-done.refs_0_.refs_1_.refs_2_.refs_3_.refs_4_.refs_5_.refs_6_.refs_7_, ...), custom_call_target="tpu_custom_call" | custom-call | bytes 19660800 | tf_op jit(solution)/shard_map/unpack_2/pallas_call | solution.py:125
  479.1 8.4 fusion.63
  487.5 8.0 reshape.305
  495.5 2.6 fusion.57
  508.6 6.1 unpack_3.1
  514.7 3.0 multiply_reduce_fusion.6
  519.9 15.8 %unpack_4.1 = bf16[1280,5120]{1,0:T(8,128)(2,1)} custom-call(s32[322]{0:T(512)} %owner_ref.31, bf16[512,64,1280]{2,1,0:T(8,128)(2,1)} %all-gather.2.cloned.1.call-done.refs_0_.refs_1_.refs_2_.refs_3_.refs_4_.refs_5_.refs_6_.refs_7_, bf16[512,64,1280]{2,1,0:T(8,128)(2,1)} %all-gather.2.cloned.1.call-done.refs_0_.refs_1_.refs_2_.refs_3_.refs_4_.refs_5_.refs_6_.refs_7_, ...), custom_call_target="tpu_custom_call" | custom-call | bytes 26214400 | tf_op jit(solution)/shard_map/unpack_4/pallas_call | solution.py:125
  535.8 11.2 divide_convert_fusion
  546.9 13.6 %unpack_5.1 = bf16[5120,1280]{1,0:T(8,128)(2,1)} custom-call(s32[322]{0:T(512)} %owner_ref.31, bf16[512,64,1280]{2,1,0:T(8,128)(2,1)} %all-gather.2.cloned.1.call-done.refs_0_.refs_1_.refs_2_.refs_3_.refs_4_.refs_5_.refs_6_.refs_7_, bf16[512,64,1280]{2,1,0:T(8,128)(2,1)} %all-gather.2.cloned.1.call-done.refs_0_.refs_1_.refs_2_.refs_3_.refs_4_.refs_5_.refs_6_.refs_7_, ...), custom_call_target="tpu_custom_call" | custom-call | bytes 26214400 | tf_op jit(solution)/shard_map/unpack_5/pallas_call | solution.py:125
  560.6 6.8 fusion.5.left_ref
  567.3 10.5 unpack_6.1
  577.8 4.7 fusion.64
  583.0 6.2 unpack_7.1
  589.2 2.9 fusion.3
  592.5 6.1 reshape.307
  598.6 7.9 slice.161
  606.5 6.0 copy.162
  615.4 3.8 copy.149
  619.3 7.7 convert_element_type.113
  627.0 4.1 fusion.58
  632.5 6.1 fusion.61
  638.6 11.7 fusion.right_ref
  650.3 8.9 multiply_reduce_fusion.2
  663.6 2.8 reshape.308
  676.3 2.5 copy.154
  678.8 5.1 convert_element_type.120.right_ref
  683.9 8.0 multiply_reduce_fusion.3
  693.3 6.8 grad_7.1.refs_0_
  702.3 2.5 fusion.59
  706.5 9.7 grad_6.1.refs_0_
  716.2 11.3 grad_5.1.refs_0_
  727.5 12.5 %grad_4.1.refs_0_ = bf16[512,64,1280]{2,1,0:T(8,128)(2,1)} custom-call(s32[322]{0:T(512)} %owner_ref.31, bf16[256,1280]{1,0:T(8,128)(2,1)} %multiply_convert_fusion.1.left_ref, bf16[256,5120]{1,0:T(8,128)(2,1)} %fusion.right_ref, bf16[512,64,1280]{2,1,0:T(8,128)(2,1)} %grad_5.1.refs_0_), custom_call_target="tpu_custom_call", output_to_operand_aliasing={{}: (3, {})} | custom-call | flops 3355443200 | bytes 13107200 | tf_op jit(solution)/shard_map/grad_4/pallas_call | solution.py:204
  740.1 6.2 grad_3.1.refs_0_
  746.2 11.0 grad_2.1.refs_0_
  757.3 6.2 grad_1.1.refs_0_
  764.7 3.2 grad_0.1
  768.0 387.4 %scatter_sum.1 = f32[16,64,1280]{2,1,0:T(8,128)} custom-call(bf16[4,2,4,16,64,1280]{5,4,3,2,1,0:T(8,128)(2,1)} %bitcast.29.slots_ref), custom_call_target="tpu_custom_call" | custom-call | tf_op jit(solution)/shard_map/scatter_sum/pallas_call | solution.py:499
  1155.6 4.5 multiply_reduce_fusion
  1160.2 39.6 %all-reduce.4 = (f32[2,3]{1,0:T(2,128)S(1)}, f32[]{:T(128)}, f32[11520]{0:T(1024)S(1)}) all-reduce(f32[2,3]{1,0:T(2,128)S(1)} %pad_maximum_fusion.7, f32[]{:T(128)} %multiply_reduce_fusion, f32[11520]{0:T(1024)S(1)} %constant_dynamic-update-slice_fusion), channel_id=1, replica_groups=mesh['wide'=8,'narrow'=4] {'wide','narrow'}, use_global_device_ids=true, to_apply=%region_9.10 | all-reduce | flops 11527 | bytes 92216 | tf_op jit(solution)/shard_map/psum | solution.py:753
  1203.1 14.2 %fusion.51 = (bf16[16,64,1280]{2,1,0:T(8,128)(2,1)}, f32[16,64,1280]{2,1,0:T(8,128)}, f32[16,64,1280]{2,1,0:T(8,128)}, f32[16,64,1280]{2,1,0:T(8,128)}) fusion(f32[16,64,1280]{2,1,0:T(8,128)} %param.16, f32[]{:T(128)} %bitcast.31, f32[]{:T(128)S(6)} %min.3, f32[16,64,1280]{2,1,0:T(8,128)} %scatter_sum.1, pred[16]{0:T(512)(128)(4,1)S(1)} %copy-done.84, ...), kind=kLoop, calls=%fused_computation.160 | loop fusion | flops 22282240 | bytes 39321624 | tf_op jit(solution)/shard_map/convert_element_type | solution.py:810
  (280 shorter events, 50.9 us)
Async XLA Ops:
  7.2 444.2 %all-gather.2.cloned.1.call-start = ((), (), s32[]{:S(2)}) async-start(), calls=%async_computation | async-start | bytes 86507520 | tf_op jit(solution)/shard_map/all_gather | solution.py:714
  11.5 6.8 copy-start.81
  11.5 53.6 %copy-start.48 = (f32[16,640]{1,0:T(8,128)S(1)}, f32[16,640]{1,0:T(8,128)}, u32[]{:S(2)}) copy-start(f32[16,640]{1,0:T(8,128)} %param.11) | copy-start | bytes 122884
  12.3 53.3 %slice-start.1 = ((f32[11520]{0:T(1024)}), f32[3840]{0:T(1024)S(1)}, s32[]{:S(2)}) async-start(f32[11520]{0:T(1024)} %param.19), calls=%async_computation.2 | async-start | bytes 32768 | tf_op jit(solution)/shard_map/slice | solution.py:538
  65.1 9.7 copy-start.42
  65.3 11.6 copy-start.45
  74.2 379.6 %copy-start.91 = (f32[3]{0:T(128)}, f32[3]{0:T(128)S(1)}, u32[]{:S(2)}) copy-start(f32[3]{0:T(128)S(1)} %get-tuple-element.36) | copy-start | bytes 40
  75.6 378.2 %copy-start.41 = (bf16[256,64]{1,0:T(8,128)(2,1)}, bf16[256,64]{1,0:T(8,128)(2,1)S(1)}, u32[]{:S(2)}) copy-start(bf16[256,64]{1,0:T(8,128)(2,1)S(1)} %pad_maximum_fusion.6.left_ref) | copy-start | bytes 98308
  77.5 377.8 %copy-start.61 = (f32[1280]{0:T(1024)}, f32[1280]{0:T(1024)S(1)}, u32[]{:S(2)}) copy-start(f32[1280]{0:T(1024)S(1)} %get-tuple-element.56) | copy-start | bytes 15364
  77.5 387.6 %copy-start.51 = (f32[1280]{0:T(1024)}, f32[1280]{0:T(1024)S(1)}, u32[]{:S(2)}) copy-start(f32[1280]{0:T(1024)S(1)} %get-tuple-element.54) | copy-start | bytes 15364
  455.3 6.6 copy-start.10
  465.0 14.1 %copy-start.70 = (f32[256]{0:T(256)}, f32[256]{0:T(256)S(1)}, u32[]{:S(2)}) copy-start(f32[256]{0:T(256)S(1)} %get-tuple-element.66) | copy-start | bytes 3076
  466.3 12.8 %copy-start.32 = (bf16[256,1280]{1,0:T(8,128)(2,1)}, bf16[256,1280]{1,0:T(8,128)(2,1)S(1)}, u32[]{:S(2)}) copy-start(bf16[256,1280]{1,0:T(8,128)(2,1)S(1)} %multiply_convert_fusion.2.left_ref) | copy-start | bytes 1966084
  517.7 18.0 %copy-start.74 = (f32[256]{0:T(256)}, f32[256]{0:T(256)S(1)}, u32[]{:S(2)}) copy-start(f32[256]{0:T(256)S(1)} %get-tuple-element.70) | copy-start | bytes 3076
  519.9 15.8 %copy-start.29 = (bf16[256,1280]{1,0:T(8,128)(2,1)S(1)}, bf16[256,1280]{1,0:T(8,128)(2,1)}, u32[]{:S(2)}) copy-start(bf16[256,1280]{1,0:T(8,128)(2,1)} %multiply_convert_fusion.1.left_ref) | copy-start | bytes 1966084
  546.9 13.6 %copy-start.8 = (f32[256,1280]{1,0:T(8,128)S(1)}, f32[256,1280]{1,0:T(8,128)}, u32[]{:S(2)}) copy-start(f32[256,1280]{1,0:T(8,128)} %copy-done.7) | copy-start | bytes 3932164
  546.9 13.6 %copy-start.31 = (bf16[256,5120]{1,0:T(8,128)(2,1)S(1)}, bf16[256,5120]{1,0:T(8,128)(2,1)}, u32[]{:S(2)}) copy-start(bf16[256,5120]{1,0:T(8,128)(2,1)} %get-tuple-element.72.left_ref) | copy-start | bytes 7864324
  567.3 10.5 copy-start.37
  582.6 6.6 copy-start.40
  606.5 6.5 copy-start.27
  606.5 6.5 copy-start.85
  606.5 6.5 copy-start.86
  619.3 7.7 copy-start.28
  638.6 11.7 copy-start.9
  638.6 11.7 copy-start.56
  638.6 11.7 copy-start.73
  650.3 8.9 copy-start.75
  683.9 8.0 copy-start.18
  683.9 8.0 copy-start.71
  683.9 8.0 copy-start.25
  693.0 8.3 copy-start.22
  693.2 6.8 copy-start.20
  693.2 6.8 copy-start.38
  693.2 8.1 copy-start.5
  693.2 8.0 copy-start.62
  767.9 387.5 %copy-start.57 = (f32[3840]{0:T(1024)S(1)}, f32[3840]{0:T(1024)}, u32[]{:S(2)}) copy-start(f32[3840]{0:T(1024)} %reshape.311) | copy-start | bytes 46084
  767.9 387.5 %copy-start.58 = (f32[11520]{0:T(1024)S(1)}, f32[11520]{0:T(1024)}, u32[]{:S(2)}) copy-start(f32[11520]{0:T(1024)} %custom-call) | copy-start | bytes 138244
  767.9 387.5 %copy-start.80 = (f32[1280]{0:T(1024)S(1)}, f32[1280]{0:T(1024)}, u32[]{:S(2)}) copy-start(f32[1280]{0:T(1024)} %get-tuple-element.49) | copy-start | bytes 15364
  768.0 387.5 %copy-start.66 = (f32[1280]{0:T(1024)S(1)}, f32[1280]{0:T(1024)}, u32[]{:S(2)}) copy-start(f32[1280]{0:T(1024)} %get-tuple-element.31) | copy-start | bytes 15364
  768.0 387.5 %copy-start.79 = (f32[1280]{0:T(1024)S(1)}, f32[1280]{0:T(1024)}, u32[]{:S(2)}) copy-start(f32[1280]{0:T(1024)} %get-tuple-element.11) | copy-start | bytes 15364
  768.0 387.5 %copy-start.78 = (f32[1280]{0:T(1024)S(1)}, f32[1280]{0:T(1024)}, u32[]{:S(2)}) copy-start(f32[1280]{0:T(1024)} %get-tuple-element.9) | copy-start | bytes 15364
  768.0 387.5 %copy-start.77 = (f32[1280]{0:T(1024)S(1)}, f32[1280]{0:T(1024)}, u32[]{:S(2)}) copy-start(f32[1280]{0:T(1024)} %get-tuple-element.47) | copy-start | bytes 15364
  768.0 387.5 %copy-start.67 = (f32[1280]{0:T(1024)S(1)}, f32[1280]{0:T(1024)}, u32[]{:S(2)}) copy-start(f32[1280]{0:T(1024)} %reduce_sum.295) | copy-start | bytes 15364
  768.0 387.6 %copy-start.84 = (pred[16]{0:T(512)(128)(4,1)S(1)}, pred[16]{0:T(512)(128)(4,1)}, u32[]{:S(2)}) copy-start(pred[16]{0:T(512)(128)(4,1)} %compare_reduce_fusion) | copy-start | bytes 52
  1155.6 46.1 %copy-start.92 = (f32[3]{0:T(128)S(1)}, f32[3]{0:T(128)}, u32[]{:S(2)}) copy-start(f32[3]{0:T(128)} %copy-done.91) | copy-start | bytes 40
  1155.6 46.8 %copy-start.46 = (f32[11520]{0:T(1024)S(1)}, f32[11520]{0:T(1024)}, u32[]{:S(2)}) copy-start(f32[11520]{0:T(1024)} %param.19) | copy-start | bytes 138244
  1155.6 46.8 %copy-start.59 = (f32[11520]{0:T(1024)S(1)}, f32[11520]{0:T(1024)}, u32[]{:S(2)}) copy-start(f32[11520]{0:T(1024)} %param.21) | copy-start | bytes 138244
  1155.6 46.8 %copy-start.60 = (f32[11520]{0:T(1024)S(1)}, f32[11520]{0:T(1024)}, u32[]{:S(2)}) copy-start(f32[11520]{0:T(1024)} %param.20) | copy-start | bytes 138244
  (48 other events, 151.2 us)
Sparse Core Ops, SparseCore 0:
  11.7 439.6 all-gather.1

commit v4 on v3

--- a/solution.py
+++ b/solution.py
@@ -534,6 +534,331 @@
     )(slots.reshape(4, 2, narrow, slot_count, BR, D))
 
 
+LATE = 4
+EARLY = CHUNKS - LATE
+COMBOS = 4 * LATE
+GATHER_STEPS = EARLY + 5
+
+
+def gather_kernel(
+    own_ref,
+    count_ref,
+    all_ref,
+    counts_ref,
+    own_sem,
+    recv,
+    pair_recv,
+    line_send,
+    plane_send,
+    turn_send,
+    late_send,
+    pair_send,
+    late_pair_send,
+    count_send,
+    count_recv,
+):
+    wide, z = lax.axis_index("wide"), lax.axis_index("narrow")
+    core, here = lax.rem(wide, 2), lax.div(wide, 2)
+    x, y = lax.rem(here, 2), lax.div(here, 2)
+    side, front, far = y * 2 + 1 - x, (1 - y) * 2 + x, 3 - here
+    places = 8 * 4
+    me = wide * 4 + z
+
+    barrier = pltpu.get_barrier_semaphore()
+
+    def greet(i, carry):
+        other = lax.rem(me + i, places)
+        pl.semaphore_signal(
+            barrier,
+            inc=1,
+            device_id=(lax.div(other, 4), lax.rem(other, 4)),
+            device_id_type=MESH,
+        )
+        return carry
+
+    lax.fori_loop(1, places, greet, 0)
+    fill = pltpu.make_async_copy(own_ref, all_ref.at[here, core, z], own_sem)
+    fill.start()
+    counts_ref[me] = count_ref[...]
+    pl.semaphore_wait(barrier, places - 1)
+    fill.wait()
+
+    def count_copy(i):
+        other = lax.rem(me + i, places)
+        return pltpu.make_async_remote_copy(
+            src_ref=count_ref,
+            dst_ref=counts_ref.at[me],
+            send_sem=count_send.at[i],
+            recv_sem=count_recv.at[i],
+            device_id=(lax.div(other, 4), lax.rem(other, 4)),
+            device_id_type=MESH,
+        )
+
+    def count_start(i, carry):
+        count_copy(i).start()
+        return carry
+
+    lax.fori_loop(1, places, count_start, 0)
+
+    def piece(p, n, k, send, to):
+        return pltpu.make_async_remote_copy(
+            src_ref=all_ref.at[p, core, n, k],
+            dst_ref=all_ref.at[p, core, n, k],
+            send_sem=send,
+            recv_sem=recv.at[p, n, k],
+            device_id=to,
+            device_id_type=MESH,
+        )
+
+    up, down = (wide, z + 1), (wide, z - 1)
+    to_side, to_front = (side * 2 + core, z), (front * 2 + core, z)
+
+    def line(n, k, step):
+        return piece(here, n, k, line_send.at[step, n, k], (up, down)[step])
+
+    def plane(n, k, which):
+        return piece(here, n, k, plane_send.at[which, n, k], (to_side, to_front)[which])
+
+    def turn(n, k, which):
+        return piece(
+            (side, front)[which], n, k, turn_send.at[n, k], (to_front, to_side)[which]
+        )
+
+    def late(c, n, step):
+        p, k = lax.rem(here + c, 4), EARLY + lax.div(c, 4)
+        return piece(p, n, k, late_send.at[step, c, n], (up, down)[step])
+
+    def pair(p, k, send):
+        return pltpu.make_async_remote_copy(
+            src_ref=all_ref.at[p, core, :, k],
+            dst_ref=all_ref.at[p, core, :, k],
+            send_sem=send,
+            recv_sem=pair_recv,
+            device_id=(here * 2 + 1 - core, z),
+            device_id_type=MESH,
+        )
+
+    def early_pair(p, k):
+        return pair(p, k, pair_send.at[p, k])
+
+    def late_pair(c):
+        p, k = lax.rem(here + c, 4), EARLY + lax.div(c, 4)
+        return pair(p, k, late_pair_send.at[c])
+
+    def both_lines(make, n, j, start):
+        @pl.when(jnp.logical_and(start, z < 3))
+        def _():
+            if j <= 0:
+                make(n, 0)
+
+        @pl.when(jnp.logical_and(start, z > 0))
+        def _():
+            if j >= 0:
+                make(n, 1)
+
+    def early(k):
+        return jnp.logical_and(k >= 0, k < EARLY)
+
+    def swap(n, k, go):
+        even = lax.rem(n + k, 2) == 0
+
+        @pl.when(jnp.logical_and(go, even))
+        def _():
+            turn(n, k, 0).start()
+
+        @pl.when(jnp.logical_and(go, jnp.logical_not(even)))
+        def _():
+            turn(n, k, 1).start()
+
+    for k in range(EARLY, CHUNKS):
+        plane(z, k, 0).start()
+        plane(z, k, 1).start()
+
+    def step(t, carry):
+        @pl.when(early(t))
+        def _():
+            plane(z, t, 0).start()
+            plane(z, t, 1).start()
+
+        both_lines(lambda n, way: line(n, t, way).start(), z, 0, early(t))
+
+        for j in (-1, 1, -2, 2, -3, 3):
+            n, k = z + j, t - abs(j)
+            there = jnp.logical_and(early(k), jnp.logical_and(n >= 0, n < 4))
+
+            @pl.when(there)
+            def _(n=n, k=k, j=j):
+                piece(here, n, k, plane_send.at[0, n, k], to_side).wait_recv()
+
+            both_lines(lambda n, way, k=k: line(n, k, way).start(), n, j, there)
+
+            @pl.when(there)
+            def _(n=n, k=k):
+                plane(n, k, 0).start()
+                plane(n, k, 1).start()
+
+        @pl.when(t == 1)
+        def _():
+            for k in range(EARLY, CHUNKS):
+                plane_wait(side, z, k)
+                plane_wait(front, z, k)
+                swap(z, k, True)
+
+        @pl.when(t == 2)
+        def _():
+            for k in range(EARLY, CHUNKS):
+                plane_wait(far, z, k)
+
+        for j in (0, -1, 1, -2, 2, -3, 3):
+            m = t - 2 - abs(j)
+            n = z + j
+            first = m + lax.div(m + 2, 3)
+            for c, more in ((first, True), (first + 1, lax.rem(m, 3) == 0)):
+                there = jnp.logical_and(
+                    jnp.logical_and(m >= 0, c < COMBOS),
+                    jnp.logical_and(jnp.logical_and(n >= 0, n < 4), more),
+                )
+                if j:
+
+                    @pl.when(there)
+                    def _(n=n, c=c):
+                        plane_wait(lax.rem(here + c, 4), n, EARLY + lax.div(c, 4))
+
+                both_lines(lambda n, way, c=c: late(c, n, way).start(), n, j, there)
+
+        for n in range(4):
+            gap = jnp.abs(z - n)
+            k = t - 1 - gap
+
+            @pl.when(early(k))
+            def _(n=n, k=k):
+                plane_wait(side, n, k)
+                plane_wait(front, n, k)
+
+            swap(n, k, early(k))
+            k = t - 2 - gap
+
+            @pl.when(early(k))
+            def _(n=n, k=k):
+                plane_wait(far, n, k)
+
+        for lag, sent in ((3, (here,)), (4, (side, front)), (5, (far,))):
+            k = t - lag
+
+            @pl.when(early(k))
+            def _(k=k, sent=sent):
+                for p in sent:
+                    early_pair(p, k).start()
+
+        m = t - 5
+        first = m + lax.div(m + 2, 3)
+        for c, more in ((first, True), (first + 1, lax.rem(m, 3) == 0)):
+
+            @pl.when(jnp.logical_and(jnp.logical_and(m >= 0, c < COMBOS), more))
+            def _(c=c):
+                late_pair(c).start()
+
+        return carry
+
+    def plane_wait(p, n, k):
+        piece(p, n, k, plane_send.at[0, n, k], to_side).wait_recv()
+
+    lax.fori_loop(0, GATHER_STEPS, step, 0)
+
+    def finish(k, carry):
+        for n in range(4):
+            plane_used = jnp.logical_or(k < EARLY, n == z)
+
+            @pl.when(plane_used)
+            def _(n=n):
+                plane(n, k, 0).wait_send()
+                plane(n, k, 1).wait_send()
+                turn(n, k, 0).wait_send()
+
+            @pl.when(jnp.logical_and(k < EARLY, jnp.logical_and(n <= z, z < 3)))
+            def _(n=n):
+                line(n, k, 0).wait_send()
+
+            @pl.when(jnp.logical_and(k < EARLY, jnp.logical_and(n >= z, z > 0)))
+            def _(n=n):
+                line(n, k, 1).wait_send()
+
+            @pl.when(jnp.logical_and(n <= z, z < 3))
+            def _(n=n):
+                late(k, n, 0).wait_send()
+
+            @pl.when(jnp.logical_and(n >= z, z > 0))
+            def _(n=n):
+                late(k, n, 1).wait_send()
+
+        @pl.when(k < EARLY)
+        def _():
+            for p in range(4):
+                early_pair(p, k).wait_send()
+
+        late_pair(k).wait_send()
+        return carry
+
+    lax.fori_loop(0, CHUNKS, finish, 0)
+
+    def count_wait(i, carry):
+        count_copy(i).wait()
+        return carry
+
+    lax.fori_loop(1, places, count_wait, 0)
+    pltpu.make_async_copy(
+        all_ref.at[:, 1 - core], all_ref.at[:, 1 - core], pair_recv
+    ).wait()
+
+
+def gather_all(low, local_counts):
+    slot_count = low.shape[0]
+    wide, narrow = lax.axis_size("wide"), lax.axis_size("narrow")
+    if (wide, narrow, slot_count) != (8, 4, CHUNKS):
+        return (
+            lax.all_gather(low, ("wide", "narrow"), axis=0, tiled=True),
+            lax.psum(local_counts, ("wide", "narrow")),
+        )
+    dma = pltpu.SemaphoreType.DMA
+    tile = jnp.zeros((8, LANES), jnp.float32).at[0, :NCLASS].set(local_counts)
+    gathered, tiles = pl.pallas_call(
+        gather_kernel,
+        out_shape=(
+            jax.ShapeDtypeStruct((4, 2, narrow, slot_count, BR, D), jnp.bfloat16),
+            jax.ShapeDtypeStruct((wide * narrow, 8, LANES), jnp.float32),
+        ),
+        in_specs=[
+            pl.BlockSpec(memory_space=pltpu.VMEM),
+            pl.BlockSpec(memory_space=pltpu.VMEM),
+        ],
+        out_specs=(
+            pl.BlockSpec(memory_space=pl.ANY),
+            pl.BlockSpec(memory_space=pltpu.VMEM),
+        ),
+        scratch_shapes=[
+            dma,
+            dma((4, 4, CHUNKS)),
+            dma,
+            dma((2, 4, EARLY)),
+            dma((2, 4, CHUNKS)),
+            dma((4, CHUNKS)),
+            dma((2, COMBOS, 4)),
+            dma((4, EARLY)),
+            dma((COMBOS,)),
+            dma((wide * narrow,)),
+            dma((wide * narrow,)),
+        ],
+        compiler_params=pltpu.CompilerParams(
+            collective_id=2, has_side_effects=True, vmem_limit_bytes=VMEM_LIMIT
+        ),
+        name="gather_all",
+    )(low, tile)
+    return (
+        gathered.reshape(wide * narrow * slot_count, BR, D),
+        jnp.sum(tiles[:, 0, :NCLASS], axis=0),
+    )
+
+
 def split_small(small):
     freq = small[: NCLASS * D].reshape(NCLASS, D)
     rest = small[NCLASS * D :]
@@ -711,9 +1036,6 @@
     small_m2,
 ):
     slot_count = master.shape[0]
-    gathered = lax.all_gather(master.astype(jnp.bfloat16), ("wide", "narrow"), axis=0, tiled=True)
-    mats = tuple(unpack(gathered, owner, which) for which in range(len(MATS)))
-    tok_in, tok_out, head_in, head_out = (mats[0], mats[1], mats[6], mats[7])
     parts = split_small(small_master)
     freq, bias_one, bias_two, head_bias, out_bias = (
         parts[0],
@@ -729,7 +1051,9 @@
         jnp.float32
     )
     local_counts = jnp.sum(onehot * jnp.sum(tmask, axis=(1, 2))[:, None], 0)
-    counts = lax.psum(local_counts, ("wide", "narrow"))
+    gathered, counts = gather_all(master.astype(jnp.bfloat16), local_counts)
+    mats = tuple(unpack(gathered, owner, which) for which in range(len(MATS)))
+    tok_in, tok_out, head_in, head_out = (mats[0], mats[1], mats[6], mats[7])
     class_weight = 1.0 / (counts * NCLASS)
     cosine, sine = tables()
     causal = jnp.arange(NPATCH)[:, None] >= jnp.arange(NPATCH)[None, :]

time: 1240 us -> 1140 us (0.919)
  waiting for transfers between devices: 374 us -> 0 us
  Pallas kernels: 528 us -> 862 us
  blocking collectives: 86.3 us -> 38.7 us
  between operations: 19.1 us -> 5.82 us
    all_gather x1 -> x0, waiting for transfers between devices: 374 us -> none  [on_device(): lax.all_gather(master.astype(jnp.bfloat16), ('wide', 'narrow'), axis=0, t...]
    pallas_call x0 -> x1, Pallas kernels: none -> 336 us  [gather_all(): pl.pallas_call(gather_kernel, out_shape=(jax.ShapeDtypeStruct((4, 2, narr...]
    psum x1 -> x0, blocking collectives: 46.7 us -> none  [on_device(): counts = lax.psum(local_counts, ('wide', 'narrow'))]
  transfers between devices with their start and end apart: 1 -> 0, of which waited for: 1 -> 0; matrix products, arithmetic and copies ran while one was open for 1% -> 0% of each run, Pallas kernels for 0% -> 0%
where the time goes in v4:
time: 1140 us; the launch traced here: 1130 us
  Pallas kernels  862 us (76%)
  matrix products  92.3 us (8%)
  local copies, waits for them, and re-layouts  82.9 us (7%)
  other arithmetic  45.5 us (4%)
  blocking collectives  38.7 us (3%)
    pallas_call x1, Pallas kernels, scatter_sum(): pl.pallas_call(scatter_kernel, out_shape=jax.ShapeDtypeStruct((slot_count...  386 us
    pallas_call x1, Pallas kernels, gather_all(): pl.pallas_call(gather_kernel, out_shape=(jax.ShapeDtypeStruct((4, 2, narr...  336 us
    pallas_call x8, Pallas kernels, unpack(): pl.pallas_call(functools.partial(unpack_kernel, groups, count), out_shape...  73.7 us
    pallas_call x8, Pallas kernels, grad_blocks(): pl.pallas_call(functools.partial(grad_kernel, groups, count, BASES[which]...  66.4 us
    dot_general x7, matrix products, backmul(): lax.dot_general(left, right, (((1,), (1,)), ((), ())), preferred_element_...  43.9 us
    dot_general x8, matrix products, matmul(): return jnp.dot(left, right, preferred_element_type=jnp.float32)  41.6 us
    psum x1, blocking collectives, on_device(): sums = lax.psum(local_sums, ('wide', 'narrow'))  38.7 us

profile of v4, /device:TPU:0, one launch (start us, length us, event | category | flops | bytes accessed | tf_op | source)
XLA Modules:
  0.0 1127.5 jit_solution(5635172319021916342)
XLA Ops:
  1.7 5.5 gather_fusion
  8.2 4.3 convert_element_type.100.own_ref
  12.5 336.2 %gather_all.1 = (bf16[4,2,4,16,64,1280]{5,4,3,2,1,0:T(8,128)(2,1)}, f32[32,8,128]{2,1,0:T(8,128)}) custom-call(bf16[16,64,1280]{2,1,0:T(8,128)(2,1)} %convert_element_type.100.own_ref, f32[8,128]{1,0:T(8,128)} %scatter.4.count_ref), custom_call_target="tpu_custom_call" | custom-call | tf_op jit(solution)/shard_map/gather_all/pallas_call | solution.py:824
  348.7 2.6 unpack_0.1
  355.1 6.2 unpack_1.1
  361.6 3.1 multiply_reduce_fusion.7
  366.0 12.8 %unpack_2.1 = bf16[1280,3840]{1,0:T(8,128)(2,1)} custom-call(s32[322]{0:T(512)} %owner_ref.31, bf16[512,64,1280]{2,1,0:T(8,128)(2,1)} %bitcast.2.refs_0_.refs_1_.refs_2_.refs_3_.refs_4_.refs_5_.refs_6_.refs_7_, bf16[512,64,1280]{2,1,0:T(8,128)(2,1)} %bitcast.2.refs_0_.refs_1_.refs_2_.refs_3_.refs_4_.refs_5_.refs_6_.refs_7_, ...), custom_call_target="tpu_custom_call" | custom-call | bytes 19660800 | tf_op jit(solution)/shard_map/unpack_2/pallas_call | solution.py:125
  378.8 8.4 fusion.63
  387.2 8.0 reshape.361
  395.2 2.6 fusion.57
  409.2 6.1 unpack_3.1
  415.3 3.0 multiply_reduce_fusion.6
  420.5 15.8 %unpack_4.1 = bf16[1280,5120]{1,0:T(8,128)(2,1)} custom-call(s32[322]{0:T(512)} %owner_ref.31, bf16[512,64,1280]{2,1,0:T(8,128)(2,1)} %bitcast.2.refs_0_.refs_1_.refs_2_.refs_3_.refs_4_.refs_5_.refs_6_.refs_7_, bf16[512,64,1280]{2,1,0:T(8,128)(2,1)} %bitcast.2.refs_0_.refs_1_.refs_2_.refs_3_.refs_4_.refs_5_.refs_6_.refs_7_, ...), custom_call_target="tpu_custom_call" | custom-call | bytes 26214400 | tf_op jit(solution)/shard_map/unpack_4/pallas_call | solution.py:125
  436.4 11.2 divide_convert_fusion
  447.5 13.6 %unpack_5.1 = bf16[5120,1280]{1,0:T(8,128)(2,1)} custom-call(s32[322]{0:T(512)} %owner_ref.31, bf16[512,64,1280]{2,1,0:T(8,128)(2,1)} %bitcast.2.refs_0_.refs_1_.refs_2_.refs_3_.refs_4_.refs_5_.refs_6_.refs_7_, bf16[512,64,1280]{2,1,0:T(8,128)(2,1)} %bitcast.2.refs_0_.refs_1_.refs_2_.refs_3_.refs_4_.refs_5_.refs_6_.refs_7_, ...), custom_call_target="tpu_custom_call" | custom-call | bytes 26214400 | tf_op jit(solution)/shard_map/unpack_5/pallas_call | solution.py:125
  461.2 6.8 fusion.5.left_ref
  467.9 10.5 unpack_6.1
  478.4 4.7 fusion.64
  483.6 6.1 unpack_7.1
  489.7 2.9 fusion.3
  493.1 6.0 reshape.363
  499.1 7.9 slice.181
  507.0 5.9 copy.139
  513.1 5.5 gather_fusion.1
  525.6 4.0 copy.126
  529.6 7.6 convert_element_type.113
  537.1 3.5 fusion.58
  542.0 5.2 fusion.61
  547.2 15.6 %fusion.right_ref = bf16[256,5120]{1,0:T(8,128)(2,1)} fusion(bf16[256,1280]{1,0:T(8,128)(2,1)S(1)} %get-tuple-element.91.right_ref, bf16[5120,1280]{1,0:T(8,128)(2,1)} %unpack_5.1, f32[256,5120]{1,0:T(8,128)} %get-tuple-element.89), kind=kOutput, calls=%fused_computation.5 | convolution fusion | flops 3367239680 | bytes 21626880 | tf_op jit(solution)/shard_map/dot_general | solution.py:45
  562.8 8.3 multiply_reduce_fusion.2
  575.5 2.8 reshape.364
  578.4 2.3 multiply_reduce_fusion.1
  588.3 2.5 copy.131
  590.8 5.4 convert_element_type.120.right_ref
  596.2 7.4 multiply_reduce_fusion.3
  606.4 2.0 fusion.59
  609.1 6.2 grad_7.1.refs_0_
  616.6 9.7 grad_6.1.refs_0_
  626.3 11.3 grad_5.1.refs_0_
  637.6 12.6 %grad_4.1.refs_0_ = bf16[512,64,1280]{2,1,0:T(8,128)(2,1)} custom-call(s32[322]{0:T(512)} %owner_ref.31, bf16[256,1280]{1,0:T(8,128)(2,1)} %multiply_convert_fusion.1.left_ref, bf16[256,5120]{1,0:T(8,128)(2,1)} %fusion.right_ref, bf16[512,64,1280]{2,1,0:T(8,128)(2,1)} %grad_5.1.refs_0_), custom_call_target="tpu_custom_call", output_to_operand_aliasing={{}: (3, {})} | custom-call | flops 3355443200 | bytes 13107200 | tf_op jit(solution)/shard_map/grad_4/pallas_call | solution.py:204
  650.1 6.1 grad_3.1.refs_0_
  656.3 11.0 grad_2.1.refs_0_
  667.3 6.3 grad_1.1.refs_0_
  674.8 3.2 grad_0.1
  678.0 386.1 %scatter_sum.1 = f32[16,64,1280]{2,1,0:T(8,128)} custom-call(bf16[4,2,4,16,64,1280]{5,4,3,2,1,0:T(8,128)(2,1)} %bitcast.30.slots_ref), custom_call_target="tpu_custom_call" | custom-call | tf_op jit(solution)/shard_map/scatter_sum/pallas_call | solution.py:499
  1064.4 4.6 multiply_reduce_fusion
  1069.0 38.7 %all-reduce.5 = (f32[2,3]{1,0:T(2,128)S(1)}, f32[]{:T(128)}, f32[11520]{0:T(1024)S(1)}) all-reduce(f32[2,3]{1,0:T(2,128)S(1)} %pad_maximum_fusion.7, f32[]{:T(128)} %multiply_reduce_fusion, f32[11520]{0:T(1024)S(1)} %copy-done.62), channel_id=1, replica_groups=mesh['wide'=8,'narrow'=4] {'wide','narrow'}, use_global_device_ids=true, to_apply=%region_11.12 | all-reduce | flops 11527 | bytes 92216 | tf_op jit(solution)/shard_map/psum | solution.py:1077
  1111.1 14.3 %fusion.51 = (bf16[16,64,1280]{2,1,0:T(8,128)(2,1)}, f32[16,64,1280]{2,1,0:T(8,128)}, f32[16,64,1280]{2,1,0:T(8,128)}, f32[16,64,1280]{2,1,0:T(8,128)}) fusion(f32[16,64,1280]{2,1,0:T(8,128)} %param.18, f32[]{:T(128)} %bitcast.32, f32[]{:T(128)S(6)} %min.3, f32[16,64,1280]{2,1,0:T(8,128)} %scatter_sum.1, pred[16]{0:T(512)(128)(4,1)S(1)} %compare_reduce_fusion, ...), kind=kLoop, calls=%fused_computation.161 | loop fusion | flops 22282240 | bytes 39321624 | tf_op jit(solution)/shard_map/convert_element_type | solution.py:1134
  (263 shorter events, 49.6 us)
Async XLA Ops:
  0.6 6.8 copy-start.78
  1.7 10.8 copy-start.59
  7.2 5.3 copy-start.26
  353.2 8.4 copy-start.10
  353.9 10.9 copy-start.53
  355.1 6.5 copy-start.21
  355.1 6.2 slice-start.1
  364.7 14.0 %copy-start.71 = (f32[256]{0:T(256)}, f32[256]{0:T(256)S(1)}, u32[]{:S(2)}) copy-start(f32[256]{0:T(256)S(1)} %get-tuple-element.82) | copy-start | bytes 3076
  366.0 12.8 %copy-start.33 = (bf16[256,1280]{1,0:T(8,128)(2,1)}, bf16[256,1280]{1,0:T(8,128)(2,1)S(1)}, u32[]{:S(2)}) copy-start(bf16[256,1280]{1,0:T(8,128)(2,1)S(1)} %multiply_convert_fusion.2.left_ref) | copy-start | bytes 1966084
  409.2 6.1 copy-start.24
  409.2 6.1 copy-start.3
  418.3 18.0 %copy-start.75 = (f32[256]{0:T(256)}, f32[256]{0:T(256)S(1)}, u32[]{:S(2)}) copy-start(f32[256]{0:T(256)S(1)} %get-tuple-element.86) | copy-start | bytes 3076
  420.5 15.8 %copy-start.30 = (bf16[256,1280]{1,0:T(8,128)(2,1)S(1)}, bf16[256,1280]{1,0:T(8,128)(2,1)}, u32[]{:S(2)}) copy-start(bf16[256,1280]{1,0:T(8,128)(2,1)} %multiply_convert_fusion.1.left_ref) | copy-start | bytes 1966084
  447.5 13.6 %copy-start.8 = (f32[256,1280]{1,0:T(8,128)S(1)}, f32[256,1280]{1,0:T(8,128)}, u32[]{:S(2)}) copy-start(f32[256,1280]{1,0:T(8,128)} %copy-done.7) | copy-start | bytes 3932164
  447.5 13.6 %copy-start.32 = (bf16[256,5120]{1,0:T(8,128)(2,1)S(1)}, bf16[256,5120]{1,0:T(8,128)(2,1)}, u32[]{:S(2)}) copy-start(bf16[256,5120]{1,0:T(8,128)(2,1)} %get-tuple-element.88.left_ref) | copy-start | bytes 7864324
  467.9 10.5 copy-start.37
  478.4 4.7 copy-start.68
  483.1 6.6 copy-start.41
  483.6 6.1 copy-start.31
  483.6 6.1 copy-start.77
  507.0 5.9 copy-start.50
  507.0 6.1 copy-start.60
  529.6 7.6 copy-start.29
  541.9 5.2 copy-start.19
  547.2 15.7 %copy-start.38 = (bf16[256,1280]{1,0:T(8,128)(2,1)}, bf16[256,1280]{1,0:T(8,128)(2,1)S(1)}, u32[]{:S(2)}) copy-start(bf16[256,1280]{1,0:T(8,128)(2,1)S(1)} %get-tuple-element.91.right_ref) | copy-start | bytes 1966084
  547.2 15.6 %copy-start.9 = (f32[256,1280]{1,0:T(8,128)S(1)}, f32[256,1280]{1,0:T(8,128)}, u32[]{:S(2)}) copy-start(f32[256,1280]{1,0:T(8,128)} %copy-done.7) | copy-start | bytes 3932164
  547.2 15.6 %copy-start.56 = (f32[1280]{0:T(1024)S(1)}, f32[1280]{0:T(1024)}, u32[]{:S(2)}) copy-start(f32[1280]{0:T(1024)} %get-tuple-element.69) | copy-start | bytes 15364
  547.2 15.6 %copy-start.74 = (f32[256]{0:T(256)S(1)}, f32[256]{0:T(256)}, u32[]{:S(2)}) copy-start(f32[256]{0:T(256)} %copy-done.73) | copy-start | bytes 3076
  562.8 8.3 copy-start.76
  573.6 4.7 copy-start.36
  573.6 4.7 copy-start.45
  573.6 4.7 copy-start.1
  590.7 5.4 copy-start.4
  590.8 5.4 copy-start.54
  590.8 5.4 copy-start.70
  596.2 7.4 copy-start.18
  596.2 7.4 copy-start.72
  596.2 7.4 copy-start.25
  609.1 6.3 copy-start.61
  609.1 6.3 copy-start.20
  609.1 6.3 copy-start.39
  667.3 6.3 copy-start.23
  667.3 6.3 copy-start.40
  678.0 386.1 %copy-start.43 = (s32[322]{0:T(512)S(1)}, s32[322]{0:T(512)}, u32[]{:S(2)}) copy-start(s32[322]{0:T(512)} %owner_ref.31) | copy-start | bytes 3868
  1064.3 46.0 %copy-start.47 = (f32[11520]{0:T(1024)S(1)}, f32[11520]{0:T(1024)}, u32[]{:S(2)}) copy-start(f32[11520]{0:T(1024)} %param.21) | copy-start | bytes 138244
  1064.3 46.0 %copy-start.63 = (f32[11520]{0:T(1024)S(1)}, f32[11520]{0:T(1024)}, u32[]{:S(2)}) copy-start(f32[11520]{0:T(1024)} %param.23) | copy-start | bytes 138244
  1064.4 46.0 %copy-start.64 = (f32[11520]{0:T(1024)S(1)}, f32[11520]{0:T(1024)}, u32[]{:S(2)}) copy-start(f32[11520]{0:T(1024)} %param.22) | copy-start | bytes 138244
  1111.1 14.3 %copy-start.84 = (f32[3]{0:T(128)S(1)}, f32[3]{0:T(128)}, u32[]{:S(2)}) copy-start(f32[3]{0:T(128)} %copy-done.83) | copy-start | bytes 40
  (39 other events, 79.3 us)

commit v5 on v4

--- a/solution.py
+++ b/solution.py
@@ -240,7 +240,12 @@
 
 def scatter_kernel(
     slots_ref,
+    small_ref,
+    filled_ref,
     out_ref,
+    small_out,
+    square_out,
+    small_in,
     own,
     pair_in,
     pair_sum,
@@ -265,6 +270,12 @@
     down_send,
     down_recv,
     result_sem,
+    share_send,
+    share_recv,
+    spread_send,
+    spread_recv,
+    square_send,
+    square_recv,
 ):
     wide, z = lax.axis_index("wide"), lax.axis_index("narrow")
     core, here = lax.rem(wide, 2), lax.div(wide, 2)
@@ -280,22 +291,50 @@
         along_y = lax.rem(k + which, 2)
         return (y + along_y - 2 * y * along_y) * 2 + (x + (1 - along_y) - 2 * x * (1 - along_y))
 
+    places = 8 * 4
+    me = wide * 4 + z
     barrier = pltpu.get_barrier_semaphore()
-    pl.semaphore_signal(barrier, inc=1, device_id=partner, device_id_type=MESH)
-    for which in range(2):
-        pl.semaphore_signal(
-            barrier, inc=1, device_id=device(near(0, which), z), device_id_type=MESH
-        )
-
-    @pl.when(z > 0)
-    def _():
-        pl.semaphore_signal(barrier, inc=1, device_id=device(here, z - 1), device_id_type=MESH)
-
-    @pl.when(z < 3)
-    def _():
-        pl.semaphore_signal(barrier, inc=1, device_id=device(here, z + 1), device_id_type=MESH)
-
-    pl.semaphore_wait(barrier, 3 + jnp.minimum(z, 1) + jnp.minimum(3 - z, 1))
+
+    def each(action):
+        def body(i, carry):
+            other = lax.rem(me + i, places)
+            action(i, other, (lax.div(other, 4), lax.rem(other, 4)))
+            return carry
+
+        lax.fori_loop(1, places, body, 0)
+
+    def greet(i, other, to):
+        pl.semaphore_signal(barrier, inc=1, device_id=to, device_id_type=MESH)
+
+    def share(i, other, to):
+        return pltpu.make_async_remote_copy(
+            src_ref=small_ref.at[other],
+            dst_ref=small_in.at[me],
+            send_sem=share_send.at[i],
+            recv_sem=share_recv.at[i],
+            device_id=to,
+            device_id_type=MESH,
+        )
+
+    def tell(ref, send, recv):
+        def make(i, other, to):
+            return pltpu.make_async_remote_copy(
+                src_ref=ref.at[me],
+                dst_ref=ref.at[me],
+                send_sem=send.at[i],
+                recv_sem=recv.at[i],
+                device_id=to,
+                device_id_type=MESH,
+            )
+
+        return make
+
+    spread = tell(small_out, spread_send, spread_recv)
+    square = tell(square_out, square_send, square_recv)
+    each(greet)
+    small_in[me] = small_ref[me]
+    square_out[me] = jnp.zeros((8, LANES), jnp.float32)
+    pl.semaphore_wait(barrier, places - 1)
 
     def own_copy(k):
         at = lax.rem(k, 2)
@@ -358,6 +397,7 @@
 
     own_copy(0).start()
     pair_copy(0).start()
+    each(lambda *at: share(*at).start())
 
     def step(t, carry):
         @pl.when(valid(t - 3))
@@ -479,29 +519,69 @@
             def _():
                 result[lax.rem(k, 2)] += down_in[lax.rem(k, 6), z].astype(jnp.float32)
 
+            kept = jnp.where(filled_ref[k, 0:1, 0:1] > 0.0, result[lax.rem(k, 2)], 0.0)
+            result[lax.rem(k, 2)] = kept
+            squares = square_out[me]
+            for i in range(BR // 8):
+                for j in range(D // LANES):
+                    part = kept[i * 8 : (i + 1) * 8, j * LANES : (j + 1) * LANES]
+                    squares = squares + part * part
+            square_out[me] = squares
             result_copy(k).start()
 
+        @pl.when(t == CHUNKS // 2)
+        def _():
+            each(lambda *at: share(*at).wait())
+            small = small_in[0]
+            for i in range(1, places):
+                small = small + small_in[i]
+            small_out[me] = small
+            each(lambda *at: spread(*at).start())
+
         return carry
 
     lax.fori_loop(0, STEPS, step, 0)
-
-
-def scatter_sum(slots, slot_count):
+    each(lambda *at: square(*at).start())
+    each(lambda *at: spread(*at).wait())
+    each(lambda *at: square(*at).wait())
+
+
+def scatter_sum(slots, filled, small):
+    slot_count = filled.shape[0]
     wide, narrow = lax.axis_size("wide"), lax.axis_size("narrow")
     if (wide, narrow, slot_count) != (8, 4, CHUNKS):
         part = lax.psum_scatter(slots, "wide", scatter_dimension=0, tiled=True)
-        return lax.psum_scatter(
+        owned = lax.psum_scatter(
             part.astype(jnp.float32), "narrow", scatter_dimension=0, tiled=True
         )
+        owned = jnp.where(filled[:, None, None], owned, 0.0)
+        square = lax.psum(jnp.sum(owned * owned), ("wide", "narrow"))
+        return owned, square, lax.psum(small, ("wide", "narrow"))
+    tiles = (wide * narrow, 8, LANES)
+    room = wide * narrow * 8 * LANES - small.shape[0]
+    assert room >= 0
     low = functools.partial(pltpu.VMEM, dtype=jnp.bfloat16)
     dma = pltpu.SemaphoreType.DMA
     block = (BR, D)
-    return pl.pallas_call(
+    owned, small_tiles, square_tiles = pl.pallas_call(
         scatter_kernel,
-        out_shape=jax.ShapeDtypeStruct((slot_count,) + block, jnp.float32),
-        in_specs=[pl.BlockSpec(memory_space=pl.ANY)],
-        out_specs=pl.BlockSpec(memory_space=pl.ANY),
+        out_shape=(
+            jax.ShapeDtypeStruct((slot_count,) + block, jnp.float32),
+            jax.ShapeDtypeStruct(tiles, jnp.float32),
+            jax.ShapeDtypeStruct(tiles, jnp.float32),
+        ),
+        in_specs=[
+            pl.BlockSpec(memory_space=pl.ANY),
+            pl.BlockSpec(memory_space=pltpu.VMEM),
+            pl.BlockSpec(memory_space=pltpu.VMEM),
+        ],
+        out_specs=(
+            pl.BlockSpec(memory_space=pl.ANY),
+            pl.BlockSpec(memory_space=pltpu.VMEM),
+            pl.BlockSpec(memory_space=pltpu.VMEM),
+        ),
         scratch_shapes=[
+            pltpu.VMEM(tiles, jnp.float32),
             low((2, 4, 4) + block),
             low((2, 4, 4) + block),
             low((3, 4, 4) + block),
@@ -526,12 +606,20 @@
             dma((2, 4)),
             dma((6, 4)),
             dma((2,)),
-        ],
+        ]
+        + [dma((wide * narrow,))] * 6,
         compiler_params=pltpu.CompilerParams(
             collective_id=1, has_side_effects=True, vmem_limit_bytes=VMEM_LIMIT
         ),
         name="scatter_sum",
-    )(slots.reshape(4, 2, narrow, slot_count, BR, D))
+    )(
+        slots.reshape(4, 2, narrow, slot_count, BR, D),
+        jnp.pad(small, (0, room)).reshape(tiles),
+        jnp.broadcast_to(
+            filled.astype(jnp.float32)[:, None, None], (slot_count, 8, LANES)
+        ),
+    )
+    return owned, jnp.sum(square_tiles), small_tiles.reshape(-1)[: small.shape[0]]
 
 
 LATE = 4
@@ -879,21 +967,37 @@
     context = (series[:, :CTX] * valid[:, :CTX]).reshape(count_series, NPATCH, PATCH)
     marks = pad_mask[:, :CTX].astype(jnp.float32).reshape(count_series, NPATCH, PATCH)
     feat = jnp.concatenate([context, marks], axis=-1)
-    index = (jnp.arange(NPATCH, dtype=jnp.int32)[:, None] + 1) * PATCH + jnp.arange(
-        HORIZON, dtype=jnp.int32
-    )[None, :]
-    return (feat, series[:, index], valid[:, index])
-
-
-def class_sums(out, target, tmask, onehot):
-    pred = out.reshape(onehot.shape[0], NPATCH, HORIZON, NQ + 1)
-    error = pred[..., 0] - target
-    square = jnp.sum(error * error * tmask, axis=(1, 2))
-    levels = (jnp.arange(NQ, dtype=jnp.float32) + 1.0) / (NQ + 1)
-    diff = target[..., None] - pred[..., 1:]
-    pinball = jnp.sum(jnp.maximum(levels * diff, (levels - 1.0) * diff), axis=-1)
-    quant = jnp.sum(pinball * tmask, axis=(1, 2))
-    return jnp.stack([jnp.sum(onehot * square[:, None], 0), jnp.sum(onehot * quant[:, None], 0)])
+    return (feat, horizons(series), horizons(valid))
+
+
+def horizons(points):
+    count_series = points.shape[0]
+    pieces = points.reshape(count_series, -1, PATCH)
+    return jnp.concatenate(
+        [pieces[:, 1 + j : 1 + j + NPATCH] for j in range(HORIZON // PATCH)], axis=-1
+    ).reshape(count_series * NPATCH, HORIZON)
+
+
+def loss_parts(out, target, tmask, onehot, class_weight):
+    column = lax.broadcasted_iota(jnp.int32, (HORIZON, OUTW), 1)
+    row = lax.broadcasted_iota(jnp.int32, (HORIZON, OUTW), 0)
+    spread = (lax.div(column, NQ + 1) == row).astype(jnp.float32)
+    wanted = jnp.dot(target, spread, precision=lax.Precision.HIGHEST)
+    mask = matmul(tmask.astype(jnp.bfloat16), spread.astype(jnp.bfloat16))
+    kind = lax.rem(lax.broadcasted_iota(jnp.int32, (1, OUTW), 1), NQ + 1)
+    level = kind.astype(jnp.float32) / (NQ + 1)
+    error = out - wanted
+    above, below = level * -error, (level - 1.0) * -error
+    slope = jnp.where(above > below, -level, jnp.where(above < below, 1.0 - level, 0.5 - level))
+    square = jnp.sum(jnp.where(kind == 0, error * error * mask, 0.0), axis=1)
+    quant = jnp.sum(jnp.where(kind == 0, 0.0, jnp.maximum(above, below) * mask), axis=1)
+    weight = jnp.repeat(jnp.sum(onehot * class_weight[None, :], axis=1), NPATCH)[:, None]
+    grad = weight * mask * jnp.where(kind == 0, 2.0 * error, slope / NQ)
+    sums = [
+        jnp.sum(onehot * jnp.sum(part.reshape(-1, NPATCH), axis=1)[:, None], 0)
+        for part in (square, quant)
+    ]
+    return jnp.stack(sums), grad.astype(jnp.bfloat16)
 
 
 def layer_forward(state_zero, mats, parts, cosine, sine, causal):
@@ -1050,7 +1154,9 @@
     onehot = (freq_class[:, None] == jnp.arange(NCLASS, dtype=jnp.int32)[None, :]).astype(
         jnp.float32
     )
-    local_counts = jnp.sum(onehot * jnp.sum(tmask, axis=(1, 2))[:, None], 0)
+    local_counts = jnp.sum(
+        onehot * jnp.sum(tmask.reshape(count_series, -1), axis=1)[:, None], 0
+    )
     gathered, counts = gather_all(master.astype(jnp.bfloat16), local_counts)
     mats = tuple(unpack(gathered, owner, which) for which in range(len(MATS)))
     tok_in, tok_out, head_in, head_out = (mats[0], mats[1], mats[6], mats[7])
@@ -1068,14 +1174,7 @@
     head_hidden = silu(head_pre[:, :D] + head_bias).astype(jnp.bfloat16)
     out = matmul(head_hidden, head_out) + out_bias + head_pre[:, D:]
 
-    def loss_of(value):
-        sums_here = class_sums(value, target, tmask, onehot)
-        return (jnp.sum((sums_here[0] + sums_here[1] / NQ) * class_weight), sums_here)
-
-    _, pull, local_sums = jax.vjp(loss_of, out, has_aux=True)
-    (grad_out,) = pull(jnp.ones((), jnp.float32))
-    sums = lax.psum(local_sums, ("wide", "narrow"))
-    grad_out = grad_out.astype(jnp.bfloat16)
+    local_sums, grad_out = loss_parts(out, target, tmask, onehot, class_weight)
     grad_out_bias = jnp.sum(grad_out.astype(jnp.float32), axis=0)
     slots = grad_blocks(head_hidden, grad_out, owner, 7, None)
     grad_head_first = backmul(grad_out, head_out) * silu_slope(head_pre[:, :D] + head_bias)
@@ -1108,16 +1207,15 @@
             grad_gain_two,
             grad_head_bias,
             grad_out_bias,
+            local_sums.reshape(-1),
         ]
     )
-    small_grad = lax.psum(small_local, ("wide", "narrow"))
-    owned = scatter_sum(slots, slot_count)
     rank = lax.axis_index("wide") * lax.axis_size("narrow") + lax.axis_index("narrow")
     mine = rank * slot_count + jnp.arange(slot_count, dtype=jnp.int32)
     filled = jnp.any(owner[:, None] == mine[None, :], axis=0)
-    owned = jnp.where(filled[:, None, None], owned, 0.0)
-    local_square = jnp.sum(owned * owned)
-    square_total = lax.psum(local_square, ("wide", "narrow"))
+    owned, square_total, small_total = scatter_sum(slots, filled, small_local)
+    small_grad = small_total[: small_master.shape[0]]
+    sums = small_total[small_master.shape[0] :].reshape(2, NCLASS)
     grad_norm = jnp.sqrt(square_total + jnp.sum(small_grad * small_grad))
     scale = jnp.minimum(1.0, CLIP / grad_norm)
     loss = jnp.sum((sums[0] + sums[1] / NQ) * class_weight)

time: 1140 us -> 1070 us (0.939)
  local copies, waits for them, and re-layouts: 82.9 us -> 39.1 us
  blocking collectives: 38.7 us -> 0 us
  Pallas kernels: 862 us -> 879 us
    psum x1 -> x0, blocking collectives: 38.7 us -> none  [on_device(): sums = lax.psum(local_sums, ('wide', 'narrow'))]
    pallas_call x1, Pallas kernels: 386 us -> 403 us  [scatter_sum(): pl.pallas_call(scatter_kernel, out_shape=(jax.ShapeDtypeStruct((slot_coun...]
    convert_element_type x4 -> x0, local copies, waits for them, and re-layouts: 13 us -> none  [the longest x3 12.9 us: on_device(): grad_out = grad_out.astype(jnp.bfloat16)]
    gather x4 -> x0, local copies, waits for them, and re-layouts: 11.5 us -> none  [prepare(): return (feat, series[:, index], valid[:, index])]
    dot_general x8 -> x9, matrix products: 41.6 us -> 43.3 us  [matmul(): return jnp.dot(left, right, preferred_element_type=jnp.float32)]
where the time goes in v5:
time: 1070 us; the launch traced here: 1060 us
  Pallas kernels  879 us (82%)
  matrix products  91.9 us (9%)
  other arithmetic  44.8 us (4%)
  local copies, waits for them, and re-layouts  39.1 us (4%)
    pallas_call x1, Pallas kernels, scatter_sum(): pl.pallas_call(scatter_kernel, out_shape=(jax.ShapeDtypeStruct((slot_coun...  403 us
    pallas_call x1, Pallas kernels, gather_all(): pl.pallas_call(gather_kernel, out_shape=(jax.ShapeDtypeStruct((4, 2, narr...  336 us
    pallas_call x8, Pallas kernels, unpack(): pl.pallas_call(functools.partial(unpack_kernel, groups, count), out_shape...  73.7 us
    pallas_call x8, Pallas kernels, grad_blocks(): pl.pallas_call(functools.partial(grad_kernel, groups, count, BASES[which]...  66.7 us
    dot_general x9, matrix products, matmul(): return jnp.dot(left, right, preferred_element_type=jnp.float32)  43.3 us
    dot_general x7, matrix products, backmul(): lax.dot_general(left, right, (((1,), (1,)), ((), ())), preferred_element_...  41.2 us

profile of v5, /device:TPU:0, one launch (start us, length us, event | category | flops | bytes accessed | tf_op | source)
XLA Modules:
  0.0 1060.8 jit_solution(179299465761983969)
XLA Ops:
  3.2 4.3 convert_element_type.144.own_ref
  7.5 336.2 %gather_all.1 = (bf16[4,2,4,16,64,1280]{5,4,3,2,1,0:T(8,128)(2,1)}, f32[32,8,128]{2,1,0:T(8,128)}) custom-call(bf16[16,64,1280]{2,1,0:T(8,128)(2,1)} %convert_element_type.144.own_ref, f32[8,128]{1,0:T(8,128)} %scatter.4.count_ref), custom_call_target="tpu_custom_call" | custom-call | tf_op jit(solution)/shard_map/gather_all/pallas_call | solution.py:912
  343.7 2.6 unpack_0.1
  346.7 1.5 fusion.67
  350.1 6.2 unpack_1.1
  356.6 3.1 multiply_reduce_fusion.6
  361.0 12.8 %unpack_2.1 = bf16[1280,3840]{1,0:T(8,128)(2,1)} custom-call(s32[322]{0:T(512)} %owner_ref.31, bf16[512,64,1280]{2,1,0:T(8,128)(2,1)} %bitcast.2.refs_0_.refs_1_.refs_2_.refs_3_.refs_4_.refs_5_.refs_6_.refs_7_, bf16[512,64,1280]{2,1,0:T(8,128)(2,1)} %bitcast.2.refs_0_.refs_1_.refs_2_.refs_3_.refs_4_.refs_5_.refs_6_.refs_7_, ...), custom_call_target="tpu_custom_call" | custom-call | bytes 19660800 | tf_op jit(solution)/shard_map/unpack_2/pallas_call | solution.py:125
  373.8 8.4 fusion.68
  382.2 8.0 reshape.325
  390.2 2.6 fusion.60
  392.9 1.7 copy_bitcast_fusion
  399.7 1.8 slice.207
  404.1 6.1 unpack_3.1
  410.2 3.0 multiply_reduce_fusion.5
  415.4 15.8 %unpack_4.1 = bf16[1280,5120]{1,0:T(8,128)(2,1)} custom-call(s32[322]{0:T(512)} %owner_ref.31, bf16[512,64,1280]{2,1,0:T(8,128)(2,1)} %bitcast.2.refs_0_.refs_1_.refs_2_.refs_3_.refs_4_.refs_5_.refs_6_.refs_7_, bf16[512,64,1280]{2,1,0:T(8,128)(2,1)} %bitcast.2.refs_0_.refs_1_.refs_2_.refs_3_.refs_4_.refs_5_.refs_6_.refs_7_, ...), custom_call_target="tpu_custom_call" | custom-call | bytes 26214400 | tf_op jit(solution)/shard_map/unpack_4/pallas_call | solution.py:125
  431.2 11.2 %divide_convert_fusion = (bf16[256,5120]{1,0:T(8,128)(2,1)}, f32[256,5120]{1,0:T(8,128)}) fusion(bf16[256,1280]{1,0:T(8,128)(2,1)S(1)} %copy-done.31, bf16[1280,5120]{1,0:T(8,128)(2,1)} %unpack_4.1), kind=kOutput, calls=%fused_computation.6 | convolution fusion | flops 3360686080 | bytes 21626880 | tf_op jit(solution)/shard_map/dot_general | solution.py:35
  442.4 13.6 %unpack_5.1 = bf16[5120,1280]{1,0:T(8,128)(2,1)} custom-call(s32[322]{0:T(512)} %owner_ref.31, bf16[512,64,1280]{2,1,0:T(8,128)(2,1)} %bitcast.2.refs_0_.refs_1_.refs_2_.refs_3_.refs_4_.refs_5_.refs_6_.refs_7_, bf16[512,64,1280]{2,1,0:T(8,128)(2,1)} %bitcast.2.refs_0_.refs_1_.refs_2_.refs_3_.refs_4_.refs_5_.refs_6_.refs_7_, ...), custom_call_target="tpu_custom_call" | custom-call | bytes 26214400 | tf_op jit(solution)/shard_map/unpack_5/pallas_call | solution.py:125
  456.0 6.8 fusion.5.left_ref
  462.8 10.5 unpack_6.1
  473.3 4.7 fusion.69
  478.5 6.1 unpack_7.1
  484.6 3.0 fusion.3
  488.9 1.7 select_reduce_fusion.2
  492.6 2.5 convert_reduce_fusion
  495.3 2.7 fusion.61
  498.0 3.0 fusion.66
  501.0 15.9 %fusion.right_ref = bf16[256,5120]{1,0:T(8,128)(2,1)} fusion(bf16[256,1280]{1,0:T(8,128)(2,1)S(1)} %get-tuple-element.102.right_ref, bf16[5120,1280]{1,0:T(8,128)(2,1)} %unpack_5.1, f32[256,5120]{1,0:T(8,128)} %get-tuple-element.99), kind=kOutput, calls=%fused_computation.3 | convolution fusion | flops 3367239680 | bytes 21626880 | tf_op jit(solution)/shard_map/dot_general | solution.py:45
  516.9 8.4 multiply_reduce_fusion.1
  525.3 1.4 fusion.58
  527.7 1.9 convolution_convert_fusion
  529.6 2.8 reshape.329
  532.5 2.3 multiply_reduce_fusion
  542.4 2.5 copy.53
  544.9 5.4 convert_element_type.167.right_ref
  550.3 7.4 multiply_reduce_fusion.2
  560.5 2.0 fusion.62
  563.7 6.3 grad_7.1.refs_0_
  571.2 9.7 grad_6.1.refs_0_
  580.9 11.3 %grad_5.1.refs_0_ = bf16[512,64,1280]{2,1,0:T(8,128)(2,1)} custom-call(s32[322]{0:T(512)} %owner_ref.31, bf16[256,5120]{1,0:T(8,128)(2,1)} %get-tuple-element.98.left_ref, bf16[256,1280]{1,0:T(8,128)(2,1)} %copy-done.40, bf16[512,64,1280]{2,1,0:T(8,128)(2,1)} %grad_6.1.refs_0_), custom_call_target="tpu_custom_call", output_to_operand_aliasing={{}: (3, {})} | custom-call | flops 3355443200 | bytes 13107200 | tf_op jit(solution)/shard_map/grad_5/pallas_call | solution.py:204
  592.2 12.6 %grad_4.1.refs_0_ = bf16[512,64,1280]{2,1,0:T(8,128)(2,1)} custom-call(s32[322]{0:T(512)} %owner_ref.31, bf16[256,1280]{1,0:T(8,128)(2,1)} %multiply_convert_fusion.2.left_ref, bf16[256,5120]{1,0:T(8,128)(2,1)} %fusion.right_ref, bf16[512,64,1280]{2,1,0:T(8,128)(2,1)} %grad_5.1.refs_0_), custom_call_target="tpu_custom_call", output_to_operand_aliasing={{}: (3, {})} | custom-call | flops 3355443200 | bytes 13107200 | tf_op jit(solution)/shard_map/grad_4/pallas_call | solution.py:204
  604.8 6.1 grad_3.1.refs_0_
  611.0 11.1 %grad_2.1.refs_0_ = bf16[512,64,1280]{2,1,0:T(8,128)(2,1)} custom-call(s32[322]{0:T(512)} %owner_ref.31, bf16[256,1280]{1,0:T(8,128)(2,1)} %copy-done.34, bf16[256,3840]{1,0:T(8,128)(2,1)} %copy-done.18, bf16[512,64,1280]{2,1,0:T(8,128)(2,1)} %grad_3.1.refs_0_), custom_call_target="tpu_custom_call", output_to_operand_aliasing={{}: (3, {})} | custom-call | flops 2516582400 | bytes 9830400 | tf_op jit(solution)/shard_map/grad_2/pallas_call | solution.py:204
  622.0 6.3 grad_1.1.refs_0_
  629.5 3.4 grad_0.1
  633.8 402.6 %scatter_sum.1 = (f32[16,64,1280]{2,1,0:T(8,128)}, f32[32,8,128]{2,1,0:T(8,128)}, f32[32,8,128]{2,1,0:T(8,128)}) custom-call(bf16[4,2,4,16,64,1280]{5,4,3,2,1,0:T(8,128)(2,1)} %bitcast.16.slots_ref, f32[32,8,128]{2,1,0:T(8,128)} %pad_bitcast_fusion.small_ref, f32[16,8,128]{2,1,0:T(8,128)} %broadcast_in_dim.138.filled_ref), custom_call_target="tpu_custom_call" | custom-call | tf_op jit(solution)/shard_map/scatter_sum/pallas_call | solution.py:566
  1037.9 1.5 reduce_sum.324
  1041.5 1.5 multiply_subtract_fusion.2
  1043.0 14.8 %fusion.54 = (bf16[16,64,1280]{2,1,0:T(8,128)(2,1)}, f32[16,64,1280]{2,1,0:T(8,128)}, f32[16,64,1280]{2,1,0:T(8,128)}, f32[16,64,1280]{2,1,0:T(8,128)}) fusion(f32[16,64,1280]{2,1,0:T(8,128)} %param.18, f32[]{:T(128)} %bitcast.22, f32[16,64,1280]{2,1,0:T(8,128)} %get-tuple-element.30, f32[]{:T(128)S(6)} %min.3, f32[16,64,1280]{2,1,0:T(8,128)} %param.20, ...), kind=kLoop, calls=%fused_computation.167 | loop fusion | flops 20971520 | bytes 39321608 | tf_op jit(solution)/shard_map/convert_element_type | solution.py:1232
  (256 shorter events, 38.3 us)
Async XLA Ops:
  1.5 5.9 copy-start.27
  348.2 8.4 copy-start.10
  348.9 10.9 %copy-start.56 = (f32[1280]{0:T(1024)}, f32[1280]{0:T(1024)S(1)}, u32[]{:S(2)}) copy-start(f32[1280]{0:T(1024)S(1)} %get-tuple-element.82) | copy-start | bytes 15364
  350.0 6.6 copy-start.21
  350.0 6.2 slice-start.2
  350.1 6.2 copy-start.77
  359.7 14.1 %copy-start.70 = (f32[256]{0:T(256)}, f32[256]{0:T(256)S(1)}, u32[]{:S(2)}) copy-start(f32[256]{0:T(256)S(1)} %get-tuple-element.92) | copy-start | bytes 3076
  361.0 12.8 %copy-start.34 = (bf16[256,1280]{1,0:T(8,128)(2,1)}, bf16[256,1280]{1,0:T(8,128)(2,1)S(1)}, u32[]{:S(2)}) copy-start(bf16[256,1280]{1,0:T(8,128)(2,1)S(1)} %multiply_convert_fusion.3.left_ref) | copy-start | bytes 1966084
  397.9 3.7 copy-start.54
  404.1 6.2 copy-start.24
  404.1 6.1 copy-start.3
  410.2 4.2 copy-start.58
  413.3 18.0 %copy-start.74 = (f32[256]{0:T(256)}, f32[256]{0:T(256)S(1)}, u32[]{:S(2)}) copy-start(f32[256]{0:T(256)S(1)} %get-tuple-element.96) | copy-start | bytes 3076
  415.4 15.8 %copy-start.31 = (bf16[256,1280]{1,0:T(8,128)(2,1)S(1)}, bf16[256,1280]{1,0:T(8,128)(2,1)}, u32[]{:S(2)}) copy-start(bf16[256,1280]{1,0:T(8,128)(2,1)} %multiply_convert_fusion.2.left_ref) | copy-start | bytes 1966084
  442.4 13.6 %copy-start.8 = (f32[256,1280]{1,0:T(8,128)S(1)}, f32[256,1280]{1,0:T(8,128)}, u32[]{:S(2)}) copy-start(f32[256,1280]{1,0:T(8,128)} %copy-done.7) | copy-start | bytes 3932164
  442.4 13.6 %copy-start.33 = (bf16[256,5120]{1,0:T(8,128)(2,1)S(1)}, bf16[256,5120]{1,0:T(8,128)(2,1)}, u32[]{:S(2)}) copy-start(bf16[256,5120]{1,0:T(8,128)(2,1)} %get-tuple-element.98.left_ref) | copy-start | bytes 7864324
  462.8 10.5 copy-start.39
  473.3 4.7 copy-start.67
  478.0 6.5 copy-start.44
  478.4 6.1 copy-start.32
  478.5 6.1 copy-start.76
  488.8 3.1 copy-start.78
  488.9 9.1 slice-start
  497.9 3.0 copy-start.41
  501.0 15.9 %copy-start.40 = (bf16[256,1280]{1,0:T(8,128)(2,1)}, bf16[256,1280]{1,0:T(8,128)(2,1)S(1)}, u32[]{:S(2)}) copy-start(bf16[256,1280]{1,0:T(8,128)(2,1)S(1)} %get-tuple-element.102.right_ref) | copy-start | bytes 1966084
  501.0 15.9 %copy-start.9 = (f32[256,1280]{1,0:T(8,128)S(1)}, f32[256,1280]{1,0:T(8,128)}, u32[]{:S(2)}) copy-start(f32[256,1280]{1,0:T(8,128)} %copy-done.7) | copy-start | bytes 3932164
  501.0 15.9 %copy-start.59 = (f32[1280]{0:T(1024)S(1)}, f32[1280]{0:T(1024)}, u32[]{:S(2)}) copy-start(f32[1280]{0:T(1024)} %get-tuple-element.81) | copy-start | bytes 15364
  501.0 15.9 %copy-start.73 = (f32[256]{0:T(256)S(1)}, f32[256]{0:T(256)}, u32[]{:S(2)}) copy-start(f32[256]{0:T(256)} %copy-done.72) | copy-start | bytes 3076
  516.8 8.4 copy-start.75
  516.9 8.5 copy-start.36
  527.7 4.7 copy-start.38
  527.7 4.7 copy-start.48
  527.7 4.7 copy-start.1
  544.9 5.4 copy-start.4
  544.9 5.4 copy-start.57
  544.9 5.4 copy-start.69
  550.3 7.4 copy-start.18
  550.3 7.4 copy-start.71
  550.3 7.4 copy-start.26
  563.7 6.3 copy-start.20
  563.7 6.3 copy-start.42
  622.0 6.3 copy-start.23
  622.0 6.3 copy-start.43
  629.5 3.4 copy-start.46
  633.8 407.7 %copy-start.50 = (f32[11520]{0:T(1024)S(1)}, f32[11520]{0:T(1024)}, u32[]{:S(2)}) copy-start(f32[11520]{0:T(1024)} %param.21) | copy-start | bytes 138244
  633.8 407.7 %copy-start.62 = (f32[11520]{0:T(1024)S(1)}, f32[11520]{0:T(1024)}, u32[]{:S(2)}) copy-start(f32[11520]{0:T(1024)} %param.23) | copy-start | bytes 138244
  633.8 407.7 %copy-start.63 = (f32[11520]{0:T(1024)S(1)}, f32[11520]{0:T(1024)}, u32[]{:S(2)}) copy-start(f32[11520]{0:T(1024)} %param.22) | copy-start | bytes 138244
  1043.0 14.8 %copy-start.80 = (f32[3]{0:T(128)S(1)}, f32[3]{0:T(128)}, u32[]{:S(2)}) copy-start(f32[3]{0:T(128)} %copy-done.79) | copy-start | bytes 40
  (36 other events, 64.7 us)

commit v6 on v5

--- a/solution.py
+++ b/solution.py
@@ -83,7 +83,7 @@
     (D, 1, 4),
     (D, FF // D, 8),
     (FF, 1, 8),
-    (D, (D + OUTW) // D, 4),
+    (D, (D + OUTW) // D, 8),
     (D, 1, 4),
 )
 BASES = tuple(sum(r * g for r, g, _ in MATS[:i]) // BR for i in range(len(MATS)))
@@ -91,139 +91,207 @@
 VMEM_LIMIT = 56 * 1024 * 1024
 
 
-def unpack_kernel(groups, count, owner_ref, *refs):
-    out_ref = refs[count]
-    if groups == 1:
-        for b in range(count):
-            out_ref[b * BR : (b + 1) * BR, :] = refs[b][...]
-        return
-    wide_ref = refs[count + 1]
-    for b in range(count):
-        for c in range(D // LANES):
-            wide_ref[c, b * BR : (b + 1) * BR, :] = refs[b][
-                :, c * LANES : (c + 1) * LANES
-            ].astype(jnp.float32)
-    rows = count * BR // groups
-    for j in range(groups):
-        for c in range(D // LANES):
-            at = j * D + c * LANES
-            out_ref[:, at : at + LANES] = wide_ref[c, pl.ds(j, rows, stride=groups), :].astype(
-                jnp.bfloat16
-            )
-
-
-def unpack(gathered, owner, which):
+RING = 48
+
+
+def steps_of(which):
     total, groups, count = MATS[which]
-    base = BASES[which]
-    rows = count * BR // groups
-
-    def spec(b):
-        return pl.BlockSpec(
-            (None, BR, D), lambda i, own, b=b: (own[base + i * count + b], 0, 0)
-        )
-
+    return total * groups // (count * BR)
+
+
+def stages(kind):
+    return [pltpu.VMEM((2,) + kind(*MATS[which]), jnp.bfloat16) for which in range(len(MATS))]
+
+
+def unpack_kernel(owner_ref, gathered_ref, *refs):
+    outs, held = refs[:8], refs[8:16]
+    ring, wide_ref, load_sem, store_sem = refs[16:]
+
+    def load(b):
+        at = lax.rem(b, RING)
+        return pltpu.make_async_copy(
+            gathered_ref.at[owner_ref[b]], ring.at[at], load_sem.at[at]
+        )
+
+    def first_load(b, carry):
+        load(b).start()
+        return carry
+
+    lax.fori_loop(0, RING, first_load, 0)
+
+    def store(which, i):
+        total, groups, count = MATS[which]
+        rows = count * BR // groups
+        at = lax.rem(i, 2)
+        return pltpu.make_async_copy(
+            held[which].at[at],
+            outs[which].at[pl.ds(pl.multiple_of(i * rows, rows), rows)],
+            store_sem.at[which, at],
+        )
+
+    for which, (total, groups, count) in enumerate(MATS):
+        rows = count * BR // groups
+
+        def step(i, carry, which=which, groups=groups, count=count, rows=rows):
+            first = BASES[which] + i * count
+            at = lax.rem(i, 2)
+
+            @pl.when(i >= 2)
+            def _():
+                store(which, i - 2).wait()
+
+            for b in range(count):
+                load(first + b).wait()
+            for b in range(count):
+                block = ring.at[lax.rem(first + b, RING)]
+                span = slice(b * BR, (b + 1) * BR)
+                if groups == 1:
+                    held[which][at, span, :] = block[...]
+                    continue
+                for c in range(D // LANES):
+                    wide_ref[c, span, :] = block[:, c * LANES : (c + 1) * LANES].astype(
+                        jnp.float32
+                    )
+            if groups > 1:
+                for j in range(groups):
+                    for c in range(D // LANES):
+                        left = j * D + c * LANES
+                        held[which][at, :, left : left + LANES] = wide_ref[
+                            c, pl.ds(j, rows, stride=groups), :
+                        ].astype(jnp.bfloat16)
+            store(which, i).start()
+            for b in range(count):
+
+                @pl.when(first + b + RING < NBLK)
+                def _(b=b):
+                    load(first + b + RING).start()
+
+            return carry
+
+        lax.fori_loop(0, steps_of(which), step, 0)
+
+    for which in range(len(MATS)):
+        for i in range(max(steps_of(which) - 2, 0), steps_of(which)):
+            store(which, i).wait()
+
+
+def unpack(gathered, owner):
+    dma = pltpu.SemaphoreType.DMA
     return pl.pallas_call(
-        functools.partial(unpack_kernel, groups, count),
-        out_shape=jax.ShapeDtypeStruct((total, groups * D), jnp.bfloat16),
-        grid_spec=pltpu.PrefetchScalarGridSpec(
-            num_scalar_prefetch=1,
-            grid=(total // rows,),
-            in_specs=[spec(b) for b in range(count)],
-            out_specs=pl.BlockSpec((rows, groups * D), lambda i, own: (i, 0)),
-            scratch_shapes=[]
-            if groups == 1
-            else [pltpu.VMEM((D // LANES, count * BR, LANES), jnp.float32)],
+        unpack_kernel,
+        out_shape=tuple(
+            jax.ShapeDtypeStruct((total, groups * D), jnp.bfloat16) for total, groups, _ in MATS
         ),
+        in_specs=[
+            pl.BlockSpec(memory_space=pltpu.SMEM),
+            pl.BlockSpec(memory_space=pl.ANY),
+        ],
+        out_specs=tuple(pl.BlockSpec(memory_space=pl.ANY) for _ in MATS),
+        scratch_shapes=stages(lambda total, groups, count: (count * BR // groups, groups * D))
+        + [
+            pltpu.VMEM((RING, BR, D), jnp.bfloat16),
+            pltpu.VMEM((D // LANES, 8 * BR, LANES), jnp.float32),
+            dma((RING,)),
+            dma((len(MATS), 2)),
+        ],
         compiler_params=pltpu.CompilerParams(vmem_limit_bytes=VMEM_LIMIT),
         cost_estimate=pl.CostEstimate(
-            flops=0, bytes_accessed=4 * total * groups * D, transcendentals=0
+            flops=0, bytes_accessed=4 * ROWS * D, transcendentals=0
         ),
-        name=f"unpack_{which}",
-    )(owner, *([gathered] * count))
-
-
-def grad_kernel(groups, count, base, steps, owner_ref, left_ref, right_ref, *refs):
-    out_ref, stage_ref, sems = refs[-3 - (groups > 1)], refs[-2 - (groups > 1)], refs[-1 - (groups > 1)]
-    step = pl.program_id(0)
-    slot = lax.rem(step, 2)
-    rows = count * BR // groups
-
-    def copy(at, b, when):
+        name="unpack",
+    )(owner, gathered)
+
+
+def grad_kernel(owner_ref, *refs):
+    lefts, rights, out_ref = refs[:8], refs[8:16], refs[16]
+    left_in, right_in, held = refs[17:25], refs[25:33], refs[33:41]
+    wide_ref, load_sem, store_sem = refs[41:]
+
+    def loads(which):
+        return (
+            pltpu.make_async_copy(lefts[which], left_in[which], load_sem.at[which, 0]),
+            pltpu.make_async_copy(rights[which], right_in[which], load_sem.at[which, 1]),
+        )
+
+    def store(which, i, b):
+        at = lax.rem(i, 2)
         return pltpu.make_async_copy(
-            stage_ref.at[at, pl.ds(b * BR, BR), :],
-            out_ref.at[owner_ref[base + when * count + b]],
-            sems.at[at, b],
-        )
-
-    @pl.when(step >= 2)
-    def _():
-        for b in range(count):
-            copy(slot, b, step - 2).wait()
-
-    left = left_ref[...]
-    for j in range(groups):
-        part = tmatmul(left, right_ref[:, j * D : (j + 1) * D])
-        if groups == 1:
-            stage_ref[slot] = part.astype(jnp.bfloat16)
-        else:
-            for c in range(D // LANES):
-                refs[-1][c, pl.ds(j, rows, stride=groups), :] = part[
-                    :, c * LANES : (c + 1) * LANES
-                ]
-    if groups > 1:
-        for c in range(D // LANES):
-            stage_ref[slot, :, c * LANES : (c + 1) * LANES] = refs[-1][c].astype(jnp.bfloat16)
-    for b in range(count):
-        copy(slot, b, step).start()
-
-    @pl.when(step == steps - 1)
-    def _():
-        for b in range(count):
-            copy(slot, b, step).wait()
-
-    if steps > 1:
-
-        @pl.when(step == steps - 1)
-        def _():
+            held[which].at[at, pl.ds(b * BR, BR), :],
+            out_ref.at[owner_ref[BASES[which] + i * MATS[which][2] + b]],
+            store_sem.at[which, at, b],
+        )
+
+    order = tuple(reversed(range(len(MATS))))
+    for which in order:
+        for copy in loads(which):
+            copy.start()
+    for which in order:
+        total, groups, count = MATS[which]
+        rows = count * BR // groups
+        for copy in loads(which):
+            copy.wait()
+
+        def step(i, carry, which=which, groups=groups, count=count, rows=rows):
+            at = lax.rem(i, 2)
+
+            @pl.when(i >= 2)
+            def _():
+                for b in range(count):
+                    store(which, i - 2, b).wait()
+
+            if steps_of(which) == 1:
+                left = left_in[which][...]
+            else:
+                left = left_in[which][:, pl.ds(pl.multiple_of(i * rows, rows), rows)]
+            for j in range(groups):
+                part = tmatmul(left, right_in[which][:, j * D : (j + 1) * D])
+                if groups == 1:
+                    held[which][at] = part.astype(jnp.bfloat16)
+                    continue
+                for c in range(D // LANES):
+                    wide_ref[c, pl.ds(j, rows, stride=groups), :] = part[
+                        :, c * LANES : (c + 1) * LANES
+                    ]
+            if groups > 1:
+                for c in range(D // LANES):
+                    held[which][at, :, c * LANES : (c + 1) * LANES] = wide_ref[
+                        c, 0 : count * BR, :
+                    ].astype(jnp.bfloat16)
             for b in range(count):
-                copy(1 - slot, b, step - 1).wait()
-
-
-def grad_blocks(left, right, owner, which, slots):
-    total, groups, count = MATS[which]
-    rows = count * BR // groups
-    steps = total // rows
-    tokens = left.shape[0]
-    scratch = [
-        pltpu.VMEM((2, count * BR, D), jnp.bfloat16),
-        pltpu.SemaphoreType.DMA((2, count)),
-    ]
-    if groups > 1:
-        scratch.append(pltpu.VMEM((D // LANES, count * BR, LANES), jnp.float32))
-    held = [] if slots is None else [slots]
+                store(which, i, b).start()
+            return carry
+
+        lax.fori_loop(0, steps_of(which), step, 0)
+    for which in order:
+        for i in range(max(steps_of(which) - 2, 0), steps_of(which)):
+            for b in range(MATS[which][2]):
+                store(which, i, b).wait()
+
+
+def grad_blocks(pairs, owner):
+    lefts, rights = zip(*pairs)
+    dma = pltpu.SemaphoreType.DMA
+    tokens = lefts[0].shape[0]
     return pl.pallas_call(
-        functools.partial(grad_kernel, groups, count, BASES[which], steps),
+        grad_kernel,
         out_shape=jax.ShapeDtypeStruct((TOTAL_SLOTS, BR, D), jnp.bfloat16),
-        grid_spec=pltpu.PrefetchScalarGridSpec(
-            num_scalar_prefetch=1,
-            grid=(steps,),
-            in_specs=[
-                pl.BlockSpec((tokens, rows), lambda i, own: (0, i)),
-                pl.BlockSpec((tokens, groups * D), lambda i, own: (0, 0)),
-            ]
-            + [pl.BlockSpec(memory_space=pl.ANY)] * len(held),
-            out_specs=pl.BlockSpec(memory_space=pl.ANY),
-            scratch_shapes=scratch,
-        ),
-        input_output_aliases={3: 0} if held else {},
+        in_specs=[pl.BlockSpec(memory_space=pltpu.SMEM)]
+        + [pl.BlockSpec(memory_space=pl.ANY)] * (2 * len(MATS)),
+        out_specs=pl.BlockSpec(memory_space=pl.ANY),
+        scratch_shapes=[pltpu.VMEM(left.shape, jnp.bfloat16) for left in lefts]
+        + [pltpu.VMEM(right.shape, jnp.bfloat16) for right in rights]
+        + stages(lambda total, groups, count: (count * BR, D))
+        + [
+            pltpu.VMEM((D // LANES, 8 * BR, LANES), jnp.float32),
+            dma((len(MATS), 2)),
+            dma((len(MATS), 2, 8)),
+        ],
         compiler_params=pltpu.CompilerParams(vmem_limit_bytes=VMEM_LIMIT),
         cost_estimate=pl.CostEstimate(
-            flops=2 * tokens * total * groups * D,
-            bytes_accessed=2 * total * groups * D,
-            transcendentals=0,
+            flops=2 * tokens * ROWS * D, bytes_accessed=2 * ROWS * D, transcendentals=0
         ),
-        name=f"grad_{which}",
-    )(owner, left, right, *held)
+        name="grad_blocks",
+    )(owner, *lefts, *rights)
 
 
 CHUNKS = 16
@@ -1040,9 +1108,7 @@
     )
 
 
-def layer_backward(
-    grad_two, state_zero, kept, mats, parts, cosine, sine, causal, owner, slots
-):
+def layer_backward(grad_two, state_zero, kept, mats, parts, cosine, sine, causal):
     (
         normed_one,
         queries,
@@ -1060,16 +1126,13 @@
     tokens = state_zero.shape[0]
     count_series = tokens // NPATCH
     grad_mlp = grad_two.astype(jnp.bfloat16)
-    slots = grad_blocks(activ, grad_mlp, owner, 5, slots)
     grad_act = backmul(grad_mlp, w_down)
     grad_up_pre = (grad_act * silu_slope(up_pre)).astype(jnp.bfloat16)
-    slots = grad_blocks(normed_two, grad_up_pre, owner, 4, slots)
     grad_normed = backmul(grad_up_pre, w_up)
     _, pull = jax.vjp(rms_norm, state_one, gain_two)
     grad_norm_in, grad_gain_two = pull(grad_normed)
     grad_one = grad_two + grad_norm_in
     grad_proj = grad_one.astype(jnp.bfloat16)
-    slots = grad_blocks(mixed, grad_proj, owner, 3, slots)
     grad_mixed = (
         backmul(grad_proj, w_out).astype(jnp.bfloat16).reshape(count_series, NPATCH, HEADS, HDIM)
     )
@@ -1102,13 +1165,17 @@
         axis=2,
     )
     grad_qkv = grad_qkv.reshape(tokens, 3 * D).astype(jnp.bfloat16)
-    slots = grad_blocks(normed_one, grad_qkv, owner, 2, slots)
     grad_normed_one = backmul(grad_qkv, w_qkv)
     _, pull = jax.vjp(rms_norm, state_zero, gain_one)
     grad_zero_in, grad_gain_one = pull(grad_normed_one)
     return (
         grad_one + grad_zero_in,
-        slots,
+        (
+            (normed_one, grad_qkv),
+            (mixed, grad_proj),
+            (normed_two, grad_up_pre),
+            (activ, grad_mlp),
+        ),
         grad_gain_one,
         grad_gain_two,
     )
@@ -1158,7 +1225,7 @@
         onehot * jnp.sum(tmask.reshape(count_series, -1), axis=1)[:, None], 0
     )
     gathered, counts = gather_all(master.astype(jnp.bfloat16), local_counts)
-    mats = tuple(unpack(gathered, owner, which) for which in range(len(MATS)))
+    mats = unpack(gathered, owner)
     tok_in, tok_out, head_in, head_out = (mats[0], mats[1], mats[6], mats[7])
     class_weight = 1.0 / (counts * NCLASS)
     cosine, sine = tables()
@@ -1176,23 +1243,25 @@
 
     local_sums, grad_out = loss_parts(out, target, tmask, onehot, class_weight)
     grad_out_bias = jnp.sum(grad_out.astype(jnp.float32), axis=0)
-    slots = grad_blocks(head_hidden, grad_out, owner, 7, None)
     grad_head_first = backmul(grad_out, head_out) * silu_slope(head_pre[:, :D] + head_bias)
     grad_head_bias = jnp.sum(grad_head_first, axis=0)
     grad_head_pre = jnp.concatenate([grad_head_first, grad_out.astype(jnp.float32)], axis=1).astype(
         jnp.bfloat16
     )
-    slots = grad_blocks(state_low, grad_head_pre, owner, 6, slots)
     grad_two = backmul(grad_head_pre, head_in)
     _, kept = layer_forward(state_zero, mats, parts, cosine, sine, causal)
-    grad_zero, slots, grad_gain_one, grad_gain_two = layer_backward(
-        grad_two, state_zero, kept, mats, parts, cosine, sine, causal, owner, slots
+    grad_zero, layer_pairs, grad_gain_one, grad_gain_two = layer_backward(
+        grad_two, state_zero, kept, mats, parts, cosine, sine, causal
     )
     grad_prod = grad_zero.astype(jnp.bfloat16)
-    slots = grad_blocks(hidden, grad_prod, owner, 1, slots)
     grad_first = backmul(grad_prod, tok_out) * silu_slope(tok_pre[:, :D] + bias_one)
     grad_tok_pre = jnp.concatenate([grad_first, grad_zero], axis=1).astype(jnp.bfloat16)
-    slots = grad_blocks(patch_in, grad_tok_pre, owner, 0, slots)
+    slots = grad_blocks(
+        ((patch_in, grad_tok_pre), (hidden, grad_prod))
+        + layer_pairs
+        + ((state_low, grad_head_pre), (head_hidden, grad_out)),
+        owner,
+    )
     grad_freq = jnp.dot(
         onehot.T,
         grad_zero.reshape(count_series, NPATCH, D).sum(axis=1),

time: 1070 us -> 1020 us (0.953)
  Pallas kernels: 879 us -> 817 us
  local copies, waits for them, and re-layouts: 39.1 us -> 53.4 us
    pallas_call x16 -> x2, Pallas kernels: 140 us -> 77.7 us  [the longest x1 41.7 us: grad_blocks(): pl.pallas_call(grad_kernel, out_shape=jax.ShapeDtypeStruct((TOTAL_SLOTS,...]
where the time goes in v6:
time: 1020 us; the launch traced here: 1010 us
  Pallas kernels  817 us (80%)
  matrix products  82.4 us (8%)
  local copies, waits for them, and re-layouts  53.4 us (5%)
  other arithmetic  49.6 us (5%)
    pallas_call x1, Pallas kernels, scatter_sum(): pl.pallas_call(scatter_kernel, out_shape=(jax.ShapeDtypeStruct((slot_coun...  403 us
    pallas_call x1, Pallas kernels, gather_all(): pl.pallas_call(gather_kernel, out_shape=(jax.ShapeDtypeStruct((4, 2, narr...  336 us
    pallas_call x1, Pallas kernels, grad_blocks(): pl.pallas_call(grad_kernel, out_shape=jax.ShapeDtypeStruct((TOTAL_SLOTS,...  41.7 us
    dot_general x7, matrix products, backmul(): lax.dot_general(left, right, (((1,), (1,)), ((), ())), preferred_element_...  39.8 us
    pallas_call x1, Pallas kernels, unpack(): pl.pallas_call(unpack_kernel, out_shape=tuple((jax.ShapeDtypeStruct((tota...  36 us
    dot_general x9, matrix products, matmul(): return jnp.dot(left, right, preferred_element_type=jnp.float32)  34.9 us

profile of v6, /device:TPU:0, one launch (start us, length us, event | category | flops | bytes accessed | tf_op | source)
XLA Modules:
  0.0 1007.5 jit_solution(18146685825969233390)
XLA Ops:
  3.2 4.3 convert_element_type.144.own_ref
  7.5 336.2 %gather_all.1 = (bf16[4,2,4,16,64,1280]{5,4,3,2,1,0:T(8,128)(2,1)}, f32[32,8,128]{2,1,0:T(8,128)}) custom-call(bf16[16,64,1280]{2,1,0:T(8,128)(2,1)} %convert_element_type.144.own_ref, f32[8,128]{1,0:T(8,128)} %scatter.4.count_ref), custom_call_target="tpu_custom_call" | custom-call | tf_op jit(solution)/shard_map/gather_all/pallas_call | solution.py:980
  343.7 36.0 %unpack.1 = (bf16[64,2560]{1,0:T(8,128)(2,1)}, bf16[1280,1280]{1,0:T(8,128)(2,1)}, bf16[1280,3840]{1,0:T(8,128)(2,1)}, bf16[1280,1280]{1,0:T(8,128)(2,1)}, bf16[...) custom-call(s32[322]{0:T(512)} %owner_ref.3, ...), custom_call_target="tpu_custom_call" | custom-call | bytes 105512960 | tf_op jit(solution)/shard_map/unpack/pallas_call | solution.py:180
  380.1 1.5 fusion.67
  383.9 3.6 multiply_reduce_fusion.6
  389.3 4.6 fusion.68
  394.0 8.0 reshape.325
  402.0 2.6 fusion.60
  404.7 1.7 copy_bitcast_fusion
  407.1 1.3 subtract_convert_fusion.1
  411.5 1.8 slice.207
  414.3 1.2 copy.42
  415.5 2.9 reshape.326.refs_3_
  418.4 3.2 multiply_reduce_fusion.5
  422.4 12.0 %divide_convert_fusion = (bf16[256,5120]{1,0:T(8,128)(2,1)S(1)}, f32[256,5120]{1,0:T(8,128)}) fusion(bf16[256,1280]{1,0:T(8,128)(2,1)S(1)} %multiply_convert_fusion.2.refs_4_, bf16[1280,5120]{1,0:T(8,128)(2,1)} %get-tuple-element.39), kind=kOutput, calls=%fused_computation.6 | convolution fusion | flops 3360686080 | bytes 21626880 | tf_op jit(solution)/shard_map/dot_general | solution.py:35
  434.4 3.7 fusion.5.refs_6_
  438.2 1.9 fusion.69
  441.8 2.1 fusion.3
  443.9 1.6 reshape.327
  445.5 1.4 fusion.64
  448.1 2.3 select_reduce_fusion.2
  450.4 1.3 reshape.333
  451.7 1.3 reduce_sum.318
  453.0 1.3 reshape.334
  454.4 1.3 reduce_sum.321
  457.2 1.3 select_reduce_fusion.4
  459.1 1.3 reshape.335
  460.4 1.3 broadcast_in_dim.83
  461.7 1.3 mul.647
  463.1 3.1 convert_reduce_fusion
  466.2 4.0 fusion.61
  470.2 3.2 fusion.66
  473.4 11.8 %fusion.refs_12_ = bf16[256,5120]{1,0:T(8,128)(2,1)} fusion(bf16[256,1280]{1,0:T(8,128)(2,1)} %get-tuple-element.118.refs_13_, bf16[5120,1280]{1,0:T(8,128)(2,1)} %get-tuple-element.40, f32[256,5120]{1,0:T(8,128)} %get-tuple-element.115), kind=kOutput, calls=%fused_computation.3 | convolution fusion | flops 3367239680 | bytes 21626880 | tf_op jit(solution)/shard_map/dot_general | solution.py:45
  485.2 10.4 %multiply_reduce_fusion.1 = (f32[1280]{0:T(1024)}, f32[256]{0:T(256)S(1)}, f32[256,1280]{1,0:T(8,128)S(1)}) fusion(f32[256,1280]{1,0:T(8,128)} %copy-done, f32[256]{0:T(256)} %copy-done.58, f32[1280]{0:T(1024)} %get-tuple-element.97, bf16[256,5120]{1,0:T(8,128)(2,1)} %fusion.refs_12_, bf16[1280,5120]{1,0:T(8,128)(2,1)} %get-tuple-element.39), kind=kOutput, calls=%fused_computation.62 | convolution fusion | flops 3357407744 | bytes 18362368 | tf_op jit(solution)/shard_map/dot_general | solution.py:45
  495.6 1.4 fusion.58
  498.0 1.9 convolution_convert_fusion
  499.9 3.5 reshape.329
  504.4 2.6 multiply_reduce_fusion
  515.2 2.5 copy.46
  517.7 5.3 convert_element_type.167.refs_10_
  523.0 7.4 multiply_reduce_fusion.2
  537.9 41.7 %grad_blocks.1 = bf16[512,64,1280]{2,1,0:T(8,128)(2,1)} custom-call(s32[322]{0:T(512)} %owner_ref.3, bf16[256,64]{1,0:T(8,128)(2,1)} %copy-done.35, bf16[256,1280]{1,0:T(8,128)(2,1)} %copy-done.12, bf16[256,1280]{1,0:T(8,128)(2,1)} %copy-done.23, bf16[256,1280]{1,0:T(8,128)(2,1)} %reshape.326.refs_3_, bf16[256,1280]{1,0:T(8,128)(2,1)} %copy-done.24, ...), custom_call_target="tpu_custom_call" | custom-call | flops 13505658880 | bytes 52756480 | tf_op jit(solution)/shard_map/grad_blocks/pallas_call | solution.py:275
  580.6 402.6 %scatter_sum.1 = (f32[16,64,1280]{2,1,0:T(8,128)}, f32[32,8,128]{2,1,0:T(8,128)}, f32[32,8,128]{2,1,0:T(8,128)}) custom-call(bf16[4,2,4,16,64,1280]{5,4,3,2,1,0:T(8,128)(2,1)} %bitcast.16.slots_ref, f32[32,8,128]{2,1,0:T(8,128)} %pad_bitcast_fusion.small_ref, f32[16,8,128]{2,1,0:T(8,128)} %broadcast_in_dim.138.filled_ref), custom_call_target="tpu_custom_call" | custom-call | tf_op jit(solution)/shard_map/scatter_sum/pallas_call | solution.py:634
  983.2 1.4 multiply_reduce_fusion.7
  984.6 1.5 reduce_sum.324
  988.2 1.5 multiply_subtract_fusion.2
  989.7 14.8 %fusion.54 = (bf16[16,64,1280]{2,1,0:T(8,128)(2,1)}, f32[16,64,1280]{2,1,0:T(8,128)}, f32[16,64,1280]{2,1,0:T(8,128)}, f32[16,64,1280]{2,1,0:T(8,128)}) fusion(f32[16,64,1280]{2,1,0:T(8,128)} %param.18, f32[]{:T(128)} %bitcast.22, f32[16,64,1280]{2,1,0:T(8,128)} %get-tuple-element.46, f32[]{:T(128)S(6)} %min.3, f32[16,64,1280]{2,1,0:T(8,128)} %param.20, ...), kind=kLoop, calls=%fused_computation.167 | loop fusion | flops 20971520 | bytes 39321608 | tf_op jit(solution)/shard_map/convert_element_type | solution.py:1301
  1004.5 1.4 fusion.47
  (240 shorter events, 35.6 us)
Async XLA Ops:
  1.5 5.9 copy-start.18
  343.7 36.1 %copy-start.40 = (f32[16,640]{1,0:T(8,128)S(1)}, f32[16,640]{1,0:T(8,128)}, u32[]{:S(2)}) copy-start(f32[16,640]{1,0:T(8,128)} %param.13) | copy-start | bytes 122884
  343.7 36.2 %copy-start.39 = (s32[16,640]{1,0:T(8,128)S(1)}, s32[16,640]{1,0:T(8,128)}, u32[]{:S(2)}) copy-start(s32[16,640]{1,0:T(8,128)} %param.14) | copy-start | bytes 122884
  380.1 3.4 copy-start.35
  380.1 3.5 slice-start
  380.1 3.5 copy-start.66
  383.5 4.0 copy-start.12
  383.9 5.4 copy-start.70
  387.6 6.4 copy-start.56
  411.5 2.7 copy-start.36
  418.4 3.3 copy-start.41
  421.7 12.7 %copy-start = (f32[256,1280]{1,0:T(8,128)}, f32[256,1280]{1,0:T(8,128)S(1)}, u32[]{:S(2)}) copy-start(f32[256,1280]{1,0:T(8,128)S(1)} %get-tuple-element.113) | copy-start | bytes 3932164
  421.7 12.7 %slice-start.1 = ((s8[13107200]{0:T(1024)(128)(4,1)}), s8[4194304]{0:T(1024)(128)(4,1)S(1)}, s32[]{:S(2)}) async-start(s8[13107200]{0:T(1024)(128)(4,1)} %bitcast.90), calls=%async_computation.1 | async-start | bytes 8388608
  421.7 16.4 %slice-start.5 = ((s8[6553600]{0:T(1024)(128)(4,1)}), s8[4194304]{0:T(1024)(128)(4,1)S(1)}, s32[]{:S(2)}) async-start(s8[6553600]{0:T(1024)(128)(4,1)} %bitcast.92), calls=%async_computation.5 | async-start | bytes 8388608
  422.3 12.0 %copy-start.24 = (bf16[256,1280]{1,0:T(8,128)(2,1)}, bf16[256,1280]{1,0:T(8,128)(2,1)S(1)}, u32[]{:S(2)}) copy-start(bf16[256,1280]{1,0:T(8,128)(2,1)S(1)} %multiply_convert_fusion.2.refs_4_) | copy-start | bytes 1966084
  422.3 12.1 %slice-start.2 = ((s8[13107200]{0:T(1024)(128)(4,1)}), s8[4194304]{0:T(1024)(128)(4,1)S(1)}, s32[]{:S(2)}) async-start(s8[13107200]{0:T(1024)(128)(4,1)} %bitcast.90), calls=%async_computation.2 | async-start | bytes 8388608
  422.4 12.1 %slice-start.3 = ((s8[13107200]{0:T(1024)(128)(4,1)}), s8[4194304]{0:T(1024)(128)(4,1)S(1)}, s32[]{:S(2)}) async-start(s8[13107200]{0:T(1024)(128)(4,1)} %bitcast.90), calls=%async_computation.3 | async-start | bytes 8388608
  422.4 12.1 %slice-start.4 = ((s8[13107200]{0:T(1024)(128)(4,1)}), s8[524288]{0:T(1024)(128)(4,1)S(1)}, s32[]{:S(2)}) async-start(s8[13107200]{0:T(1024)(128)(4,1)} %bitcast.90), calls=%async_computation.4 | async-start | bytes 1048576
  422.4 15.8 %slice-start.6 = ((s8[6553600]{0:T(1024)(128)(4,1)}), s8[2359296]{0:T(1024)(128)(4,1)S(1)}, s32[]{:S(2)}) async-start(s8[6553600]{0:T(1024)(128)(4,1)} %bitcast.92), calls=%async_computation.6 | async-start | bytes 4718592
  434.4 3.7 copy-start.27
  438.2 3.6 copy-start.62
  438.2 3.6 copy-start.71
  445.5 2.3 copy-start.19
  447.8 2.5 copy-start.16
  448.1 2.3 copy-start.53
  463.0 3.1 copy-start.34
  463.0 3.1 copy-start.51
  463.1 7.1 slice-start.7
  466.2 4.0 copy-start.13
  466.2 4.0 slice-start.8
  470.2 3.2 copy-start.31
  485.1 10.4 %copy-start.61 = (f32[256]{0:T(256)S(1)}, f32[256]{0:T(256)}, u32[]{:S(2)}) copy-start(f32[256]{0:T(256)} %copy-done.60) | copy-start | bytes 3076
  485.1 10.4 %copy-start.1 = (f32[256,1280]{1,0:T(8,128)S(1)}, f32[256,1280]{1,0:T(8,128)}, u32[]{:S(2)}) copy-start(f32[256,1280]{1,0:T(8,128)} %copy-done) | copy-start | bytes 3932164
  485.1 10.4 %copy-start.29 = (f32[256,1280]{1,0:T(8,128)S(1)}, f32[256,1280]{1,0:T(8,128)}, u32[]{:S(2)}) copy-start(f32[256,1280]{1,0:T(8,128)} %get-tuple-element.119) | copy-start | bytes 3932164
  485.1 10.4 %copy-start.42 = (f32[1280]{0:T(1024)S(1)}, f32[1280]{0:T(1024)}, u32[]{:S(2)}) copy-start(f32[1280]{0:T(1024)} %get-tuple-element.97) | copy-start | bytes 15364
  485.1 10.4 %copy-start.59 = (f32[256]{0:T(256)S(1)}, f32[256]{0:T(256)}, u32[]{:S(2)}) copy-start(f32[256]{0:T(256)} %copy-done.58) | copy-start | bytes 3076
  495.6 2.5 copy-start.22
  523.0 7.4 copy-start.11
  523.0 7.4 copy-start.57
  523.0 7.4 copy-start.17
  530.4 2.7 copy-start.21
  530.4 2.7 copy-start.48
  533.1 3.6 copy-start.15
  537.9 41.7 %copy-start.55 = (s32[322]{0:T(512)S(1)}, s32[322]{0:T(512)}, u32[]{:S(2)}) copy-start(s32[322]{0:T(512)} %owner_ref.3) | copy-start | bytes 3868
  580.6 407.7 %copy-start.38 = (f32[11520]{0:T(1024)S(1)}, f32[11520]{0:T(1024)}, u32[]{:S(2)}) copy-start(f32[11520]{0:T(1024)} %param.21) | copy-start | bytes 138244
  580.6 407.7 %copy-start.45 = (f32[11520]{0:T(1024)S(1)}, f32[11520]{0:T(1024)}, u32[]{:S(2)}) copy-start(f32[11520]{0:T(1024)} %param.23) | copy-start | bytes 138244
  580.6 407.7 %copy-start.46 = (f32[11520]{0:T(1024)S(1)}, f32[11520]{0:T(1024)}, u32[]{:S(2)}) copy-start(f32[11520]{0:T(1024)} %param.22) | copy-start | bytes 138244
  989.7 14.8 %copy-start.69 = (f32[3]{0:T(128)S(1)}, f32[3]{0:T(128)}, u32[]{:S(2)}) copy-start(f32[3]{0:T(128)} %copy-done.68) | copy-start | bytes 40
  (34 other events, 47.2 us)

commit v7 on v6

--- a/solution.py
+++ b/solution.py
@@ -89,6 +89,7 @@
 BASES = tuple(sum(r * g for r, g, _ in MATS[:i]) // BR for i in range(len(MATS)))
 LANES = 128
 VMEM_LIMIT = 56 * 1024 * 1024
+SCATTER_VMEM = 61 * 1024 * 1024
 
 
 RING = 48
@@ -295,7 +296,10 @@
 
 
 CHUNKS = 16
-STEPS = CHUNKS + 7
+LATE = 4
+EARLY = CHUNKS - LATE
+COMBOS = 4 * LATE
+STEPS = COMBOS + 5
 MESH = pl.DeviceIdType.MESH
 
 
@@ -326,6 +330,18 @@
     up_out,
     down_out,
     result,
+    late_own,
+    late_pair_in,
+    late_sum,
+    late_up_in,
+    late_down_in,
+    late_up_out,
+    late_down_out,
+    late_column,
+    late_first_in,
+    late_second_in,
+    late_second_out,
+    late_result,
     own_sem,
     pair_send,
     pair_recv,
@@ -338,6 +354,18 @@
     down_send,
     down_recv,
     result_sem,
+    late_own_sem,
+    late_pair_send,
+    late_pair_recv,
+    late_up_send,
+    late_up_recv,
+    late_down_send,
+    late_down_recv,
+    late_first_send,
+    late_first_recv,
+    late_second_send,
+    late_second_recv,
+    late_result_sem,
     share_send,
     share_recv,
     spread_send,
@@ -440,31 +468,133 @@
             device_id_type=MESH,
         )
 
-    def line_copy(k, level, source, target, send, recv, step):
+    def line_copy(source, target, send, recv, way):
+        base = 1 if way > 0 else 0
+
+        def make(k, level):
+            return pltpu.make_async_remote_copy(
+                src_ref=source.at[lax.rem(k, 2), level - base],
+                dst_ref=target.at[lax.rem(k, 6), level - base],
+                send_sem=send.at[lax.rem(k, 2), level - base],
+                recv_sem=recv.at[lax.rem(k, 6), level - base],
+                device_id=device(here, z + way),
+                device_id_type=MESH,
+            )
+
+        return make
+
+    def late_own_copy(c):
+        at = lax.rem(c, 2)
+        return pltpu.make_async_copy(
+            slots_ref.at[lax.rem(c, 4), core, :, EARLY + lax.div(c, 4)],
+            late_own.at[at],
+            late_own_sem.at[at],
+        )
+
+    def late_pair_copy(c):
+        at = lax.rem(c, 2)
         return pltpu.make_async_remote_copy(
-            src_ref=source.at[lax.rem(k, 2), level],
-            dst_ref=target.at[lax.rem(k, 6), level],
-            send_sem=send.at[lax.rem(k, 2), level],
-            recv_sem=recv.at[lax.rem(k, 6), level],
-            device_id=device(here, z + step),
+            src_ref=slots_ref.at[lax.rem(c, 4), 1 - core, :, EARLY + lax.div(c, 4)],
+            dst_ref=late_pair_in.at[at],
+            send_sem=late_pair_send.at[at],
+            recv_sem=late_pair_recv.at[at],
+            device_id=partner,
             device_id_type=MESH,
         )
 
-    def up_copy(k, level):
-        return line_copy(k, level, up_out, up_in, up_send, up_recv, 1)
-
-    def down_copy(k, level):
-        return line_copy(k, level, down_out, down_in, down_send, down_recv, -1)
+    def late_first_copy(slot, part):
+        place = near(slot, 0)
+        return pltpu.make_async_remote_copy(
+            src_ref=late_column.at[slot, far if part == 0 else place],
+            dst_ref=late_first_in.at[slot, part],
+            send_sem=late_first_send.at[slot, part],
+            recv_sem=late_first_recv.at[slot, part],
+            device_id=device(place, z),
+            device_id_type=MESH,
+        )
+
+    def late_second_copy(slot):
+        return pltpu.make_async_remote_copy(
+            src_ref=late_second_out.at[slot],
+            dst_ref=late_second_in.at[slot],
+            send_sem=late_second_send.at[slot],
+            recv_sem=late_second_recv.at[slot],
+            device_id=device(near(slot, 1), z),
+            device_id_type=MESH,
+        )
+
+    def late_result_copy(slot):
+        return pltpu.make_async_copy(late_result, out_ref.at[EARLY + slot], late_result_sem)
 
     def result_copy(k):
         at = lax.rem(k, 2)
         return pltpu.make_async_copy(result.at[at], out_ref.at[k], result_sem.at[at])
 
     def valid(k):
-        return jnp.logical_and(k >= 0, k < CHUNKS)
+        return jnp.logical_and(k >= 0, k < EARLY)
+
+    def valid_late(c):
+        return jnp.logical_and(c >= 0, c < COMBOS)
+
+    def keep(ref, k):
+        kept = jnp.where(filled_ref[k, 0:1, 0:1] > 0.0, ref[...], 0.0)
+        ref[...] = kept
+        squares = square_out[me]
+        for i in range(BR // 8):
+            for j in range(D // LANES):
+                part = kept[i * 8 : (i + 1) * 8, j * LANES : (j + 1) * LANES]
+                squares = squares + part * part
+        square_out[me] = squares
+
+    def flows(lags, known, sums, ring, ins, outs, copies):
+        for base, lag, behind, copy, arrived, leaving in zip(
+            (1, 0), lags, (z > 0, z < 3), copies, ins, outs
+        ):
+            k = lag
+            for n in range(base, base + 3):
+                ahead = n > z if base else n < z
+
+                @pl.when(jnp.logical_and(known(k - 2), ahead))
+                def _(n=n, k=k, copy=copy):
+                    copy(k - 2, n).wait_send()
+
+                @pl.when(
+                    jnp.logical_and(
+                        jnp.logical_and(known(k), behind), jnp.logical_or(ahead, n == z)
+                    )
+                )
+                def _(n=n, k=k, copy=copy):
+                    copy(k, n).wait_recv()
+
+                moving = jnp.logical_and(known(k), ahead)
+
+                @pl.when(jnp.logical_and(moving, behind))
+                def _(n=n, k=k, base=base, arrived=arrived, leaving=leaving):
+                    leaving[lax.rem(k, 2), n - base] = total_of(
+                        sums[lax.rem(k, ring), n], arrived[lax.rem(k, 6), n - base]
+                    ).astype(jnp.bfloat16)
+
+                @pl.when(jnp.logical_and(moving, jnp.logical_not(behind)))
+                def _(n=n, k=k, base=base, leaving=leaving):
+                    leaving[lax.rem(k, 2), n - base] = sums[lax.rem(k, ring), n]
+
+                @pl.when(moving)
+                def _(n=n, k=k, copy=copy):
+                    copy(k, n).start()
+
+    copies = (
+        line_copy(up_out, up_in, up_send, up_recv, 1),
+        line_copy(down_out, down_in, down_send, down_recv, -1),
+    )
+    late_copies = (
+        line_copy(late_up_out, late_up_in, late_up_send, late_up_recv, 1),
+        line_copy(late_down_out, late_down_in, late_down_send, late_down_recv, -1),
+    )
 
     own_copy(0).start()
     pair_copy(0).start()
+    late_own_copy(0).start()
+    late_pair_copy(0).start()
     each(lambda *at: share(*at).start())
 
     def step(t, carry):
@@ -494,10 +624,32 @@
         def _():
             pair_copy(t - 1).wait_send()
 
-        @pl.when(t + 1 < CHUNKS)
+        @pl.when(t + 1 < EARLY)
         def _():
             own_copy(t + 1).start()
             pair_copy(t + 1).start()
+
+        @pl.when(valid_late(t))
+        def _():
+            late_own_copy(t).wait()
+            late_pair_copy(t).wait_recv()
+
+            def add(n, inner):
+                late_sum[lax.rem(t, 4), n] = total_of(
+                    late_own[lax.rem(t, 2), n], late_pair_in[lax.rem(t, 2), n]
+                ).astype(jnp.bfloat16)
+                return inner
+
+            lax.fori_loop(0, 4, add, 0)
+
+        @pl.when(valid_late(t - 1))
+        def _():
+            late_pair_copy(t - 1).wait_send()
+
+        @pl.when(t + 1 < COMBOS)
+        def _():
+            late_own_copy(t + 1).start()
+            late_pair_copy(t + 1).start()
 
         @pl.when(valid(t - 3))
         def _():
@@ -534,40 +686,68 @@
 
             lax.fori_loop(0, 4, add, 0)
 
-        for lag, ahead, behind, copy, arrived, leaving in (
-            (z, lambda n: n > z, z > 0, up_copy, up_in, up_out),
-            (3 - z, lambda n: n < z, z < 3, down_copy, down_in, down_out),
-        ):
-            k = t - 2 - lag
-            for n in range(4):
-
-                @pl.when(jnp.logical_and(valid(k - 2), ahead(n)))
-                def _(n=n, k=k, copy=copy):
-                    copy(k - 2, n).wait_send()
-
-                @pl.when(
-                    jnp.logical_and(
-                        jnp.logical_and(valid(k), behind), jnp.logical_or(ahead(n), n == z)
-                    )
+        flows(
+            (t - 2 - z, t - 5 + z), valid, column, 4, (up_in, down_in), (up_out, down_out), copies
+        )
+        flows(
+            (t - z, t - 3 + z),
+            valid_late,
+            late_sum,
+            4,
+            (late_up_in, late_down_in),
+            (late_up_out, late_down_out),
+            late_copies,
+        )
+        c = t - 3
+
+        @pl.when(valid_late(c))
+        def _():
+            slot, p = lax.div(c, 4), lax.rem(c, 4)
+            mine = late_sum.at[lax.rem(c, 4), z]
+            below = late_up_in.at[lax.rem(c, 6), jnp.maximum(z - 1, 0)]
+            above = late_down_in.at[lax.rem(c, 6), jnp.minimum(z, 2)]
+
+            @pl.when(z == 0)
+            def _():
+                late_column[slot, p] = total_of(mine[...], above[...]).astype(jnp.bfloat16)
+
+            @pl.when(z == 3)
+            def _():
+                late_column[slot, p] = total_of(mine[...], below[...]).astype(jnp.bfloat16)
+
+            @pl.when(jnp.logical_and(z > 0, z < 3))
+            def _():
+                late_column[slot, p] = total_of(mine[...], below[...], above[...]).astype(
+                    jnp.bfloat16
                 )
-                def _(n=n, k=k, copy=copy):
-                    copy(k, n).wait_recv()
-
-                moving = jnp.logical_and(valid(k), ahead(n))
-
-                @pl.when(jnp.logical_and(moving, behind))
-                def _(n=n, k=k, arrived=arrived, leaving=leaving):
-                    leaving[lax.rem(k, 2), n] = total_of(
-                        column[lax.rem(k, 4), n], arrived[lax.rem(k, 6), n]
-                    ).astype(jnp.bfloat16)
-
-                @pl.when(jnp.logical_and(moving, jnp.logical_not(behind)))
-                def _(n=n, k=k, leaving=leaving):
-                    leaving[lax.rem(k, 2), n] = column[lax.rem(k, 4), n]
-
-                @pl.when(moving)
-                def _(n=n, k=k, copy=copy):
-                    copy(k, n).start()
+
+        for slot in range(LATE):
+            place = near(slot, 1)
+
+            @pl.when(t == 4 * slot + 6)
+            def _(slot=slot):
+                late_first_copy(slot, 0).start()
+                late_first_copy(slot, 1).start()
+
+            @pl.when(t == 4 * slot + 7)
+            def _(slot=slot, place=place):
+                late_first_copy(slot, 0).wait_recv()
+                late_second_out[slot] = total_of(
+                    late_column[slot, place], late_first_in[slot, 0]
+                ).astype(jnp.bfloat16)
+                late_second_copy(slot).start()
+
+            @pl.when(t == 4 * slot + 8)
+            def _(slot=slot):
+                late_first_copy(slot, 1).wait_recv()
+                late_second_copy(slot).wait_recv()
+                if slot:
+                    late_result_copy(slot - 1).wait()
+                late_result[...] = total_of(
+                    late_column[slot, here], late_first_in[slot, 1], late_second_in[slot]
+                )
+                keep(late_result, EARLY + slot)
+                late_result_copy(slot).start()
 
         k = t - 5
 
@@ -581,20 +761,13 @@
 
             @pl.when(z > 0)
             def _():
-                result[lax.rem(k, 2)] += up_in[lax.rem(k, 6), z].astype(jnp.float32)
+                result[lax.rem(k, 2)] += up_in[lax.rem(k, 6), z - 1].astype(jnp.float32)
 
             @pl.when(z < 3)
             def _():
                 result[lax.rem(k, 2)] += down_in[lax.rem(k, 6), z].astype(jnp.float32)
 
-            kept = jnp.where(filled_ref[k, 0:1, 0:1] > 0.0, result[lax.rem(k, 2)], 0.0)
-            result[lax.rem(k, 2)] = kept
-            squares = square_out[me]
-            for i in range(BR // 8):
-                for j in range(D // LANES):
-                    part = kept[i * 8 : (i + 1) * 8, j * LANES : (j + 1) * LANES]
-                    squares = squares + part * part
-            square_out[me] = squares
+            keep(result.at[lax.rem(k, 2)], k)
             result_copy(k).start()
 
         @pl.when(t == CHUNKS // 2)
@@ -610,6 +783,11 @@
 
     lax.fori_loop(0, STEPS, step, 0)
     each(lambda *at: square(*at).start())
+    late_result_copy(LATE - 1).wait()
+    for slot in range(LATE):
+        late_first_copy(slot, 0).wait_send()
+        late_first_copy(slot, 1).wait_send()
+        late_second_copy(slot).wait_send()
     each(lambda *at: spread(*at).wait())
     each(lambda *at: square(*at).wait())
 
@@ -657,11 +835,23 @@
             low((4, 4) + block),
             low((2, 4) + block),
             low((4, 4) + block),
-            low((6, 4) + block),
-            low((6, 4) + block),
+            low((6, 3) + block),
+            low((6, 3) + block),
+            low((2, 3) + block),
+            low((2, 3) + block),
+            pltpu.VMEM((2,) + block, jnp.float32),
             low((2, 4) + block),
             low((2, 4) + block),
-            pltpu.VMEM((2,) + block, jnp.float32),
+            low((4, 4) + block),
+            low((6, 3) + block),
+            low((6, 3) + block),
+            low((2, 3) + block),
+            low((2, 3) + block),
+            low((LATE, 4) + block),
+            low((LATE, 2) + block),
+            low((LATE,) + block),
+            low((LATE,) + block),
+            pltpu.VMEM(block, jnp.float32),
             dma((2,)),
             dma((2,)),
             dma((2,)),
@@ -669,15 +859,27 @@
             dma((5, 2)),
             dma((2,)),
             dma((4,)),
-            dma((2, 4)),
-            dma((6, 4)),
-            dma((2, 4)),
-            dma((6, 4)),
+            dma((2, 3)),
+            dma((6, 3)),
+            dma((2, 3)),
+            dma((6, 3)),
             dma((2,)),
+            dma((2,)),
+            dma((2,)),
+            dma((2,)),
+            dma((2, 3)),
+            dma((6, 3)),
+            dma((2, 3)),
+            dma((6, 3)),
+            dma((LATE, 2)),
+            dma((LATE, 2)),
+            dma((LATE,)),
+            dma((LATE,)),
+            dma,
         ]
         + [dma((wide * narrow,))] * 6,
         compiler_params=pltpu.CompilerParams(
-            collective_id=1, has_side_effects=True, vmem_limit_bytes=VMEM_LIMIT
+            collective_id=1, has_side_effects=True, vmem_limit_bytes=SCATTER_VMEM
         ),
         name="scatter_sum",
     )(
@@ -690,9 +892,6 @@
     return owned, jnp.sum(square_tiles), small_tiles.reshape(-1)[: small.shape[0]]
 
 
-LATE = 4
-EARLY = CHUNKS - LATE
-COMBOS = 4 * LATE
 GATHER_STEPS = EARLY + 5
 
 

time: 1020 us -> 995 us (0.975)
  Pallas kernels: 817 us -> 794 us
    pallas_call x1, Pallas kernels: 403 us -> 380 us  [scatter_sum(): pl.pallas_call(scatter_kernel, out_shape=(jax.ShapeDtypeStruct((slot_coun...]
where the time goes in v7:
time: 995 us; the launch traced here: 985 us
  Pallas kernels  794 us (80%)
  matrix products  82.4 us (8%)
  local copies, waits for them, and re-layouts  53.4 us (5%)
  other arithmetic  49.6 us (5%)
    pallas_call x1, Pallas kernels, scatter_sum(): pl.pallas_call(scatter_kernel, out_shape=(jax.ShapeDtypeStruct((slot_coun...  380 us
    pallas_call x1, Pallas kernels, gather_all(): pl.pallas_call(gather_kernel, out_shape=(jax.ShapeDtypeStruct((4, 2, narr...  336 us
    pallas_call x1, Pallas kernels, grad_blocks(): pl.pallas_call(grad_kernel, out_shape=jax.ShapeDtypeStruct((TOTAL_SLOTS,...  41.7 us
    dot_general x7, matrix products, backmul(): lax.dot_general(left, right, (((1,), (1,)), ((), ())), preferred_element_...  39.8 us
    pallas_call x1, Pallas kernels, unpack(): pl.pallas_call(unpack_kernel, out_shape=tuple((jax.ShapeDtypeStruct((tota...  36 us
    dot_general x9, matrix products, matmul(): return jnp.dot(left, right, preferred_element_type=jnp.float32)  34.9 us

profile of v7, /device:TPU:0, one launch (start us, length us, event | category | flops | bytes accessed | tf_op | source)
XLA Modules:
  0.0 985.1 jit_solution(14017246827107273804)
XLA Ops:
  3.2 4.3 convert_element_type.144.own_ref
  7.5 336.2 %gather_all.1 = (bf16[4,2,4,16,64,1280]{5,4,3,2,1,0:T(8,128)(2,1)}, f32[32,8,128]{2,1,0:T(8,128)}) custom-call(bf16[16,64,1280]{2,1,0:T(8,128)(2,1)} %convert_element_type.144.own_ref, f32[8,128]{1,0:T(8,128)} %scatter.4.count_ref), custom_call_target="tpu_custom_call" | custom-call | tf_op jit(solution)/shard_map/gather_all/pallas_call | solution.py:1179
  343.7 36.0 %unpack.1 = (bf16[64,2560]{1,0:T(8,128)(2,1)}, bf16[1280,1280]{1,0:T(8,128)(2,1)}, bf16[1280,3840]{1,0:T(8,128)(2,1)}, bf16[1280,1280]{1,0:T(8,128)(2,1)}, bf16[...) custom-call(s32[322]{0:T(512)} %owner_ref.3, ...), custom_call_target="tpu_custom_call" | custom-call | bytes 105512960 | tf_op jit(solution)/shard_map/unpack/pallas_call | solution.py:181
  380.1 1.5 fusion.67
  383.9 3.6 multiply_reduce_fusion.6
  389.3 4.6 fusion.68
  394.0 8.0 reshape.325
  402.0 2.6 fusion.60
  404.7 1.7 copy_bitcast_fusion
  407.1 1.3 subtract_convert_fusion.1
  411.5 1.8 slice.207
  414.3 1.2 copy.42
  415.5 2.9 reshape.326.refs_3_
  418.4 3.2 multiply_reduce_fusion.5
  422.4 12.0 %divide_convert_fusion = (bf16[256,5120]{1,0:T(8,128)(2,1)S(1)}, f32[256,5120]{1,0:T(8,128)}) fusion(bf16[256,1280]{1,0:T(8,128)(2,1)S(1)} %multiply_convert_fusion.2.refs_4_, bf16[1280,5120]{1,0:T(8,128)(2,1)} %get-tuple-element.39), kind=kOutput, calls=%fused_computation.6 | convolution fusion | flops 3360686080 | bytes 21626880 | tf_op jit(solution)/shard_map/dot_general | solution.py:35
  434.4 3.7 fusion.5.refs_6_
  438.2 1.9 fusion.69
  441.8 2.1 fusion.3
  443.9 1.6 reshape.327
  445.5 1.4 fusion.64
  448.1 2.3 select_reduce_fusion.2
  450.4 1.3 reshape.333
  451.7 1.3 reduce_sum.318
  453.0 1.3 reshape.334
  454.4 1.3 reduce_sum.321
  457.2 1.3 select_reduce_fusion.4
  459.1 1.3 reshape.335
  460.4 1.3 broadcast_in_dim.83
  461.7 1.3 mul.647
  463.1 3.1 convert_reduce_fusion
  466.2 4.0 fusion.61
  470.2 3.2 fusion.66
  473.4 11.8 %fusion.refs_12_ = bf16[256,5120]{1,0:T(8,128)(2,1)} fusion(bf16[256,1280]{1,0:T(8,128)(2,1)} %get-tuple-element.118.refs_13_, bf16[5120,1280]{1,0:T(8,128)(2,1)} %get-tuple-element.40, f32[256,5120]{1,0:T(8,128)} %get-tuple-element.115), kind=kOutput, calls=%fused_computation.3 | convolution fusion | flops 3367239680 | bytes 21626880 | tf_op jit(solution)/shard_map/dot_general | solution.py:45
  485.2 10.4 %multiply_reduce_fusion.1 = (f32[1280]{0:T(1024)}, f32[256]{0:T(256)S(1)}, f32[256,1280]{1,0:T(8,128)S(1)}) fusion(f32[256,1280]{1,0:T(8,128)} %copy-done, f32[256]{0:T(256)} %copy-done.58, f32[1280]{0:T(1024)} %get-tuple-element.97, bf16[256,5120]{1,0:T(8,128)(2,1)} %fusion.refs_12_, bf16[1280,5120]{1,0:T(8,128)(2,1)} %get-tuple-element.39), kind=kOutput, calls=%fused_computation.62 | convolution fusion | flops 3357407744 | bytes 18362368 | tf_op jit(solution)/shard_map/dot_general | solution.py:45
  495.6 1.4 fusion.58
  498.0 1.9 convolution_convert_fusion
  499.9 3.5 reshape.329
  504.4 2.6 multiply_reduce_fusion
  515.2 2.5 copy.46
  517.7 5.3 convert_element_type.167.refs_10_
  523.0 7.4 multiply_reduce_fusion.2
  537.9 41.7 %grad_blocks.1 = bf16[512,64,1280]{2,1,0:T(8,128)(2,1)} custom-call(s32[322]{0:T(512)} %owner_ref.3, bf16[256,64]{1,0:T(8,128)(2,1)} %copy-done.35, bf16[256,1280]{1,0:T(8,128)(2,1)} %copy-done.12, bf16[256,1280]{1,0:T(8,128)(2,1)} %copy-done.23, bf16[256,1280]{1,0:T(8,128)(2,1)} %reshape.326.refs_3_, bf16[256,1280]{1,0:T(8,128)(2,1)} %copy-done.24, ...), custom_call_target="tpu_custom_call" | custom-call | flops 13505658880 | bytes 52756480 | tf_op jit(solution)/shard_map/grad_blocks/pallas_call | solution.py:276
  580.6 380.1 %scatter_sum.1 = (f32[16,64,1280]{2,1,0:T(8,128)}, f32[32,8,128]{2,1,0:T(8,128)}, f32[32,8,128]{2,1,0:T(8,128)}) custom-call(bf16[4,2,4,16,64,1280]{5,4,3,2,1,0:T(8,128)(2,1)} %bitcast.16.slots_ref, f32[32,8,128]{2,1,0:T(8,128)} %pad_bitcast_fusion.small_ref, f32[16,8,128]{2,1,0:T(8,128)} %broadcast_in_dim.138.filled_ref), custom_call_target="tpu_custom_call" | custom-call | tf_op jit(solution)/shard_map/scatter_sum/pallas_call | solution.py:812
  960.7 1.4 multiply_reduce_fusion.7
  962.1 1.5 reduce_sum.324
  965.8 1.5 multiply_subtract_fusion.2
  967.2 14.8 %fusion.54 = (bf16[16,64,1280]{2,1,0:T(8,128)(2,1)}, f32[16,64,1280]{2,1,0:T(8,128)}, f32[16,64,1280]{2,1,0:T(8,128)}, f32[16,64,1280]{2,1,0:T(8,128)}) fusion(f32[16,64,1280]{2,1,0:T(8,128)} %param.18, f32[]{:T(128)} %bitcast.22, f32[16,64,1280]{2,1,0:T(8,128)} %get-tuple-element.46, f32[]{:T(128)S(6)} %min.3, f32[16,64,1280]{2,1,0:T(8,128)} %param.20, ...), kind=kLoop, calls=%fused_computation.167 | loop fusion | flops 20971520 | bytes 39321608 | tf_op jit(solution)/shard_map/convert_element_type | solution.py:1500
  982.0 1.4 fusion.47
  (240 shorter events, 35.6 us)
Async XLA Ops:
  1.5 5.9 copy-start.18
  343.7 36.1 %copy-start.40 = (f32[16,640]{1,0:T(8,128)S(1)}, f32[16,640]{1,0:T(8,128)}, u32[]{:S(2)}) copy-start(f32[16,640]{1,0:T(8,128)} %param.13) | copy-start | bytes 122884
  343.7 36.2 %copy-start.39 = (s32[16,640]{1,0:T(8,128)S(1)}, s32[16,640]{1,0:T(8,128)}, u32[]{:S(2)}) copy-start(s32[16,640]{1,0:T(8,128)} %param.14) | copy-start | bytes 122884
  380.1 3.4 copy-start.35
  380.1 3.5 slice-start
  380.1 3.5 copy-start.66
  383.5 4.0 copy-start.12
  383.9 5.4 copy-start.70
  387.6 6.4 copy-start.56
  411.5 2.7 copy-start.36
  418.4 3.3 copy-start.41
  421.7 12.7 %copy-start = (f32[256,1280]{1,0:T(8,128)}, f32[256,1280]{1,0:T(8,128)S(1)}, u32[]{:S(2)}) copy-start(f32[256,1280]{1,0:T(8,128)S(1)} %get-tuple-element.113) | copy-start | bytes 3932164
  421.7 12.7 %slice-start.1 = ((s8[13107200]{0:T(1024)(128)(4,1)}), s8[4194304]{0:T(1024)(128)(4,1)S(1)}, s32[]{:S(2)}) async-start(s8[13107200]{0:T(1024)(128)(4,1)} %bitcast.90), calls=%async_computation.1 | async-start | bytes 8388608
  421.7 16.4 %slice-start.5 = ((s8[6553600]{0:T(1024)(128)(4,1)}), s8[4194304]{0:T(1024)(128)(4,1)S(1)}, s32[]{:S(2)}) async-start(s8[6553600]{0:T(1024)(128)(4,1)} %bitcast.92), calls=%async_computation.5 | async-start | bytes 8388608
  422.3 12.0 %copy-start.24 = (bf16[256,1280]{1,0:T(8,128)(2,1)}, bf16[256,1280]{1,0:T(8,128)(2,1)S(1)}, u32[]{:S(2)}) copy-start(bf16[256,1280]{1,0:T(8,128)(2,1)S(1)} %multiply_convert_fusion.2.refs_4_) | copy-start | bytes 1966084
  422.3 12.1 %slice-start.2 = ((s8[13107200]{0:T(1024)(128)(4,1)}), s8[4194304]{0:T(1024)(128)(4,1)S(1)}, s32[]{:S(2)}) async-start(s8[13107200]{0:T(1024)(128)(4,1)} %bitcast.90), calls=%async_computation.2 | async-start | bytes 8388608
  422.4 12.1 %slice-start.3 = ((s8[13107200]{0:T(1024)(128)(4,1)}), s8[4194304]{0:T(1024)(128)(4,1)S(1)}, s32[]{:S(2)}) async-start(s8[13107200]{0:T(1024)(128)(4,1)} %bitcast.90), calls=%async_computation.3 | async-start | bytes 8388608
  422.4 12.1 %slice-start.4 = ((s8[13107200]{0:T(1024)(128)(4,1)}), s8[524288]{0:T(1024)(128)(4,1)S(1)}, s32[]{:S(2)}) async-start(s8[13107200]{0:T(1024)(128)(4,1)} %bitcast.90), calls=%async_computation.4 | async-start | bytes 1048576
  422.4 15.8 %slice-start.6 = ((s8[6553600]{0:T(1024)(128)(4,1)}), s8[2359296]{0:T(1024)(128)(4,1)S(1)}, s32[]{:S(2)}) async-start(s8[6553600]{0:T(1024)(128)(4,1)} %bitcast.92), calls=%async_computation.6 | async-start | bytes 4718592
  434.4 3.7 copy-start.27
  438.2 3.6 copy-start.62
  438.2 3.6 copy-start.71
  445.5 2.3 copy-start.19
  447.8 2.5 copy-start.16
  448.1 2.3 copy-start.53
  463.0 3.1 copy-start.34
  463.0 3.1 copy-start.51
  463.1 7.1 slice-start.7
  466.2 4.0 copy-start.13
  466.2 4.0 slice-start.8
  470.2 3.2 copy-start.31
  485.1 10.4 %copy-start.61 = (f32[256]{0:T(256)S(1)}, f32[256]{0:T(256)}, u32[]{:S(2)}) copy-start(f32[256]{0:T(256)} %copy-done.60) | copy-start | bytes 3076
  485.1 10.4 %copy-start.1 = (f32[256,1280]{1,0:T(8,128)S(1)}, f32[256,1280]{1,0:T(8,128)}, u32[]{:S(2)}) copy-start(f32[256,1280]{1,0:T(8,128)} %copy-done) | copy-start | bytes 3932164
  485.1 10.4 %copy-start.29 = (f32[256,1280]{1,0:T(8,128)S(1)}, f32[256,1280]{1,0:T(8,128)}, u32[]{:S(2)}) copy-start(f32[256,1280]{1,0:T(8,128)} %get-tuple-element.119) | copy-start | bytes 3932164
  485.1 10.4 %copy-start.42 = (f32[1280]{0:T(1024)S(1)}, f32[1280]{0:T(1024)}, u32[]{:S(2)}) copy-start(f32[1280]{0:T(1024)} %get-tuple-element.97) | copy-start | bytes 15364
  485.1 10.4 %copy-start.59 = (f32[256]{0:T(256)S(1)}, f32[256]{0:T(256)}, u32[]{:S(2)}) copy-start(f32[256]{0:T(256)} %copy-done.58) | copy-start | bytes 3076
  495.6 2.5 copy-start.22
  523.0 7.4 copy-start.11
  523.0 7.4 copy-start.57
  523.0 7.4 copy-start.17
  530.4 2.7 copy-start.21
  530.4 2.7 copy-start.48
  533.1 3.6 copy-start.15
  537.9 41.7 %copy-start.55 = (s32[322]{0:T(512)S(1)}, s32[322]{0:T(512)}, u32[]{:S(2)}) copy-start(s32[322]{0:T(512)} %owner_ref.3) | copy-start | bytes 3868
  580.6 385.2 %copy-start.38 = (f32[11520]{0:T(1024)S(1)}, f32[11520]{0:T(1024)}, u32[]{:S(2)}) copy-start(f32[11520]{0:T(1024)} %param.21) | copy-start | bytes 138244
  580.6 385.2 %copy-start.45 = (f32[11520]{0:T(1024)S(1)}, f32[11520]{0:T(1024)}, u32[]{:S(2)}) copy-start(f32[11520]{0:T(1024)} %param.23) | copy-start | bytes 138244
  580.6 385.2 %copy-start.46 = (f32[11520]{0:T(1024)S(1)}, f32[11520]{0:T(1024)}, u32[]{:S(2)}) copy-start(f32[11520]{0:T(1024)} %param.22) | copy-start | bytes 138244
  967.2 14.8 %copy-start.69 = (f32[3]{0:T(128)S(1)}, f32[3]{0:T(128)}, u32[]{:S(2)}) copy-start(f32[3]{0:T(128)} %copy-done.68) | copy-start | bytes 40
  (34 other events, 47.2 us)

commit v8 on v7

--- a/solution.py
+++ b/solution.py
@@ -67,13 +67,100 @@
     return (jnp.cos(angle)[None, :, None, :], jnp.sin(angle)[None, :, None, :])
 
 
-def rotate(value, cosine, sine):
+SPAN = 640
+
+
+def turned(value, cosine, sine):
     half = HDIM // 2
-    first = value[..., :half]
-    second = value[..., half:]
-    return jnp.concatenate(
-        [first * cosine - second * sine, first * sine + second * cosine], axis=-1
-    )
+    lane = lax.rem(lax.broadcasted_iota(jnp.int32, value.shape, 1), HDIM)
+    other = jnp.where(lane < half, pltpu.roll(value, D - half, 1), pltpu.roll(value, half, 1))
+    shape = (value.shape[0] // NPATCH, NPATCH, D)
+    return (
+        value.reshape(shape) * cosine[None] + other.reshape(shape) * sine[None]
+    ).reshape(value.shape)
+
+
+def attended(queries, keys):
+    scores = backmul(queries, keys)
+    row = lax.broadcasted_iota(jnp.int32, scores.shape, 0)
+    column = lax.broadcasted_iota(jnp.int32, scores.shape, 1)
+    seen = jnp.logical_and(column <= row, column >= row - lax.rem(row, NPATCH))
+    scores = jnp.where(seen, scores, -1e30)
+    expo = jnp.exp(scores - jnp.max(scores, axis=-1, keepdims=True))
+    return expo / jnp.sum(expo, axis=-1, keepdims=True)
+
+
+def head_lanes(h):
+    lane = lax.broadcasted_iota(jnp.int32, (1, SPAN), 1)
+    inside = jnp.logical_and(lane >= h * HDIM, lane < (h + 1) * HDIM)
+    return jnp.where(inside, 1.0, 0.0)
+
+
+def attend_kernel(qkv_ref, cos_ref, sin_ref, query_ref, key_ref, value_ref, mixed_ref, total_ref):
+    cosine, sine = cos_ref[...], sin_ref[...]
+    query_ref[...] = (turned(qkv_ref[:, 0:D], cosine, sine) * HDIM ** (-0.5)).astype(jnp.bfloat16)
+    key_ref[...] = turned(qkv_ref[:, D : 2 * D], cosine, sine).astype(jnp.bfloat16)
+    value_ref[...] = qkv_ref[:, 2 * D : 3 * D].astype(jnp.bfloat16)
+    for first in range(0, D, SPAN):
+        span = slice(first, first + SPAN)
+        total_ref[...] = jnp.zeros_like(total_ref)
+
+        def head(h, carry, span=span):
+            lanes = head_lanes(h).astype(jnp.bfloat16)
+            attend = attended(query_ref[:, span] * lanes, key_ref[:, span])
+            total_ref[...] += matmul(attend.astype(jnp.bfloat16), value_ref[:, span] * lanes)
+            return carry
+
+        lax.fori_loop(0, SPAN // HDIM, head, 0)
+        mixed_ref[:, span] = total_ref[...].astype(jnp.bfloat16)
+
+
+def attend_back_kernel(
+    query_ref, key_ref, value_ref, grad_ref, cos_ref, sin_ref, out_ref, dq_ref, dk_ref, dv_ref
+):
+    for first in range(0, D, SPAN):
+        span = slice(first, first + SPAN)
+        for ref in (dq_ref, dk_ref, dv_ref):
+            ref[:, span] = jnp.zeros((ref.shape[0], SPAN), jnp.float32)
+
+        def head(h, carry, span=span):
+            lanes = head_lanes(h).astype(jnp.bfloat16)
+            queries, keys = query_ref[:, span] * lanes, key_ref[:, span] * lanes
+            grad = grad_ref[:, span] * lanes
+            attend = attended(queries, keys)
+            grad_attend = backmul(grad, value_ref[:, span])
+            grad_scores = (
+                attend * (grad_attend - jnp.sum(grad_attend * attend, axis=-1, keepdims=True))
+            ).astype(jnp.bfloat16)
+            dq_ref[:, span] += matmul(grad_scores, keys)
+            dk_ref[:, span] += tmatmul(grad_scores, queries)
+            dv_ref[:, span] += tmatmul(attend.astype(jnp.bfloat16), grad)
+            return carry
+
+        lax.fori_loop(0, SPAN // HDIM, head, 0)
+    cosine, sine = cos_ref[...], sin_ref[...]
+    out_ref[:, 0:D] = (turned(dq_ref[...], cosine, -sine) * HDIM ** (-0.5)).astype(jnp.bfloat16)
+    out_ref[:, D : 2 * D] = turned(dk_ref[...], cosine, -sine).astype(jnp.bfloat16)
+    out_ref[:, 2 * D : 3 * D] = dv_ref[...].astype(jnp.bfloat16)
+
+
+def flat_tables():
+    cosine, sine = (table[0, :, 0, :] for table in tables())
+    return (
+        jnp.tile(jnp.concatenate([cosine, cosine], axis=1), (1, HEADS)),
+        jnp.tile(jnp.concatenate([-sine, sine], axis=1), (1, HEADS)),
+    )
+
+
+def attend_call(kernel, operands, widths, scratch, name):
+    tokens = operands[0].shape[0]
+    return pl.pallas_call(
+        kernel,
+        out_shape=tuple(jax.ShapeDtypeStruct((tokens, width), jnp.bfloat16) for width in widths),
+        scratch_shapes=[pltpu.VMEM((tokens, width), jnp.float32) for width in scratch],
+        compiler_params=pltpu.CompilerParams(vmem_limit_bytes=VMEM_LIMIT),
+        name=name,
+    )(*operands)
 
 
 MATS = (
@@ -1258,33 +1345,21 @@
     slope = jnp.where(above > below, -level, jnp.where(above < below, 1.0 - level, 0.5 - level))
     square = jnp.sum(jnp.where(kind == 0, error * error * mask, 0.0), axis=1)
     quant = jnp.sum(jnp.where(kind == 0, 0.0, jnp.maximum(above, below) * mask), axis=1)
-    weight = jnp.repeat(jnp.sum(onehot * class_weight[None, :], axis=1), NPATCH)[:, None]
+    onehot = jnp.repeat(onehot, NPATCH, axis=0)
+    weight = jnp.sum(onehot * class_weight[None, :], axis=1, keepdims=True)
     grad = weight * mask * jnp.where(kind == 0, 2.0 * error, slope / NQ)
-    sums = [
-        jnp.sum(onehot * jnp.sum(part.reshape(-1, NPATCH), axis=1)[:, None], 0)
-        for part in (square, quant)
-    ]
-    return jnp.stack(sums), grad.astype(jnp.bfloat16)
-
-
-def layer_forward(state_zero, mats, parts, cosine, sine, causal):
+    sums = jnp.dot(jnp.stack([square, quant]), onehot, precision=lax.Precision.HIGHEST)
+    return sums, grad.astype(jnp.bfloat16)
+
+
+def layer_forward(state_zero, mats, parts, cosine, sine):
     w_qkv, w_out, w_up, w_down = (mats[2], mats[3], mats[4], mats[5])
     gain_one, gain_two = (parts[3], parts[4])
-    count_series = state_zero.shape[0] // NPATCH
     normed_one = rms_norm(state_zero, gain_one).astype(jnp.bfloat16)
-    qkv = matmul(normed_one, w_qkv).reshape(count_series, NPATCH, 3, HEADS, HDIM)
-    queries = (rotate(qkv[:, :, 0], cosine, sine) * HDIM ** (-0.5)).astype(jnp.bfloat16)
-    key_rot = rotate(qkv[:, :, 1], cosine, sine).astype(jnp.bfloat16)
-    value_all = qkv[:, :, 2].astype(jnp.bfloat16)
-    scores = jnp.einsum("sqhd,skhd->shqk", queries, key_rot, preferred_element_type=jnp.float32)
-    scores = jnp.where(causal, scores, -1e30)
-    peak = jnp.max(scores, axis=-1, keepdims=True)
-    expo = jnp.exp(scores - peak)
-    total = jnp.sum(expo, axis=-1, keepdims=True)
-    log_total = peak + jnp.log(total)
-    attend = (expo / total).astype(jnp.bfloat16)
-    mixed = jnp.einsum("shqk,skhd->sqhd", attend, value_all, preferred_element_type=jnp.float32)
-    mixed = mixed.astype(jnp.bfloat16).reshape(state_zero.shape[0], D)
+    qkv = matmul(normed_one, w_qkv)
+    queries, key_rot, value_all, mixed = attend_call(
+        attend_kernel, (qkv, cosine, sine), (D, D, D, D), (SPAN,), "attend"
+    )
     state_one = state_zero + matmul(mixed, w_out)
     normed_two = rms_norm(state_one, gain_two).astype(jnp.bfloat16)
     up_pre = matmul(normed_two, w_up)
@@ -1297,7 +1372,6 @@
             queries,
             key_rot,
             value_all,
-            log_total,
             mixed,
             state_one,
             normed_two,
@@ -1307,13 +1381,12 @@
     )
 
 
-def layer_backward(grad_two, state_zero, kept, mats, parts, cosine, sine, causal):
+def layer_backward(grad_two, state_zero, kept, mats, parts, cosine, sine):
     (
         normed_one,
         queries,
         key_rot,
         value_all,
-        log_total,
         mixed,
         state_one,
         normed_two,
@@ -1322,8 +1395,6 @@
     ) = kept
     w_qkv, w_out, w_up, w_down = (mats[2], mats[3], mats[4], mats[5])
     gain_one, gain_two = (parts[3], parts[4])
-    tokens = state_zero.shape[0]
-    count_series = tokens // NPATCH
     grad_mlp = grad_two.astype(jnp.bfloat16)
     grad_act = backmul(grad_mlp, w_down)
     grad_up_pre = (grad_act * silu_slope(up_pre)).astype(jnp.bfloat16)
@@ -1332,38 +1403,14 @@
     grad_norm_in, grad_gain_two = pull(grad_normed)
     grad_one = grad_two + grad_norm_in
     grad_proj = grad_one.astype(jnp.bfloat16)
-    grad_mixed = (
-        backmul(grad_proj, w_out).astype(jnp.bfloat16).reshape(count_series, NPATCH, HEADS, HDIM)
-    )
-    scores = jnp.einsum("sqhd,skhd->shqk", queries, key_rot, preferred_element_type=jnp.float32)
-    attend = jnp.where(causal, jnp.exp(scores - log_total), 0.0)
-    grad_attend = jnp.einsum(
-        "sqhd,skhd->shqk", grad_mixed, value_all, preferred_element_type=jnp.float32
-    )
-    grad_scores = (
-        attend * (grad_attend - jnp.sum(grad_attend * attend, axis=-1, keepdims=True))
-    ).astype(jnp.bfloat16)
-    grad_query = jnp.einsum(
-        "shqk,skhd->sqhd", grad_scores, key_rot, preferred_element_type=jnp.float32
-    )
-    grad_key = jnp.einsum(
-        "shqk,sqhd->skhd", grad_scores, queries, preferred_element_type=jnp.float32
-    )
-    grad_value = jnp.einsum(
-        "shqk,sqhd->skhd",
-        attend.astype(jnp.bfloat16),
-        grad_mixed,
-        preferred_element_type=jnp.float32,
-    )
-    grad_qkv = jnp.stack(
-        [
-            rotate(grad_query, cosine, -sine) * HDIM ** (-0.5),
-            rotate(grad_key, cosine, -sine),
-            grad_value,
-        ],
-        axis=2,
-    )
-    grad_qkv = grad_qkv.reshape(tokens, 3 * D).astype(jnp.bfloat16)
+    grad_mixed = backmul(grad_proj, w_out).astype(jnp.bfloat16)
+    (grad_qkv,) = attend_call(
+        attend_back_kernel,
+        (queries, key_rot, value_all, grad_mixed, cosine, sine),
+        (3 * D,),
+        (D, D, D),
+        "attend_back",
+    )
     grad_normed_one = backmul(grad_qkv, w_qkv)
     _, pull = jax.vjp(rms_norm, state_zero, gain_one)
     grad_zero_in, grad_gain_one = pull(grad_normed_one)
@@ -1427,14 +1474,13 @@
     mats = unpack(gathered, owner)
     tok_in, tok_out, head_in, head_out = (mats[0], mats[1], mats[6], mats[7])
     class_weight = 1.0 / (counts * NCLASS)
-    cosine, sine = tables()
-    causal = jnp.arange(NPATCH)[:, None] >= jnp.arange(NPATCH)[None, :]
+    cosine, sine = flat_tables()
     patch_in = feat.reshape(tokens, 2 * PATCH).astype(jnp.bfloat16)
     tok_pre = matmul(patch_in, tok_in)
     hidden = silu(tok_pre[:, :D] + bias_one).astype(jnp.bfloat16)
     class_rows = jnp.repeat(jnp.dot(onehot, freq, precision=lax.Precision.HIGHEST), NPATCH, axis=0)
     state_zero = matmul(hidden, tok_out) + bias_two + tok_pre[:, D:] + class_rows
-    state_two, _ = layer_forward(state_zero, mats, parts, cosine, sine, causal)
+    state_two, kept = layer_forward(state_zero, mats, parts, cosine, sine)
     state_low = state_two.astype(jnp.bfloat16)
     head_pre = matmul(state_low, head_in)
     head_hidden = silu(head_pre[:, :D] + head_bias).astype(jnp.bfloat16)
@@ -1448,9 +1494,8 @@
         jnp.bfloat16
     )
     grad_two = backmul(grad_head_pre, head_in)
-    _, kept = layer_forward(state_zero, mats, parts, cosine, sine, causal)
     grad_zero, layer_pairs, grad_gain_one, grad_gain_two = layer_backward(
-        grad_two, state_zero, kept, mats, parts, cosine, sine, causal
+        grad_two, state_zero, kept, mats, parts, cosine, sine
     )
     grad_prod = grad_zero.astype(jnp.bfloat16)
     grad_first = backmul(grad_prod, tok_out) * silu_slope(tok_pre[:, :D] + bias_one)

time: 995 us -> 971 us (0.976)
  Pallas kernels: 794 us -> 835 us
  local copies, waits for them, and re-layouts: 53.4 us -> 14.1 us
  other arithmetic: 49.6 us -> 32.8 us
    pallas_call x0 -> x2, Pallas kernels: none -> 40.9 us  [attend_call(): pl.pallas_call(kernel, out_shape=tuple((jax.ShapeDtypeStruct((tokens, wid...]
    reshape x5 -> x1, local copies, waits for them, and re-layouts: 17.1 us -> 0.09 us  [loss_parts(): onehot = jnp.repeat(onehot, NPATCH, axis=0)]
where the time goes in v8:
time: 971 us; the launch traced here: 962 us
  Pallas kernels  835 us (86%)
  matrix products  75.5 us (8%)
  other arithmetic  32.8 us (3%)
  local copies, waits for them, and re-layouts  14.1 us (1%)
    pallas_call x1, Pallas kernels, scatter_sum(): pl.pallas_call(scatter_kernel, out_shape=(jax.ShapeDtypeStruct((slot_coun...  380 us
    pallas_call x1, Pallas kernels, gather_all(): pl.pallas_call(gather_kernel, out_shape=(jax.ShapeDtypeStruct((4, 2, narr...  336 us
    pallas_call x1, Pallas kernels, grad_blocks(): pl.pallas_call(grad_kernel, out_shape=jax.ShapeDtypeStruct((TOTAL_SLOTS,...  41.6 us
    pallas_call x2, Pallas kernels, attend_call(): pl.pallas_call(kernel, out_shape=tuple((jax.ShapeDtypeStruct((tokens, wid...  40.9 us
    dot_general x7, matrix products, backmul(): lax.dot_general(left, right, (((1,), (1,)), ((), ())), preferred_element_...  40.2 us
    pallas_call x1, Pallas kernels, unpack(): pl.pallas_call(unpack_kernel, out_shape=tuple((jax.ShapeDtypeStruct((tota...  35.7 us
    dot_general x9, matrix products, matmul(): return jnp.dot(left, right, preferred_element_type=jnp.float32)  33 us

profile of v8, /device:TPU:0, one launch (start us, length us, event | category | flops | bytes accessed | tf_op | source)
XLA Modules:
  0.0 961.8 jit_solution(18151949523917436645)
XLA Ops:
  0.6 0.8 subtract_convert_fusion
  1.8 0.8 select_reduce_fusion.2
  2.6 0.6 scatter.4.count_ref
  3.2 4.3 convert_element_type.112.own_ref
  7.5 336.2 %gather_all.1 = (bf16[4,2,4,16,64,1280]{5,4,3,2,1,0:T(8,128)(2,1)}, f32[32,8,128]{2,1,0:T(8,128)}) custom-call(bf16[16,64,1280]{2,1,0:T(8,128)(2,1)} %convert_element_type.112.own_ref, f32[8,128]{1,0:T(8,128)} %scatter.4.count_ref), custom_call_target="tpu_custom_call" | custom-call | tf_op jit(solution)/shard_map/gather_all/pallas_call | solution.py:1266
  343.7 35.7 %unpack.1 = (bf16[64,2560]{1,0:T(8,128)(2,1)}, bf16[1280,1280]{1,0:T(8,128)(2,1)}, bf16[1280,3840]{1,0:T(8,128)(2,1)}, bf16[1280,1280]{1,0:T(8,128)(2,1)}, bf16[...) custom-call(s32[322]{0:T(512)} %owner_ref.3, ...), custom_call_target="tpu_custom_call" | custom-call | bytes 105512960 | tf_op jit(solution)/shard_map/unpack/pallas_call | solution.py:268
  379.8 1.5 fusion.50
  381.3 1.4 copy-done
  382.8 0.4 divide_convert_fusion.2.refs_1_
  383.6 3.6 multiply_reduce_fusion.5
  387.4 1.5 copy-done.27
  389.0 4.6 fusion.51.qkv_ref
  393.8 0.7 tile.21.sin_ref
  394.6 0.7 tile.9.cos_ref
  395.3 19.0 %attend.1 = (bf16[256,1280]{1,0:T(8,128)(2,1)}, bf16[256,1280]{1,0:T(8,128)(2,1)}, bf16[256,1280]{1,0:T(8,128)(2,1)}, bf16[256,1280]{1,0:T(8,128)(2,1)}) custom-call(f32[256,3840]{1,0:T(8,128)} %fusion.51.qkv_ref, f32[16,1280]{1,0:T(8,128)} %tile.9.cos_ref, f32[16,1280]{1,0:T(8,128)} %tile.21.sin_ref), custom_call_target="tpu_custom_call" | custom-call | tf_op jit(solution)/shard_map/attend/pallas_call | solution.py:157
  414.3 2.2 multiply_reduce_fusion.4
  416.7 11.0 %divide_convert_fusion = (bf16[256,5120]{1,0:T(8,128)(2,1)S(1)}, f32[256,5120]{1,0:T(8,128)}) fusion(bf16[256,1280]{1,0:T(8,128)(2,1)S(1)} %multiply_convert_fusion.1.refs_4_, bf16[1280,5120]{1,0:T(8,128)(2,1)} %get-tuple-element.44), kind=kOutput, calls=%fused_computation.6 | convolution fusion | flops 3360686080 | bytes 21626880 | tf_op jit(solution)/shard_map/dot_general | solution.py:35
  427.8 3.7 fusion.5.refs_6_
  431.5 1.9 fusion.52
  433.4 0.4 divide_convert_fusion.1.refs_7_
  433.8 1.1 copy-done.18
  435.2 2.1 fusion.3
  437.6 1.1 copy-done.13
  438.7 1.8 convolution_subtract_fusion
  440.5 1.0 slice_reduce_fusion.4
  441.9 2.5 select_reduce_fusion.1
  444.7 3.4 fusion.44
  448.2 6.3 fusion.49
  454.5 11.8 %fusion.refs_12_ = bf16[256,5120]{1,0:T(8,128)(2,1)} fusion(bf16[256,1280]{1,0:T(8,128)(2,1)} %get-tuple-element.108.refs_13_, bf16[5120,1280]{1,0:T(8,128)(2,1)} %get-tuple-element.45, f32[256,5120]{1,0:T(8,128)} %get-tuple-element.106), kind=kOutput, calls=%fused_computation.3 | convolution fusion | flops 3367239680 | bytes 21626880 | tf_op jit(solution)/shard_map/dot_general | solution.py:45
  466.3 8.4 multiply_reduce_fusion
  475.1 1.8 copy-done.6
  476.9 1.9 convolution_convert_fusion.grad_ref
  478.8 21.9 %attend_back.1.refs_10_ = bf16[256,3840]{1,0:T(8,128)(2,1)} custom-call(bf16[256,1280]{1,0:T(8,128)(2,1)} %get-tuple-element.49.query_ref, bf16[256,1280]{1,0:T(8,128)(2,1)} %get-tuple-element.50.key_ref, bf16[256,1280]{1,0:T(8,128)(2,1)} %get-tuple-element.51.value_ref, bf16[256,1280]{1,0:T(8,128)(2,1)} %convolution_convert_fusion.grad_ref, ...), custom_call_target="tpu_custom_call" | custom-call | tf_op jit(solution)/shard_map/attend_back/pallas_call | solution.py:157
  500.7 7.2 multiply_reduce_fusion.1
  508.5 1.3 copy-done.1
  509.7 1.0 copy-done.4
  510.7 1.2 fusion.45
  512.4 0.7 pad_bitcast_fusion.small_ref
  513.0 1.1 pad_maximum_fusion.refs_14_
  514.2 1.1 pad_maximum_fusion.1.refs_8_
  515.3 41.6 %grad_blocks.1 = bf16[512,64,1280]{2,1,0:T(8,128)(2,1)} custom-call(s32[322]{0:T(512)} %owner_ref.3, bf16[256,64]{1,0:T(8,128)(2,1)} %copy-done.19, bf16[256,1280]{1,0:T(8,128)(2,1)} %copy-done.2, bf16[256,1280]{1,0:T(8,128)(2,1)} %copy-done.7, bf16[256,1280]{1,0:T(8,128)(2,1)} %get-tuple-element.42.refs_3_, bf16[256,1280]{1,0:T(8,128)(2,1)} %copy-done.8, ...), custom_call_target="tpu_custom_call" | custom-call | flops 13505658880 | bytes 52756480 | tf_op jit(solution)/shard_map/grad_blocks/pallas_call | solution.py:363
  557.2 0.7 broadcast_in_dim.105.filled_ref
  557.9 380.1 %scatter_sum.1 = (f32[16,64,1280]{2,1,0:T(8,128)}, f32[32,8,128]{2,1,0:T(8,128)}, f32[32,8,128]{2,1,0:T(8,128)}) custom-call(bf16[4,2,4,16,64,1280]{5,4,3,2,1,0:T(8,128)(2,1)} %bitcast.5.slots_ref, f32[32,8,128]{2,1,0:T(8,128)} %pad_bitcast_fusion.small_ref, f32[16,8,128]{2,1,0:T(8,128)} %broadcast_in_dim.105.filled_ref), custom_call_target="tpu_custom_call" | custom-call | tf_op jit(solution)/shard_map/scatter_sum/pallas_call | solution.py:899
  938.0 1.4 multiply_reduce_fusion.6
  939.4 1.5 reduce_sum.252
  943.0 1.5 multiply_subtract_fusion.1
  944.5 14.5 %fusion.38 = (bf16[16,64,1280]{2,1,0:T(8,128)(2,1)}, f32[16,64,1280]{2,1,0:T(8,128)}, f32[16,64,1280]{2,1,0:T(8,128)}, f32[16,64,1280]{2,1,0:T(8,128)}) fusion(f32[16,64,1280]{2,1,0:T(8,128)} %param.18, f32[]{:T(128)} %bitcast.11, f32[16,64,1280]{2,1,0:T(8,128)} %get-tuple-element.54, f32[]{:T(128)S(6)} %min.3, f32[16,64,1280]{2,1,0:T(8,128)} %param.20, ...), kind=kLoop, calls=%fused_computation.125 | loop fusion | flops 20971520 | bytes 39321608 | tf_op jit(solution)/shard_map/convert_element_type | solution.py:1545
  959.0 1.4 fusion.34
  (126 shorter events, 4.5 us)
Async XLA Ops:
  343.6 35.8 %copy-start.22 = (f32[16,640]{1,0:T(8,128)S(1)}, f32[16,640]{1,0:T(8,128)}, u32[]{:S(2)}) copy-start(f32[16,640]{1,0:T(8,128)} %param.13) | copy-start | bytes 122884
  343.7 35.9 %copy-start.21 = (s32[16,640]{1,0:T(8,128)S(1)}, s32[16,640]{1,0:T(8,128)}, u32[]{:S(2)}) copy-start(s32[16,640]{1,0:T(8,128)} %param.14) | copy-start | bytes 122884
  379.8 1.5 copy-start.19
  379.8 1.5 copy-start.20
  381.3 1.5 copy-start
  381.3 1.9 slice-start
  381.3 1.9 copy-start.26
  383.2 4.0 copy-start.2
  383.6 5.4 copy-start.27
  387.4 6.2 copy-start.7
  395.3 19.0 %copy-start.5 = (bf16[1280,1280]{1,0:T(8,128)(2,1)S(1)}, bf16[1280,1280]{1,0:T(8,128)(2,1)}, u32[]{:S(2)}) copy-start(bf16[1280,1280]{1,0:T(8,128)(2,1)} %get-tuple-element.43) | copy-start | bytes 9830404
  416.5 11.2 %slice-start.1 = ((s8[13107200]{0:T(1024)(128)(4,1)}), s8[4194304]{0:T(1024)(128)(4,1)S(1)}, s32[]{:S(2)}) async-start(s8[13107200]{0:T(1024)(128)(4,1)} %bitcast.59), calls=%async_computation.1 | async-start | bytes 8388608
  416.5 15.0 %slice-start.5 = ((s8[6553600]{0:T(1024)(128)(4,1)}), s8[4194304]{0:T(1024)(128)(4,1)S(1)}, s32[]{:S(2)}) async-start(s8[6553600]{0:T(1024)(128)(4,1)} %bitcast.61), calls=%async_computation.5 | async-start | bytes 8388608
  416.7 11.0 %copy-start.8 = (bf16[256,1280]{1,0:T(8,128)(2,1)}, bf16[256,1280]{1,0:T(8,128)(2,1)S(1)}, u32[]{:S(2)}) copy-start(bf16[256,1280]{1,0:T(8,128)(2,1)S(1)} %multiply_convert_fusion.1.refs_4_) | copy-start | bytes 1966084
  416.7 11.0 %slice-start.2 = ((s8[13107200]{0:T(1024)(128)(4,1)}), s8[4194304]{0:T(1024)(128)(4,1)S(1)}, s32[]{:S(2)}) async-start(s8[13107200]{0:T(1024)(128)(4,1)} %bitcast.59), calls=%async_computation.2 | async-start | bytes 8388608
  416.7 11.0 %slice-start.3 = ((s8[13107200]{0:T(1024)(128)(4,1)}), s8[4194304]{0:T(1024)(128)(4,1)S(1)}, s32[]{:S(2)}) async-start(s8[13107200]{0:T(1024)(128)(4,1)} %bitcast.59), calls=%async_computation.3 | async-start | bytes 8388608
  416.7 11.0 %slice-start.4 = ((s8[13107200]{0:T(1024)(128)(4,1)}), s8[524288]{0:T(1024)(128)(4,1)S(1)}, s32[]{:S(2)}) async-start(s8[13107200]{0:T(1024)(128)(4,1)} %bitcast.59), calls=%async_computation.4 | async-start | bytes 1048576
  416.7 14.7 %slice-start.6 = ((s8[6553600]{0:T(1024)(128)(4,1)}), s8[2359296]{0:T(1024)(128)(4,1)S(1)}, s32[]{:S(2)}) async-start(s8[6553600]{0:T(1024)(128)(4,1)} %bitcast.61), calls=%async_computation.6 | async-start | bytes 4718592
  427.7 3.7 copy-start.12
  431.5 1.9 copy-start.15
  431.5 3.7 copy-start.28
  433.4 1.5 copy-start.18
  433.8 1.3 copy-start.10
  437.4 1.3 copy-start.13
  444.3 68.7 %copy-start.9 = (bf16[256,1280]{1,0:T(8,128)(2,1)}, bf16[256,1280]{1,0:T(8,128)(2,1)S(1)}, u32[]{:S(2)}) copy-start(bf16[256,1280]{1,0:T(8,128)(2,1)S(1)} %get-tuple-element.79.refs_15_) | copy-start | bytes 1966084
  448.2 6.3 copy-start.16
  466.3 8.4 copy-start.14
  474.7 2.2 copy-start.6
  475.1 3.7 copy-start.11
  508.0 1.7 copy-start.1
  508.0 2.7 copy-start.4
  510.7 3.5 copy-start.3
  511.9 1.2 copy-start.17
  515.3 41.7 %copy-start.25 = (s32[322]{0:T(512)S(1)}, s32[322]{0:T(512)}, u32[]{:S(2)}) copy-start(s32[322]{0:T(512)} %owner_ref.3) | copy-start | bytes 3868
  557.9 385.1 %copy-start.23 = (f32[11520]{0:T(1024)S(1)}, f32[11520]{0:T(1024)}, u32[]{:S(2)}) copy-start(f32[11520]{0:T(1024)} %param.23) | copy-start | bytes 138244
  557.9 385.1 %copy-start.24 = (f32[11520]{0:T(1024)S(1)}, f32[11520]{0:T(1024)}, u32[]{:S(2)}) copy-start(f32[11520]{0:T(1024)} %param.22) | copy-start | bytes 138244

commit v9 on v8

--- a/solution.py
+++ b/solution.py
@@ -67,7 +67,8 @@
     return (jnp.cos(angle)[None, :, None, :], jnp.sin(angle)[None, :, None, :])
 
 
-SPAN = 640
+SPAN = 2 * 128
+ROWS_TOGETHER = 256
 
 
 def turned(value, cosine, sine):
@@ -87,13 +88,22 @@
     seen = jnp.logical_and(column <= row, column >= row - lax.rem(row, NPATCH))
     scores = jnp.where(seen, scores, -1e30)
     expo = jnp.exp(scores - jnp.max(scores, axis=-1, keepdims=True))
-    return expo / jnp.sum(expo, axis=-1, keepdims=True)
+    return expo * (1.0 / jnp.sum(expo, axis=-1, keepdims=True))
+
+
+def parts_of(ref):
+    step = min(ROWS_TOGETHER, ref.shape[0])
+    return [slice(at, at + step) for at in range(0, ref.shape[0], step)]
 
 
 def head_lanes(h):
-    lane = lax.broadcasted_iota(jnp.int32, (1, SPAN), 1)
+    start = jnp.minimum(lax.div(h * HDIM, LANES) * LANES, D - SPAN)
+    lane = start + lax.broadcasted_iota(jnp.int32, (1, SPAN), 1)
     inside = jnp.logical_and(lane >= h * HDIM, lane < (h + 1) * HDIM)
-    return jnp.where(inside, 1.0, 0.0)
+    return (
+        pl.ds(pl.multiple_of(start, LANES), SPAN),
+        jnp.where(inside, 1.0, 0.0).astype(jnp.bfloat16),
+    )
 
 
 def attend_kernel(qkv_ref, cos_ref, sin_ref, query_ref, key_ref, value_ref, mixed_ref, total_ref):
@@ -101,43 +111,43 @@
     query_ref[...] = (turned(qkv_ref[:, 0:D], cosine, sine) * HDIM ** (-0.5)).astype(jnp.bfloat16)
     key_ref[...] = turned(qkv_ref[:, D : 2 * D], cosine, sine).astype(jnp.bfloat16)
     value_ref[...] = qkv_ref[:, 2 * D : 3 * D].astype(jnp.bfloat16)
-    for first in range(0, D, SPAN):
-        span = slice(first, first + SPAN)
-        total_ref[...] = jnp.zeros_like(total_ref)
-
-        def head(h, carry, span=span):
-            lanes = head_lanes(h).astype(jnp.bfloat16)
-            attend = attended(query_ref[:, span] * lanes, key_ref[:, span])
-            total_ref[...] += matmul(attend.astype(jnp.bfloat16), value_ref[:, span] * lanes)
-            return carry
-
-        lax.fori_loop(0, SPAN // HDIM, head, 0)
-        mixed_ref[:, span] = total_ref[...].astype(jnp.bfloat16)
+    total_ref[...] = jnp.zeros_like(total_ref)
+
+    def head(h, carry):
+        span, lanes = head_lanes(h)
+        for rows in parts_of(query_ref):
+            attend = attended(query_ref[rows, span] * lanes, key_ref[rows, span])
+            total_ref[rows, span] += matmul(
+                attend.astype(jnp.bfloat16), value_ref[rows, span] * lanes
+            )
+        return carry
+
+    lax.fori_loop(0, HEADS, head, 0, unroll=8)
+    mixed_ref[...] = total_ref[...].astype(jnp.bfloat16)
 
 
 def attend_back_kernel(
     query_ref, key_ref, value_ref, grad_ref, cos_ref, sin_ref, out_ref, dq_ref, dk_ref, dv_ref
 ):
-    for first in range(0, D, SPAN):
-        span = slice(first, first + SPAN)
-        for ref in (dq_ref, dk_ref, dv_ref):
-            ref[:, span] = jnp.zeros((ref.shape[0], SPAN), jnp.float32)
-
-        def head(h, carry, span=span):
-            lanes = head_lanes(h).astype(jnp.bfloat16)
-            queries, keys = query_ref[:, span] * lanes, key_ref[:, span] * lanes
-            grad = grad_ref[:, span] * lanes
+    for ref in (dq_ref, dk_ref, dv_ref):
+        ref[...] = jnp.zeros_like(ref)
+
+    def head(h, carry):
+        span, lanes = head_lanes(h)
+        for rows in parts_of(query_ref):
+            queries, keys = query_ref[rows, span] * lanes, key_ref[rows, span] * lanes
+            grad = grad_ref[rows, span] * lanes
             attend = attended(queries, keys)
-            grad_attend = backmul(grad, value_ref[:, span])
+            grad_attend = backmul(grad, value_ref[rows, span])
             grad_scores = (
                 attend * (grad_attend - jnp.sum(grad_attend * attend, axis=-1, keepdims=True))
             ).astype(jnp.bfloat16)
-            dq_ref[:, span] += matmul(grad_scores, keys)
-            dk_ref[:, span] += tmatmul(grad_scores, queries)
-            dv_ref[:, span] += tmatmul(attend.astype(jnp.bfloat16), grad)
-            return carry
-
-        lax.fori_loop(0, SPAN // HDIM, head, 0)
+            dq_ref[rows, span] += matmul(grad_scores, keys)
+            dk_ref[rows, span] += tmatmul(grad_scores, queries)
+            dv_ref[rows, span] += tmatmul(attend.astype(jnp.bfloat16), grad)
+        return carry
+
+    lax.fori_loop(0, HEADS, head, 0, unroll=8)
     cosine, sine = cos_ref[...], sin_ref[...]
     out_ref[:, 0:D] = (turned(dq_ref[...], cosine, -sine) * HDIM ** (-0.5)).astype(jnp.bfloat16)
     out_ref[:, D : 2 * D] = turned(dk_ref[...], cosine, -sine).astype(jnp.bfloat16)
@@ -165,13 +175,13 @@
 
 MATS = (
     (2 * PATCH, 2, 2),
-    (D, 1, 4),
+    (D, 1, 10),
     (D, 3, 6),
-    (D, 1, 4),
+    (D, 1, 10),
     (D, FF // D, 8),
     (FF, 1, 8),
     (D, (D + OUTW) // D, 8),
-    (D, 1, 4),
+    (D, 1, 10),
 )
 BASES = tuple(sum(r * g for r, g, _ in MATS[:i]) // BR for i in range(len(MATS)))
 LANES = 128
@@ -372,7 +382,7 @@
         + [
             pltpu.VMEM((D // LANES, 8 * BR, LANES), jnp.float32),
             dma((len(MATS), 2)),
-            dma((len(MATS), 2, 8)),
+            dma((len(MATS), 2, 10)),
         ],
         compiler_params=pltpu.CompilerParams(vmem_limit_bytes=VMEM_LIMIT),
         cost_estimate=pl.CostEstimate(
@@ -1358,7 +1368,7 @@
     normed_one = rms_norm(state_zero, gain_one).astype(jnp.bfloat16)
     qkv = matmul(normed_one, w_qkv)
     queries, key_rot, value_all, mixed = attend_call(
-        attend_kernel, (qkv, cosine, sine), (D, D, D, D), (SPAN,), "attend"
+        attend_kernel, (qkv, cosine, sine), (D, D, D, D), (D,), "attend"
     )
     state_one = state_zero + matmul(mixed, w_out)
     normed_two = rms_norm(state_one, gain_two).astype(jnp.bfloat16)

time: 971 us -> 950 us (0.978)
  Pallas kernels: 835 us -> 813 us
    pallas_call x2, Pallas kernels: 40.9 us -> 22.9 us  [attend_call(): pl.pallas_call(kernel, out_shape=tuple((jax.ShapeDtypeStruct((tokens, wid...]
where the time goes in v9:
time: 950 us; the launch traced here: 940 us
  Pallas kernels  813 us (86%)
  matrix products  75.5 us (8%)
  other arithmetic  32.8 us (3%)
  local copies, waits for them, and re-layouts  14 us (1%)
    pallas_call x1, Pallas kernels, scatter_sum(): pl.pallas_call(scatter_kernel, out_shape=(jax.ShapeDtypeStruct((slot_coun...  380 us
    pallas_call x1, Pallas kernels, gather_all(): pl.pallas_call(gather_kernel, out_shape=(jax.ShapeDtypeStruct((4, 2, narr...  336 us
    dot_general x7, matrix products, backmul(): lax.dot_general(left, right, (((1,), (1,)), ((), ())), preferred_element_...  40.2 us
    pallas_call x1, Pallas kernels, grad_blocks(): pl.pallas_call(grad_kernel, out_shape=jax.ShapeDtypeStruct((TOTAL_SLOTS,...  37.6 us
    pallas_call x1, Pallas kernels, unpack(): pl.pallas_call(unpack_kernel, out_shape=tuple((jax.ShapeDtypeStruct((tota...  36 us
    dot_general x9, matrix products, matmul(): return jnp.dot(left, right, preferred_element_type=jnp.float32)  33 us
    pallas_call x2, Pallas kernels, attend_call(): pl.pallas_call(kernel, out_shape=tuple((jax.ShapeDtypeStruct((tokens, wid...  22.9 us

profile of v9, /device:TPU:0, one launch (start us, length us, event | category | flops | bytes accessed | tf_op | source)
XLA Modules:
  0.0 940.2 jit_solution(18058872438967577151)
XLA Ops:
  0.6 0.8 subtract_convert_fusion
  1.8 0.8 select_reduce_fusion.2
  2.6 0.6 scatter.4.count_ref
  3.2 4.3 convert_element_type.112.own_ref
  7.5 336.2 %gather_all.1 = (bf16[4,2,4,16,64,1280]{5,4,3,2,1,0:T(8,128)(2,1)}, f32[32,8,128]{2,1,0:T(8,128)}) custom-call(bf16[16,64,1280]{2,1,0:T(8,128)(2,1)} %convert_element_type.112.own_ref, f32[8,128]{1,0:T(8,128)} %scatter.4.count_ref), custom_call_target="tpu_custom_call" | custom-call | tf_op jit(solution)/shard_map/gather_all/pallas_call | solution.py:1276
  343.7 36.0 %unpack.1 = (bf16[64,2560]{1,0:T(8,128)(2,1)}, bf16[1280,1280]{1,0:T(8,128)(2,1)}, bf16[1280,3840]{1,0:T(8,128)(2,1)}, bf16[1280,1280]{1,0:T(8,128)(2,1)}, bf16[...) custom-call(s32[322]{0:T(512)} %owner_ref.3, ...), custom_call_target="tpu_custom_call" | custom-call | bytes 105512960 | tf_op jit(solution)/shard_map/unpack/pallas_call | solution.py:278
  380.0 1.5 fusion.50
  381.6 1.4 copy-done
  383.0 0.4 divide_convert_fusion.2.refs_1_
  383.8 3.6 multiply_reduce_fusion.5
  387.7 1.5 copy-done.27
  389.2 4.6 fusion.51.qkv_ref
  394.0 0.7 tile.21.sin_ref
  394.8 0.7 tile.9.cos_ref
  395.5 8.5 attend.1
  404.0 2.2 multiply_reduce_fusion.4
  406.5 11.0 %divide_convert_fusion = (bf16[256,5120]{1,0:T(8,128)(2,1)S(1)}, f32[256,5120]{1,0:T(8,128)}) fusion(bf16[256,1280]{1,0:T(8,128)(2,1)S(1)} %multiply_convert_fusion.1.refs_4_, bf16[1280,5120]{1,0:T(8,128)(2,1)} %get-tuple-element.44), kind=kOutput, calls=%fused_computation.6 | convolution fusion | flops 3360686080 | bytes 21626880 | tf_op jit(solution)/shard_map/dot_general | solution.py:35
  417.5 3.7 fusion.5.refs_6_
  421.2 1.9 fusion.52
  423.1 0.4 divide_convert_fusion.1.refs_7_
  423.5 1.1 copy-done.18
  424.9 2.1 fusion.3
  427.4 1.1 copy-done.13
  428.4 1.8 convolution_subtract_fusion
  430.2 1.0 slice_reduce_fusion.4
  431.6 2.5 select_reduce_fusion.1
  434.4 3.4 fusion.44
  437.9 6.3 fusion.49
  444.2 11.8 %fusion.refs_12_ = bf16[256,5120]{1,0:T(8,128)(2,1)} fusion(bf16[256,1280]{1,0:T(8,128)(2,1)} %get-tuple-element.108.refs_13_, bf16[5120,1280]{1,0:T(8,128)(2,1)} %get-tuple-element.45, f32[256,5120]{1,0:T(8,128)} %get-tuple-element.106), kind=kOutput, calls=%fused_computation.3 | convolution fusion | flops 3367239680 | bytes 21626880 | tf_op jit(solution)/shard_map/dot_general | solution.py:45
  456.0 8.4 multiply_reduce_fusion
  464.8 1.8 copy-done.6
  466.6 1.9 convolution_convert_fusion.grad_ref
  468.5 14.5 %attend_back.1.refs_10_ = bf16[256,3840]{1,0:T(8,128)(2,1)} custom-call(bf16[256,1280]{1,0:T(8,128)(2,1)} %get-tuple-element.49.query_ref, bf16[256,1280]{1,0:T(8,128)(2,1)} %get-tuple-element.50.key_ref, bf16[256,1280]{1,0:T(8,128)(2,1)} %get-tuple-element.51.value_ref, bf16[256,1280]{1,0:T(8,128)(2,1)} %convolution_convert_fusion.grad_ref, ...), custom_call_target="tpu_custom_call" | custom-call | tf_op jit(solution)/shard_map/attend_back/pallas_call | solution.py:167
  483.0 7.2 multiply_reduce_fusion.1
  490.7 1.3 copy-done.1
  492.0 1.0 copy-done.4
  493.0 1.2 fusion.45
  494.6 0.7 pad_bitcast_fusion.small_ref
  495.3 1.1 pad_maximum_fusion.refs_14_
  496.4 1.1 pad_maximum_fusion.1.refs_8_
  497.6 37.6 %grad_blocks.1 = bf16[512,64,1280]{2,1,0:T(8,128)(2,1)} custom-call(s32[322]{0:T(512)} %owner_ref.3, bf16[256,64]{1,0:T(8,128)(2,1)} %copy-done.19, bf16[256,1280]{1,0:T(8,128)(2,1)} %copy-done.2, bf16[256,1280]{1,0:T(8,128)(2,1)} %copy-done.7, bf16[256,1280]{1,0:T(8,128)(2,1)} %get-tuple-element.42.refs_3_, bf16[256,1280]{1,0:T(8,128)(2,1)} %copy-done.8, ...), custom_call_target="tpu_custom_call" | custom-call | flops 13505658880 | bytes 52756480 | tf_op jit(solution)/shard_map/grad_blocks/pallas_call | solution.py:373
  535.4 0.7 broadcast_in_dim.105.filled_ref
  536.1 380.1 %scatter_sum.1 = (f32[16,64,1280]{2,1,0:T(8,128)}, f32[32,8,128]{2,1,0:T(8,128)}, f32[32,8,128]{2,1,0:T(8,128)}) custom-call(bf16[4,2,4,16,64,1280]{5,4,3,2,1,0:T(8,128)(2,1)} %bitcast.5.slots_ref, f32[32,8,128]{2,1,0:T(8,128)} %pad_bitcast_fusion.small_ref, f32[16,8,128]{2,1,0:T(8,128)} %broadcast_in_dim.105.filled_ref), custom_call_target="tpu_custom_call" | custom-call | tf_op jit(solution)/shard_map/scatter_sum/pallas_call | solution.py:909
  916.2 1.4 multiply_reduce_fusion.6
  917.6 1.5 reduce_sum.252
  921.2 1.5 multiply_subtract_fusion.1
  922.7 14.5 %fusion.38 = (bf16[16,64,1280]{2,1,0:T(8,128)(2,1)}, f32[16,64,1280]{2,1,0:T(8,128)}, f32[16,64,1280]{2,1,0:T(8,128)}, f32[16,64,1280]{2,1,0:T(8,128)}) fusion(f32[16,64,1280]{2,1,0:T(8,128)} %param.18, f32[]{:T(128)} %bitcast.11, f32[16,64,1280]{2,1,0:T(8,128)} %get-tuple-element.54, f32[]{:T(128)S(6)} %min.3, f32[16,64,1280]{2,1,0:T(8,128)} %param.20, ...), kind=kLoop, calls=%fused_computation.125 | loop fusion | flops 20971520 | bytes 39321608 | tf_op jit(solution)/shard_map/convert_element_type | solution.py:1555
  937.2 1.4 fusion.34
  (126 shorter events, 4.5 us)
Async XLA Ops:
  343.6 36.0 %copy-start.22 = (f32[16,640]{1,0:T(8,128)S(1)}, f32[16,640]{1,0:T(8,128)}, u32[]{:S(2)}) copy-start(f32[16,640]{1,0:T(8,128)} %param.13) | copy-start | bytes 122884
  343.7 36.1 %copy-start.21 = (s32[16,640]{1,0:T(8,128)S(1)}, s32[16,640]{1,0:T(8,128)}, u32[]{:S(2)}) copy-start(s32[16,640]{1,0:T(8,128)} %param.14) | copy-start | bytes 122884
  380.0 1.5 copy-start.19
  380.0 1.5 copy-start.20
  381.5 1.5 copy-start
  381.6 1.9 slice-start
  381.6 1.9 copy-start.26
  383.4 4.0 copy-start.2
  383.8 5.4 copy-start.27
  387.7 6.2 copy-start.7
  395.5 8.5 copy-start.5
  406.2 11.2 %slice-start.1 = ((s8[13107200]{0:T(1024)(128)(4,1)}), s8[4194304]{0:T(1024)(128)(4,1)S(1)}, s32[]{:S(2)}) async-start(s8[13107200]{0:T(1024)(128)(4,1)} %bitcast.59), calls=%async_computation.1 | async-start | bytes 8388608
  406.2 15.0 %slice-start.5 = ((s8[6553600]{0:T(1024)(128)(4,1)}), s8[4194304]{0:T(1024)(128)(4,1)S(1)}, s32[]{:S(2)}) async-start(s8[6553600]{0:T(1024)(128)(4,1)} %bitcast.61), calls=%async_computation.5 | async-start | bytes 8388608
  406.4 11.0 %copy-start.8 = (bf16[256,1280]{1,0:T(8,128)(2,1)}, bf16[256,1280]{1,0:T(8,128)(2,1)S(1)}, u32[]{:S(2)}) copy-start(bf16[256,1280]{1,0:T(8,128)(2,1)S(1)} %multiply_convert_fusion.1.refs_4_) | copy-start | bytes 1966084
  406.4 11.0 %slice-start.2 = ((s8[13107200]{0:T(1024)(128)(4,1)}), s8[4194304]{0:T(1024)(128)(4,1)S(1)}, s32[]{:S(2)}) async-start(s8[13107200]{0:T(1024)(128)(4,1)} %bitcast.59), calls=%async_computation.2 | async-start | bytes 8388608
  406.4 11.0 %slice-start.3 = ((s8[13107200]{0:T(1024)(128)(4,1)}), s8[4194304]{0:T(1024)(128)(4,1)S(1)}, s32[]{:S(2)}) async-start(s8[13107200]{0:T(1024)(128)(4,1)} %bitcast.59), calls=%async_computation.3 | async-start | bytes 8388608
  406.5 11.0 %slice-start.4 = ((s8[13107200]{0:T(1024)(128)(4,1)}), s8[524288]{0:T(1024)(128)(4,1)S(1)}, s32[]{:S(2)}) async-start(s8[13107200]{0:T(1024)(128)(4,1)} %bitcast.59), calls=%async_computation.4 | async-start | bytes 1048576
  406.5 14.7 %slice-start.6 = ((s8[6553600]{0:T(1024)(128)(4,1)}), s8[2359296]{0:T(1024)(128)(4,1)S(1)}, s32[]{:S(2)}) async-start(s8[6553600]{0:T(1024)(128)(4,1)} %bitcast.61), calls=%async_computation.6 | async-start | bytes 4718592
  417.4 3.7 copy-start.12
  421.2 1.9 copy-start.15
  421.2 3.7 copy-start.28
  423.1 1.5 copy-start.18
  423.5 1.3 copy-start.10
  427.1 1.3 copy-start.13
  434.1 61.2 %copy-start.9 = (bf16[256,1280]{1,0:T(8,128)(2,1)}, bf16[256,1280]{1,0:T(8,128)(2,1)S(1)}, u32[]{:S(2)}) copy-start(bf16[256,1280]{1,0:T(8,128)(2,1)S(1)} %get-tuple-element.79.refs_15_) | copy-start | bytes 1966084
  437.9 6.3 copy-start.16
  456.0 8.4 copy-start.14
  464.4 2.2 copy-start.6
  464.8 3.7 copy-start.11
  490.2 1.7 copy-start.1
  490.2 2.7 copy-start.4
  493.0 3.5 copy-start.3
  494.1 1.2 copy-start.17
  497.6 37.6 %copy-start.25 = (s32[322]{0:T(512)S(1)}, s32[322]{0:T(512)}, u32[]{:S(2)}) copy-start(s32[322]{0:T(512)} %owner_ref.3) | copy-start | bytes 3868
  536.1 385.1 %copy-start.23 = (f32[11520]{0:T(1024)S(1)}, f32[11520]{0:T(1024)}, u32[]{:S(2)}) copy-start(f32[11520]{0:T(1024)} %param.23) | copy-start | bytes 138244
  536.1 385.1 %copy-start.24 = (f32[11520]{0:T(1024)S(1)}, f32[11520]{0:T(1024)}, u32[]{:S(2)}) copy-start(f32[11520]{0:T(1024)} %param.22) | copy-start | bytes 138244

commit v10 on v9

--- a/solution.py
+++ b/solution.py
@@ -396,7 +396,10 @@
 LATE = 4
 EARLY = CHUNKS - LATE
 COMBOS = 4 * LATE
-STEPS = COMBOS + 5
+SUM_LATE = 3
+SUM_EARLY = CHUNKS - SUM_LATE
+SUM_COMBOS = 4 * SUM_LATE
+STEPS = SUM_EARLY + 7
 MESH = pl.DeviceIdType.MESH
 
 
@@ -583,7 +586,7 @@
     def late_own_copy(c):
         at = lax.rem(c, 2)
         return pltpu.make_async_copy(
-            slots_ref.at[lax.rem(c, 4), core, :, EARLY + lax.div(c, 4)],
+            slots_ref.at[lax.rem(c, 4), core, :, SUM_EARLY + lax.div(c, 4)],
             late_own.at[at],
             late_own_sem.at[at],
         )
@@ -591,7 +594,7 @@
     def late_pair_copy(c):
         at = lax.rem(c, 2)
         return pltpu.make_async_remote_copy(
-            src_ref=slots_ref.at[lax.rem(c, 4), 1 - core, :, EARLY + lax.div(c, 4)],
+            src_ref=slots_ref.at[lax.rem(c, 4), 1 - core, :, SUM_EARLY + lax.div(c, 4)],
             dst_ref=late_pair_in.at[at],
             send_sem=late_pair_send.at[at],
             recv_sem=late_pair_recv.at[at],
@@ -621,17 +624,17 @@
         )
 
     def late_result_copy(slot):
-        return pltpu.make_async_copy(late_result, out_ref.at[EARLY + slot], late_result_sem)
+        return pltpu.make_async_copy(late_result, out_ref.at[SUM_EARLY + slot], late_result_sem)
 
     def result_copy(k):
         at = lax.rem(k, 2)
         return pltpu.make_async_copy(result.at[at], out_ref.at[k], result_sem.at[at])
 
     def valid(k):
-        return jnp.logical_and(k >= 0, k < EARLY)
+        return jnp.logical_and(k >= 0, k < SUM_EARLY)
 
     def valid_late(c):
-        return jnp.logical_and(c >= 0, c < COMBOS)
+        return jnp.logical_and(c >= 0, c < SUM_COMBOS)
 
     def keep(ref, k):
         kept = jnp.where(filled_ref[k, 0:1, 0:1] > 0.0, ref[...], 0.0)
@@ -721,7 +724,7 @@
         def _():
             pair_copy(t - 1).wait_send()
 
-        @pl.when(t + 1 < EARLY)
+        @pl.when(t + 1 < SUM_EARLY)
         def _():
             own_copy(t + 1).start()
             pair_copy(t + 1).start()
@@ -743,7 +746,7 @@
         def _():
             late_pair_copy(t - 1).wait_send()
 
-        @pl.when(t + 1 < COMBOS)
+        @pl.when(t + 1 < SUM_COMBOS)
         def _():
             late_own_copy(t + 1).start()
             late_pair_copy(t + 1).start()
@@ -818,7 +821,7 @@
                     jnp.bfloat16
                 )
 
-        for slot in range(LATE):
+        for slot in range(SUM_LATE):
             place = near(slot, 1)
 
             @pl.when(t == 4 * slot + 6)
@@ -843,7 +846,7 @@
                 late_result[...] = total_of(
                     late_column[slot, here], late_first_in[slot, 1], late_second_in[slot]
                 )
-                keep(late_result, EARLY + slot)
+                keep(late_result, SUM_EARLY + slot)
                 late_result_copy(slot).start()
 
         k = t - 5
@@ -880,8 +883,8 @@
 
     lax.fori_loop(0, STEPS, step, 0)
     each(lambda *at: square(*at).start())
-    late_result_copy(LATE - 1).wait()
-    for slot in range(LATE):
+    late_result_copy(SUM_LATE - 1).wait()
+    for slot in range(SUM_LATE):
         late_first_copy(slot, 0).wait_send()
         late_first_copy(slot, 1).wait_send()
         late_second_copy(slot).wait_send()
@@ -944,10 +947,10 @@
             low((6, 3) + block),
             low((2, 3) + block),
             low((2, 3) + block),
-            low((LATE, 4) + block),
-            low((LATE, 2) + block),
-            low((LATE,) + block),
-            low((LATE,) + block),
+            low((SUM_LATE, 4) + block),
+            low((SUM_LATE, 2) + block),
+            low((SUM_LATE,) + block),
+            low((SUM_LATE,) + block),
             pltpu.VMEM(block, jnp.float32),
             dma((2,)),
             dma((2,)),
@@ -968,10 +971,10 @@
             dma((6, 3)),
             dma((2, 3)),
             dma((6, 3)),
-            dma((LATE, 2)),
-            dma((LATE, 2)),
-            dma((LATE,)),
-            dma((LATE,)),
+            dma((SUM_LATE, 2)),
+            dma((SUM_LATE, 2)),
+            dma((SUM_LATE,)),
+            dma((SUM_LATE,)),
             dma,
         ]
         + [dma((wide * narrow,))] * 6,

time: 950 us -> 921 us (0.969)
  Pallas kernels: 813 us -> 784 us
    pallas_call x1, Pallas kernels: 380 us -> 352 us  [scatter_sum(): pl.pallas_call(scatter_kernel, out_shape=(jax.ShapeDtypeStruct((slot_coun...]
where the time goes in v10:
time: 921 us; the launch traced here: 912 us
  Pallas kernels  784 us (85%)
  matrix products  75.5 us (8%)
  other arithmetic  32.8 us (4%)
  local copies, waits for them, and re-layouts  14 us (2%)
    pallas_call x1, Pallas kernels, scatter_sum(): pl.pallas_call(scatter_kernel, out_shape=(jax.ShapeDtypeStruct((slot_coun...  352 us
    pallas_call x1, Pallas kernels, gather_all(): pl.pallas_call(gather_kernel, out_shape=(jax.ShapeDtypeStruct((4, 2, narr...  336 us
    dot_general x7, matrix products, backmul(): lax.dot_general(left, right, (((1,), (1,)), ((), ())), preferred_element_...  40.2 us
    pallas_call x1, Pallas kernels, grad_blocks(): pl.pallas_call(grad_kernel, out_shape=jax.ShapeDtypeStruct((TOTAL_SLOTS,...  37.5 us
    pallas_call x1, Pallas kernels, unpack(): pl.pallas_call(unpack_kernel, out_shape=tuple((jax.ShapeDtypeStruct((tota...  36 us
    dot_general x9, matrix products, matmul(): return jnp.dot(left, right, preferred_element_type=jnp.float32)  33 us
    pallas_call x2, Pallas kernels, attend_call(): pl.pallas_call(kernel, out_shape=tuple((jax.ShapeDtypeStruct((tokens, wid...  22.9 us

profile of v10, /device:TPU:0, one launch (start us, length us, event | category | flops | bytes accessed | tf_op | source)
XLA Modules:
  0.0 911.9 jit_solution(13596744954309304831)
XLA Ops:
  0.6 0.8 subtract_convert_fusion
  1.8 0.8 select_reduce_fusion.2
  2.6 0.6 scatter.4.count_ref
  3.2 4.3 convert_element_type.112.own_ref
  7.5 336.2 %gather_all.1 = (bf16[4,2,4,16,64,1280]{5,4,3,2,1,0:T(8,128)(2,1)}, f32[32,8,128]{2,1,0:T(8,128)}) custom-call(bf16[16,64,1280]{2,1,0:T(8,128)(2,1)} %convert_element_type.112.own_ref, f32[8,128]{1,0:T(8,128)} %scatter.4.count_ref), custom_call_target="tpu_custom_call" | custom-call | tf_op jit(solution)/shard_map/gather_all/pallas_call | solution.py:1279
  343.7 36.0 %unpack.1 = (bf16[64,2560]{1,0:T(8,128)(2,1)}, bf16[1280,1280]{1,0:T(8,128)(2,1)}, bf16[1280,3840]{1,0:T(8,128)(2,1)}, bf16[1280,1280]{1,0:T(8,128)(2,1)}, bf16[...) custom-call(s32[322]{0:T(512)} %owner_ref.3, ...), custom_call_target="tpu_custom_call" | custom-call | bytes 105512960 | tf_op jit(solution)/shard_map/unpack/pallas_call | solution.py:278
  380.0 1.5 fusion.50
  381.6 1.4 copy-done
  383.0 0.4 divide_convert_fusion.2.refs_1_
  383.8 3.6 multiply_reduce_fusion.5
  387.7 1.5 copy-done.27
  389.2 4.6 fusion.51.qkv_ref
  394.0 0.7 tile.21.sin_ref
  394.8 0.7 tile.9.cos_ref
  395.5 8.5 attend.1
  404.0 2.2 multiply_reduce_fusion.4
  406.5 11.0 %divide_convert_fusion = (bf16[256,5120]{1,0:T(8,128)(2,1)S(1)}, f32[256,5120]{1,0:T(8,128)}) fusion(bf16[256,1280]{1,0:T(8,128)(2,1)S(1)} %multiply_convert_fusion.1.refs_4_, bf16[1280,5120]{1,0:T(8,128)(2,1)} %get-tuple-element.44), kind=kOutput, calls=%fused_computation.6 | convolution fusion | flops 3360686080 | bytes 21626880 | tf_op jit(solution)/shard_map/dot_general | solution.py:35
  417.5 3.7 fusion.5.refs_6_
  421.2 1.9 fusion.52
  423.1 0.4 divide_convert_fusion.1.refs_7_
  423.5 1.1 copy-done.18
  424.9 2.1 fusion.3
  427.4 1.1 copy-done.13
  428.4 1.8 convolution_subtract_fusion
  430.2 1.0 slice_reduce_fusion.4
  431.6 2.5 select_reduce_fusion.1
  434.4 3.4 fusion.44
  437.9 6.3 fusion.49
  444.2 11.8 %fusion.refs_12_ = bf16[256,5120]{1,0:T(8,128)(2,1)} fusion(bf16[256,1280]{1,0:T(8,128)(2,1)} %get-tuple-element.108.refs_13_, bf16[5120,1280]{1,0:T(8,128)(2,1)} %get-tuple-element.45, f32[256,5120]{1,0:T(8,128)} %get-tuple-element.106), kind=kOutput, calls=%fused_computation.3 | convolution fusion | flops 3367239680 | bytes 21626880 | tf_op jit(solution)/shard_map/dot_general | solution.py:45
  456.0 8.4 multiply_reduce_fusion
  464.8 1.8 copy-done.6
  466.6 1.9 convolution_convert_fusion.grad_ref
  468.5 14.5 %attend_back.1.refs_10_ = bf16[256,3840]{1,0:T(8,128)(2,1)} custom-call(bf16[256,1280]{1,0:T(8,128)(2,1)} %get-tuple-element.49.query_ref, bf16[256,1280]{1,0:T(8,128)(2,1)} %get-tuple-element.50.key_ref, bf16[256,1280]{1,0:T(8,128)(2,1)} %get-tuple-element.51.value_ref, bf16[256,1280]{1,0:T(8,128)(2,1)} %convolution_convert_fusion.grad_ref, ...), custom_call_target="tpu_custom_call" | custom-call | tf_op jit(solution)/shard_map/attend_back/pallas_call | solution.py:167
  483.0 7.2 multiply_reduce_fusion.1
  490.7 1.3 copy-done.1
  492.0 1.0 copy-done.4
  493.0 1.2 fusion.45
  494.6 0.7 pad_bitcast_fusion.small_ref
  495.3 1.1 pad_maximum_fusion.refs_14_
  496.4 1.1 pad_maximum_fusion.1.refs_8_
  497.6 37.5 %grad_blocks.1 = bf16[512,64,1280]{2,1,0:T(8,128)(2,1)} custom-call(s32[322]{0:T(512)} %owner_ref.3, bf16[256,64]{1,0:T(8,128)(2,1)} %copy-done.19, bf16[256,1280]{1,0:T(8,128)(2,1)} %copy-done.2, bf16[256,1280]{1,0:T(8,128)(2,1)} %copy-done.7, bf16[256,1280]{1,0:T(8,128)(2,1)} %get-tuple-element.42.refs_3_, bf16[256,1280]{1,0:T(8,128)(2,1)} %copy-done.8, ...), custom_call_target="tpu_custom_call" | custom-call | flops 13505658880 | bytes 52756480 | tf_op jit(solution)/shard_map/grad_blocks/pallas_call | solution.py:373
  535.4 0.7 broadcast_in_dim.105.filled_ref
  536.1 351.8 %scatter_sum.1 = (f32[16,64,1280]{2,1,0:T(8,128)}, f32[32,8,128]{2,1,0:T(8,128)}, f32[32,8,128]{2,1,0:T(8,128)}) custom-call(bf16[4,2,4,16,64,1280]{5,4,3,2,1,0:T(8,128)(2,1)} %bitcast.5.slots_ref, f32[32,8,128]{2,1,0:T(8,128)} %pad_bitcast_fusion.small_ref, f32[16,8,128]{2,1,0:T(8,128)} %broadcast_in_dim.105.filled_ref), custom_call_target="tpu_custom_call" | custom-call | tf_op jit(solution)/shard_map/scatter_sum/pallas_call | solution.py:912
  887.9 1.4 multiply_reduce_fusion.6
  889.3 1.5 reduce_sum.252
  892.9 1.5 multiply_subtract_fusion.1
  894.4 14.5 %fusion.38 = (bf16[16,64,1280]{2,1,0:T(8,128)(2,1)}, f32[16,64,1280]{2,1,0:T(8,128)}, f32[16,64,1280]{2,1,0:T(8,128)}, f32[16,64,1280]{2,1,0:T(8,128)}) fusion(f32[16,64,1280]{2,1,0:T(8,128)} %param.18, f32[]{:T(128)} %bitcast.11, f32[16,64,1280]{2,1,0:T(8,128)} %get-tuple-element.54, f32[]{:T(128)S(6)} %min.3, f32[16,64,1280]{2,1,0:T(8,128)} %param.20, ...), kind=kLoop, calls=%fused_computation.125 | loop fusion | flops 20971520 | bytes 39321608 | tf_op jit(solution)/shard_map/convert_element_type | solution.py:1558
  908.9 1.4 fusion.34
  (126 shorter events, 4.5 us)
Async XLA Ops:
  343.6 36.0 %copy-start.22 = (f32[16,640]{1,0:T(8,128)S(1)}, f32[16,640]{1,0:T(8,128)}, u32[]{:S(2)}) copy-start(f32[16,640]{1,0:T(8,128)} %param.13) | copy-start | bytes 122884
  343.7 36.1 %copy-start.21 = (s32[16,640]{1,0:T(8,128)S(1)}, s32[16,640]{1,0:T(8,128)}, u32[]{:S(2)}) copy-start(s32[16,640]{1,0:T(8,128)} %param.14) | copy-start | bytes 122884
  380.0 1.5 copy-start.19
  380.0 1.5 copy-start.20
  381.5 1.5 copy-start
  381.6 1.9 slice-start
  381.6 1.9 copy-start.26
  383.4 4.0 copy-start.2
  383.8 5.4 copy-start.27
  387.7 6.2 copy-start.7
  395.5 8.5 copy-start.5
  406.2 11.2 %slice-start.1 = ((s8[13107200]{0:T(1024)(128)(4,1)}), s8[4194304]{0:T(1024)(128)(4,1)S(1)}, s32[]{:S(2)}) async-start(s8[13107200]{0:T(1024)(128)(4,1)} %bitcast.59), calls=%async_computation.1 | async-start | bytes 8388608
  406.2 15.0 %slice-start.5 = ((s8[6553600]{0:T(1024)(128)(4,1)}), s8[4194304]{0:T(1024)(128)(4,1)S(1)}, s32[]{:S(2)}) async-start(s8[6553600]{0:T(1024)(128)(4,1)} %bitcast.61), calls=%async_computation.5 | async-start | bytes 8388608
  406.4 11.0 %copy-start.8 = (bf16[256,1280]{1,0:T(8,128)(2,1)}, bf16[256,1280]{1,0:T(8,128)(2,1)S(1)}, u32[]{:S(2)}) copy-start(bf16[256,1280]{1,0:T(8,128)(2,1)S(1)} %multiply_convert_fusion.1.refs_4_) | copy-start | bytes 1966084
  406.4 11.0 %slice-start.2 = ((s8[13107200]{0:T(1024)(128)(4,1)}), s8[4194304]{0:T(1024)(128)(4,1)S(1)}, s32[]{:S(2)}) async-start(s8[13107200]{0:T(1024)(128)(4,1)} %bitcast.59), calls=%async_computation.2 | async-start | bytes 8388608
  406.4 11.0 %slice-start.3 = ((s8[13107200]{0:T(1024)(128)(4,1)}), s8[4194304]{0:T(1024)(128)(4,1)S(1)}, s32[]{:S(2)}) async-start(s8[13107200]{0:T(1024)(128)(4,1)} %bitcast.59), calls=%async_computation.3 | async-start | bytes 8388608
  406.5 11.0 %slice-start.4 = ((s8[13107200]{0:T(1024)(128)(4,1)}), s8[524288]{0:T(1024)(128)(4,1)S(1)}, s32[]{:S(2)}) async-start(s8[13107200]{0:T(1024)(128)(4,1)} %bitcast.59), calls=%async_computation.4 | async-start | bytes 1048576
  406.5 14.7 %slice-start.6 = ((s8[6553600]{0:T(1024)(128)(4,1)}), s8[2359296]{0:T(1024)(128)(4,1)S(1)}, s32[]{:S(2)}) async-start(s8[6553600]{0:T(1024)(128)(4,1)} %bitcast.61), calls=%async_computation.6 | async-start | bytes 4718592
  417.4 3.7 copy-start.12
  421.2 1.9 copy-start.15
  421.2 3.7 copy-start.28
  423.1 1.5 copy-start.18
  423.5 1.3 copy-start.10
  427.1 1.3 copy-start.13
  434.1 61.2 %copy-start.9 = (bf16[256,1280]{1,0:T(8,128)(2,1)}, bf16[256,1280]{1,0:T(8,128)(2,1)S(1)}, u32[]{:S(2)}) copy-start(bf16[256,1280]{1,0:T(8,128)(2,1)S(1)} %get-tuple-element.79.refs_15_) | copy-start | bytes 1966084
  437.9 6.3 copy-start.16
  456.0 8.4 copy-start.14
  464.4 2.2 copy-start.6
  464.8 3.7 copy-start.11
  490.2 1.7 copy-start.1
  490.2 2.7 copy-start.4
  493.0 3.5 copy-start.3
  494.1 1.2 copy-start.17
  497.6 37.6 %copy-start.25 = (s32[322]{0:T(512)S(1)}, s32[322]{0:T(512)}, u32[]{:S(2)}) copy-start(s32[322]{0:T(512)} %owner_ref.3) | copy-start | bytes 3868
  536.1 356.8 %copy-start.23 = (f32[11520]{0:T(1024)S(1)}, f32[11520]{0:T(1024)}, u32[]{:S(2)}) copy-start(f32[11520]{0:T(1024)} %param.23) | copy-start | bytes 138244
  536.1 356.8 %copy-start.24 = (f32[11520]{0:T(1024)S(1)}, f32[11520]{0:T(1024)}, u32[]{:S(2)}) copy-start(f32[11520]{0:T(1024)} %param.22) | copy-start | bytes 138244

commit v11 on v9

--- a/solution.py
+++ b/solution.py
@@ -393,10 +393,10 @@
 
 
 CHUNKS = 16
-LATE = 4
+LATE = 3
 EARLY = CHUNKS - LATE
 COMBOS = 4 * LATE
-STEPS = COMBOS + 5
+STEPS = EARLY + 7
 MESH = pl.DeviceIdType.MESH
 
 
@@ -1162,21 +1162,18 @@
                 plane_wait(far, z, k)
 
         for j in (0, -1, 1, -2, 2, -3, 3):
-            m = t - 2 - abs(j)
+            c = t - 2 - abs(j)
             n = z + j
-            first = m + lax.div(m + 2, 3)
-            for c, more in ((first, True), (first + 1, lax.rem(m, 3) == 0)):
-                there = jnp.logical_and(
-                    jnp.logical_and(m >= 0, c < COMBOS),
-                    jnp.logical_and(jnp.logical_and(n >= 0, n < 4), more),
-                )
-                if j:
-
-                    @pl.when(there)
-                    def _(n=n, c=c):
-                        plane_wait(lax.rem(here + c, 4), n, EARLY + lax.div(c, 4))
-
-                both_lines(lambda n, way, c=c: late(c, n, way).start(), n, j, there)
+            there = jnp.logical_and(
+                jnp.logical_and(c >= 0, c < COMBOS), jnp.logical_and(n >= 0, n < 4)
+            )
+            if j:
+
+                @pl.when(there)
+                def _(n=n, c=c):
+                    plane_wait(lax.rem(here + c, 4), n, EARLY + lax.div(c, 4))
+
+            both_lines(lambda n, way, c=c: late(c, n, way).start(), n, j, there)
 
         for n in range(4):
             gap = jnp.abs(z - n)
@@ -1202,13 +1199,9 @@
                 for p in sent:
                     early_pair(p, k).start()
 
-        m = t - 5
-        first = m + lax.div(m + 2, 3)
-        for c, more in ((first, True), (first + 1, lax.rem(m, 3) == 0)):
-
-            @pl.when(jnp.logical_and(jnp.logical_and(m >= 0, c < COMBOS), more))
-            def _(c=c):
-                late_pair(c).start()
+        @pl.when(jnp.logical_and(t >= 5, t < 5 + COMBOS))
+        def _():
+            late_pair(t - 5).start()
 
         return carry
 
@@ -1235,11 +1228,11 @@
             def _(n=n):
                 line(n, k, 1).wait_send()
 
-            @pl.when(jnp.logical_and(n <= z, z < 3))
+            @pl.when(jnp.logical_and(k < COMBOS, jnp.logical_and(n <= z, z < 3)))
             def _(n=n):
                 late(k, n, 0).wait_send()
 
-            @pl.when(jnp.logical_and(n >= z, z > 0))
+            @pl.when(jnp.logical_and(k < COMBOS, jnp.logical_and(n >= z, z > 0)))
             def _(n=n):
                 late(k, n, 1).wait_send()
 
@@ -1248,7 +1241,10 @@
             for p in range(4):
                 early_pair(p, k).wait_send()
 
-        late_pair(k).wait_send()
+        @pl.when(k < COMBOS)
+        def _():
+            late_pair(k).wait_send()
+
         return carry
 
     lax.fori_loop(0, CHUNKS, finish, 0)

time: 950 us -> 906 us (0.954)
  Pallas kernels: 813 us -> 769 us
    pallas_call x1, Pallas kernels: 380 us -> 357 us  [scatter_sum(): pl.pallas_call(scatter_kernel, out_shape=(jax.ShapeDtypeStruct((slot_coun...]
    pallas_call x1, Pallas kernels: 336 us -> 316 us  [gather_all(): pl.pallas_call(gather_kernel, out_shape=(jax.ShapeDtypeStruct((4, 2, narr...]
where the time goes in v11:
time: 906 us; the launch traced here: 897 us
  Pallas kernels  769 us (85%)
  matrix products  75.5 us (8%)
  other arithmetic  32.8 us (4%)
  local copies, waits for them, and re-layouts  14 us (2%)
    pallas_call x1, Pallas kernels, scatter_sum(): pl.pallas_call(scatter_kernel, out_shape=(jax.ShapeDtypeStruct((slot_coun...  357 us
    pallas_call x1, Pallas kernels, gather_all(): pl.pallas_call(gather_kernel, out_shape=(jax.ShapeDtypeStruct((4, 2, narr...  316 us
    dot_general x7, matrix products, backmul(): lax.dot_general(left, right, (((1,), (1,)), ((), ())), preferred_element_...  40.2 us
    pallas_call x1, Pallas kernels, grad_blocks(): pl.pallas_call(grad_kernel, out_shape=jax.ShapeDtypeStruct((TOTAL_SLOTS,...  37.5 us
    pallas_call x1, Pallas kernels, unpack(): pl.pallas_call(unpack_kernel, out_shape=tuple((jax.ShapeDtypeStruct((tota...  36 us
    dot_general x9, matrix products, matmul(): return jnp.dot(left, right, preferred_element_type=jnp.float32)  33 us
    pallas_call x2, Pallas kernels, attend_call(): pl.pallas_call(kernel, out_shape=tuple((jax.ShapeDtypeStruct((tokens, wid...  22.9 us

profile of v11, /device:TPU:0, one launch (start us, length us, event | category | flops | bytes accessed | tf_op | source)
XLA Modules:
  0.0 896.6 jit_solution(3859144823989304880)
XLA Ops:
  0.6 0.8 subtract_convert_fusion
  1.8 0.8 select_reduce_fusion.2
  2.6 0.6 scatter.4.count_ref
  3.2 4.3 convert_element_type.112.own_ref
  7.5 315.7 %gather_all.1 = (bf16[4,2,4,16,64,1280]{5,4,3,2,1,0:T(8,128)(2,1)}, f32[32,8,128]{2,1,0:T(8,128)}) custom-call(bf16[16,64,1280]{2,1,0:T(8,128)(2,1)} %convert_element_type.112.own_ref, f32[8,128]{1,0:T(8,128)} %scatter.4.count_ref), custom_call_target="tpu_custom_call" | custom-call | tf_op jit(solution)/shard_map/gather_all/pallas_call | solution.py:1272
  323.2 36.0 %unpack.1 = (bf16[64,2560]{1,0:T(8,128)(2,1)}, bf16[1280,1280]{1,0:T(8,128)(2,1)}, bf16[1280,3840]{1,0:T(8,128)(2,1)}, bf16[1280,1280]{1,0:T(8,128)(2,1)}, bf16[...) custom-call(s32[322]{0:T(512)} %owner_ref.3, ...), custom_call_target="tpu_custom_call" | custom-call | bytes 105512960 | tf_op jit(solution)/shard_map/unpack/pallas_call | solution.py:278
  359.6 1.5 fusion.50
  361.1 1.4 copy-done
  362.6 0.4 divide_convert_fusion.2.refs_1_
  363.4 3.6 multiply_reduce_fusion.5
  367.2 1.5 copy-done.27
  368.8 4.6 fusion.51.qkv_ref
  373.6 0.7 tile.21.sin_ref
  374.3 0.7 tile.9.cos_ref
  375.1 8.5 attend.1
  383.5 2.2 multiply_reduce_fusion.4
  386.0 11.0 %divide_convert_fusion = (bf16[256,5120]{1,0:T(8,128)(2,1)S(1)}, f32[256,5120]{1,0:T(8,128)}) fusion(bf16[256,1280]{1,0:T(8,128)(2,1)S(1)} %multiply_convert_fusion.1.refs_4_, bf16[1280,5120]{1,0:T(8,128)(2,1)} %get-tuple-element.44), kind=kOutput, calls=%fused_computation.6 | convolution fusion | flops 3360686080 | bytes 21626880 | tf_op jit(solution)/shard_map/dot_general | solution.py:35
  397.0 3.7 fusion.5.refs_6_
  400.7 1.9 fusion.52
  402.6 0.4 divide_convert_fusion.1.refs_7_
  403.1 1.1 copy-done.18
  404.4 2.1 fusion.3
  406.9 1.1 copy-done.13
  407.9 1.8 convolution_subtract_fusion
  409.7 1.0 slice_reduce_fusion.4
  411.1 2.5 select_reduce_fusion.1
  414.0 3.4 fusion.44
  417.4 6.3 fusion.49
  423.7 11.8 %fusion.refs_12_ = bf16[256,5120]{1,0:T(8,128)(2,1)} fusion(bf16[256,1280]{1,0:T(8,128)(2,1)} %get-tuple-element.108.refs_13_, bf16[5120,1280]{1,0:T(8,128)(2,1)} %get-tuple-element.45, f32[256,5120]{1,0:T(8,128)} %get-tuple-element.106), kind=kOutput, calls=%fused_computation.3 | convolution fusion | flops 3367239680 | bytes 21626880 | tf_op jit(solution)/shard_map/dot_general | solution.py:45
  435.5 8.4 multiply_reduce_fusion
  444.4 1.8 copy-done.6
  446.1 1.9 convolution_convert_fusion.grad_ref
  448.0 14.5 %attend_back.1.refs_10_ = bf16[256,3840]{1,0:T(8,128)(2,1)} custom-call(bf16[256,1280]{1,0:T(8,128)(2,1)} %get-tuple-element.49.query_ref, bf16[256,1280]{1,0:T(8,128)(2,1)} %get-tuple-element.50.key_ref, bf16[256,1280]{1,0:T(8,128)(2,1)} %get-tuple-element.51.value_ref, bf16[256,1280]{1,0:T(8,128)(2,1)} %convolution_convert_fusion.grad_ref, ...), custom_call_target="tpu_custom_call" | custom-call | tf_op jit(solution)/shard_map/attend_back/pallas_call | solution.py:167
  462.5 7.2 multiply_reduce_fusion.1
  470.2 1.3 copy-done.1
  471.5 1.0 copy-done.4
  472.5 1.2 fusion.45
  474.1 0.7 pad_bitcast_fusion.small_ref
  474.8 1.1 pad_maximum_fusion.refs_14_
  476.0 1.1 pad_maximum_fusion.1.refs_8_
  477.1 37.5 %grad_blocks.1 = bf16[512,64,1280]{2,1,0:T(8,128)(2,1)} custom-call(s32[322]{0:T(512)} %owner_ref.3, bf16[256,64]{1,0:T(8,128)(2,1)} %copy-done.19, bf16[256,1280]{1,0:T(8,128)(2,1)} %copy-done.2, bf16[256,1280]{1,0:T(8,128)(2,1)} %copy-done.7, bf16[256,1280]{1,0:T(8,128)(2,1)} %get-tuple-element.42.refs_3_, bf16[256,1280]{1,0:T(8,128)(2,1)} %copy-done.8, ...), custom_call_target="tpu_custom_call" | custom-call | flops 13505658880 | bytes 52756480 | tf_op jit(solution)/shard_map/grad_blocks/pallas_call | solution.py:373
  514.8 0.7 broadcast_in_dim.105.filled_ref
  515.5 357.1 %scatter_sum.1 = (f32[16,64,1280]{2,1,0:T(8,128)}, f32[32,8,128]{2,1,0:T(8,128)}, f32[32,8,128]{2,1,0:T(8,128)}) custom-call(bf16[4,2,4,16,64,1280]{5,4,3,2,1,0:T(8,128)(2,1)} %bitcast.5.slots_ref, f32[32,8,128]{2,1,0:T(8,128)} %pad_bitcast_fusion.small_ref, f32[16,8,128]{2,1,0:T(8,128)} %broadcast_in_dim.105.filled_ref), custom_call_target="tpu_custom_call" | custom-call | tf_op jit(solution)/shard_map/scatter_sum/pallas_call | solution.py:909
  872.7 1.4 multiply_reduce_fusion.6
  874.1 1.5 reduce_sum.252
  877.7 1.5 multiply_subtract_fusion.1
  879.2 14.5 %fusion.38 = (bf16[16,64,1280]{2,1,0:T(8,128)(2,1)}, f32[16,64,1280]{2,1,0:T(8,128)}, f32[16,64,1280]{2,1,0:T(8,128)}, f32[16,64,1280]{2,1,0:T(8,128)}) fusion(f32[16,64,1280]{2,1,0:T(8,128)} %param.18, f32[]{:T(128)} %bitcast.11, f32[16,64,1280]{2,1,0:T(8,128)} %get-tuple-element.54, f32[]{:T(128)S(6)} %min.3, f32[16,64,1280]{2,1,0:T(8,128)} %param.20, ...), kind=kLoop, calls=%fused_computation.125 | loop fusion | flops 20971520 | bytes 39321608 | tf_op jit(solution)/shard_map/convert_element_type | solution.py:1551
  893.6 1.4 fusion.34
  (126 shorter events, 4.5 us)
Async XLA Ops:
  323.2 36.0 %copy-start.22 = (f32[16,640]{1,0:T(8,128)S(1)}, f32[16,640]{1,0:T(8,128)}, u32[]{:S(2)}) copy-start(f32[16,640]{1,0:T(8,128)} %param.13) | copy-start | bytes 122884
  323.2 36.1 %copy-start.21 = (s32[16,640]{1,0:T(8,128)S(1)}, s32[16,640]{1,0:T(8,128)}, u32[]{:S(2)}) copy-start(s32[16,640]{1,0:T(8,128)} %param.14) | copy-start | bytes 122884
  359.5 1.5 copy-start.19
  359.6 1.5 copy-start.20
  361.1 1.5 copy-start
  361.1 1.9 slice-start
  361.1 1.9 copy-start.26
  363.0 4.0 copy-start.2
  363.4 5.4 copy-start.27
  367.2 6.2 copy-start.7
  375.1 8.5 copy-start.5
  385.7 11.2 %slice-start.1 = ((s8[13107200]{0:T(1024)(128)(4,1)}), s8[4194304]{0:T(1024)(128)(4,1)S(1)}, s32[]{:S(2)}) async-start(s8[13107200]{0:T(1024)(128)(4,1)} %bitcast.59), calls=%async_computation.1 | async-start | bytes 8388608
  385.7 15.0 %slice-start.5 = ((s8[6553600]{0:T(1024)(128)(4,1)}), s8[4194304]{0:T(1024)(128)(4,1)S(1)}, s32[]{:S(2)}) async-start(s8[6553600]{0:T(1024)(128)(4,1)} %bitcast.61), calls=%async_computation.5 | async-start | bytes 8388608
  385.9 11.0 %copy-start.8 = (bf16[256,1280]{1,0:T(8,128)(2,1)}, bf16[256,1280]{1,0:T(8,128)(2,1)S(1)}, u32[]{:S(2)}) copy-start(bf16[256,1280]{1,0:T(8,128)(2,1)S(1)} %multiply_convert_fusion.1.refs_4_) | copy-start | bytes 1966084
  386.0 11.0 %slice-start.2 = ((s8[13107200]{0:T(1024)(128)(4,1)}), s8[4194304]{0:T(1024)(128)(4,1)S(1)}, s32[]{:S(2)}) async-start(s8[13107200]{0:T(1024)(128)(4,1)} %bitcast.59), calls=%async_computation.2 | async-start | bytes 8388608
  386.0 11.0 %slice-start.3 = ((s8[13107200]{0:T(1024)(128)(4,1)}), s8[4194304]{0:T(1024)(128)(4,1)S(1)}, s32[]{:S(2)}) async-start(s8[13107200]{0:T(1024)(128)(4,1)} %bitcast.59), calls=%async_computation.3 | async-start | bytes 8388608
  386.0 11.0 %slice-start.4 = ((s8[13107200]{0:T(1024)(128)(4,1)}), s8[524288]{0:T(1024)(128)(4,1)S(1)}, s32[]{:S(2)}) async-start(s8[13107200]{0:T(1024)(128)(4,1)} %bitcast.59), calls=%async_computation.4 | async-start | bytes 1048576
  386.0 14.7 %slice-start.6 = ((s8[6553600]{0:T(1024)(128)(4,1)}), s8[2359296]{0:T(1024)(128)(4,1)S(1)}, s32[]{:S(2)}) async-start(s8[6553600]{0:T(1024)(128)(4,1)} %bitcast.61), calls=%async_computation.6 | async-start | bytes 4718592
  397.0 3.7 copy-start.12
  400.7 1.9 copy-start.15
  400.7 3.7 copy-start.28
  402.6 1.5 copy-start.18
  403.0 1.3 copy-start.10
  406.6 1.3 copy-start.13
  413.6 61.2 %copy-start.9 = (bf16[256,1280]{1,0:T(8,128)(2,1)}, bf16[256,1280]{1,0:T(8,128)(2,1)S(1)}, u32[]{:S(2)}) copy-start(bf16[256,1280]{1,0:T(8,128)(2,1)S(1)} %get-tuple-element.79.refs_15_) | copy-start | bytes 1966084
  417.4 6.3 copy-start.16
  435.5 8.4 copy-start.14
  444.0 2.2 copy-start.6
  444.3 3.7 copy-start.11
  469.8 1.7 copy-start.1
  469.8 2.7 copy-start.4
  472.5 3.5 copy-start.3
  473.6 1.2 copy-start.17
  477.1 37.5 %copy-start.25 = (s32[322]{0:T(512)S(1)}, s32[322]{0:T(512)}, u32[]{:S(2)}) copy-start(s32[322]{0:T(512)} %owner_ref.3) | copy-start | bytes 3868
  515.5 362.2 %copy-start.23 = (f32[11520]{0:T(1024)S(1)}, f32[11520]{0:T(1024)}, u32[]{:S(2)}) copy-start(f32[11520]{0:T(1024)} %param.23) | copy-start | bytes 138244
  515.5 362.2 %copy-start.24 = (f32[11520]{0:T(1024)S(1)}, f32[11520]{0:T(1024)}, u32[]{:S(2)}) copy-start(f32[11520]{0:T(1024)} %param.22) | copy-start | bytes 138244
